TPU v7x, 256 devices: a whole 4x4x8 slice. The times are simulated.
256 devices in a mesh: expert: 32 (over y, z), vocab: 8 (over x, core).
Axes of the slice: x: 4, y: 4, z: 8, core: 2. Of those that a mesh axis runs over, the one named last changes fastest.
Arguments:
- layer_out: bfloat16 [1024, 2048], P('expert'), may hold values from -6 to 6
- moe_input: bfloat16 [1024, 2048], P('expert'), may hold values from -6 to 6
- final_gain: float32 [2048], replicated, may hold values from 0.1 to 1.9
- head_weight: bfloat16 [2048, 98304], P(None, ('expert', 'vocab')), may hold values from -0.125 to 0.125
- clean_ids: int32 [1024], P('expert'), may hold values from 0 to 98303
- levels: int32 [1024], P('expert'), may hold values from 0 to 15
- ratio_table: float32 [16], replicated, may hold values from 0.5 to 8
- gate_weights: float32 [1024, 8], P('expert'), may hold values from 0.05 to 0.5
- expert_ids: int32 [1024, 8], P('expert'), may hold values from 0 to 63, all different within a row; in each aligned block of 32 rows (0 to 31, 32 to 63, ...) at most 8 rows name the same one
- w_gate: bfloat16 [64, 2048, 1024], P('expert', None, 'vocab'), may hold values from -0.125 to 0.125
- w_up: bfloat16 [64, 2048, 1024], P('expert', None, 'vocab'), may hold values from -0.125 to 0.125
- w_down: bfloat16 [64, 1024, 2048], P('expert', 'vocab'), may hold values from -0.1875 to 0.1875
Outputs:
- head_grad: float32 [2048, 98304], P(None, ('expert', 'vocab'))
- residual_grad: float32 [1024, 2048], P('expert', 'vocab')
- input_grad: float32 [1024, 2048], P('expert', 'vocab')
Inputs may be any that keep to these rules, and one draw needn't show every extreme that they name: `expert_ids`: the 8 experts of a row are distinct; among the 32 rows of one index of expert no expert is named by more than 8 rows.
All inputs are finite; a program needn't handle non-finite values.
Results may differ from a plain program's by a relative error of at most 0.0044.
The roundings to bfloat16 on the way count: a program that leaves them out, or rounds other values in their place, can miss the bound.
Values may be sent and summed in bfloat16 or wider, within the bound.
No kernel may reach another device: no remote copies, remote signals or barrier semaphores. Data moves between devices by JAX's collectives and lax.ppermute only.
A program may use at most 64 MiB of HBM per device.

v0:
```python
import math

import jax
import jax.numpy as jnp
from jax import lax
from jax.experimental import pallas as pl
from jax.experimental.pallas import tpu as pltpu
from jax.sharding import Mesh, PartitionSpec as P

epsilon = 1e-05
YN, ZN, XN, CN = 4, 8, 4, 2
bf16 = jnp.bfloat16
f32 = jnp.float32


def wide_dot(a, b, dims, precision=None):
    return lax.dot_general(
        a, b, (dims, ((), ())), preferred_element_type=f32, precision=precision
    )


def along_y(a, step):
    return lax.ppermute(a, "y", [(p, (p + step) % YN) for p in range(YN)])


def along_x(a, step):
    return lax.ppermute(a, "x", [(p, (p + step) % XN) for p in range(XN)])


def across_core(a):
    return lax.ppermute(a, "core", [(p, CN - 1 - p) for p in range(CN)])


def exchanged(a, axes):
    return lax.all_to_all(a, axes, 0, 0, tiled=True)


def in_ring_order(a, move, ring):
    return [a] + [move(a, ring - k) for k in range(1, ring)]


def turned_weights(order, head_weight, w_gate, w_up, w_down):
    width, tile = head_weight.shape
    own, _, hidden = w_gate.shape
    count = order.shape[0]
    share = width // count

    def body(order_ref, head_ref, gate_ref, up_ref, down_ref, head_out, pair_out, down_out):
        head_out[...] = head_ref[...]
        pair_out[:, :, :hidden] = gate_ref[...]
        pair_out[:, :, hidden:] = up_ref[...]
        down_out[...] = down_ref[...]

    moved = 2 * (head_weight.size + 3 * w_gate.size)
    return pl.pallas_call(
        body,
        grid_spec=pltpu.PrefetchScalarGridSpec(
            num_scalar_prefetch=1,
            grid=(count,),
            in_specs=[
                pl.BlockSpec((share, tile), lambda i, s: (s[i], 0)),
                pl.BlockSpec((own, share, hidden), lambda i, s: (0, s[i], 0)),
                pl.BlockSpec((own, share, hidden), lambda i, s: (0, s[i], 0)),
                pl.BlockSpec((own, hidden, share), lambda i, s: (0, 0, s[i])),
            ],
            out_specs=[
                pl.BlockSpec((share, tile), lambda i, s: (i, 0)),
                pl.BlockSpec((own, share, 2 * hidden), lambda i, s: (0, i, 0)),
                pl.BlockSpec((own, hidden, share), lambda i, s: (0, 0, i)),
            ],
        ),
        out_shape=[
            jax.ShapeDtypeStruct((width, tile), bf16),
            jax.ShapeDtypeStruct((own, width, 2 * hidden), bf16),
            jax.ShapeDtypeStruct((own, hidden, width), bf16),
        ],
        cost_estimate=pl.CostEstimate(flops=0, bytes_accessed=2 * moved, transcendentals=0),
        name="turned_weights",
    )(order, head_weight, w_gate, w_up, w_down)


def head_gradient(order, near, far, score_grad):
    rows, side = near.shape
    tile = score_grad.shape[1]
    count = order.shape[0]
    share = 2 * side // count
    lead = count // 2

    def body(order_ref, near_ref, far_ref, grad_ref, out_ref):
        def product(rows_ref):
            out_ref[...] = wide_dot(rows_ref[...], grad_ref[...], ((0,), (0,)))

        @pl.when(pl.program_id(0) < lead)
        def _():
            product(near_ref)

        @pl.when(pl.program_id(0) >= lead)
        def _():
            product(far_ref)

    return pl.pallas_call(
        body,
        grid_spec=pltpu.PrefetchScalarGridSpec(
            num_scalar_prefetch=1,
            grid=(count,),
            in_specs=[
                pl.BlockSpec((rows, share), lambda i, s: (0, jnp.minimum(i, lead - 1))),
                pl.BlockSpec((rows, share), lambda i, s: (0, jnp.maximum(i - lead, 0))),
                pl.BlockSpec((rows, tile), lambda i, s: (0, 0)),
            ],
            out_specs=pl.BlockSpec((share, tile), lambda i, s: (s[i], 0)),
        ),
        out_shape=jax.ShapeDtypeStruct((2 * side, tile), f32),
        cost_estimate=pl.CostEstimate(
            flops=4 * rows * side * tile,
            bytes_accessed=4 * rows * side + 2 * rows * tile + 8 * side * tile,
            transcendentals=0,
        ),
        name="head_gradient",
    )(order, near, far, score_grad)


def near_gradient(score_grad, weight, far):
    rows, tile = score_grad.shape
    share = weight.shape[0] // XN
    part = rows // YN

    def body(grad_ref, weight_ref, far_ref, *outs):
        for k in range(XN):
            low = slice(k * share, (k + 1) * share)
            for i in range(YN):
                at = slice(i * part, (i + 1) * part)
                total = wide_dot(grad_ref[at, :], weight_ref[low, :], ((1,), (1,)))
                total = total + far_ref[at, low].astype(f32)
                outs[k][at, :] = total.astype(outs[k].dtype)

    whole = pl.BlockSpec(memory_space=pltpu.VMEM)
    return pl.pallas_call(
        body,
        in_specs=[whole] * 3,
        out_specs=[whole] * XN,
        out_shape=[
            jax.ShapeDtypeStruct((rows, share), t) for t in [f32] + [bf16] * (XN - 1)
        ],
        cost_estimate=pl.CostEstimate(
            flops=2 * rows * tile * share * XN,
            bytes_accessed=8 * rows * share * XN,
            transcendentals=0,
        ),
        compiler_params=pltpu.CompilerParams(vmem_limit_bytes=32 * 1024 * 1024),
        name="near_gradient",
    )(score_grad, weight, far)


def on_device(
    layer_out,
    moe_input,
    final_gain,
    head_weight,
    clean_ids,
    levels,
    ratio_table,
    gate_weights,
    expert_ids,
    w_gate,
    w_up,
    w_down,
):
    rows, width = layer_out.shape
    n_expert = YN * ZN
    n_vocab = XN * CN
    all_rows = rows * n_expert
    own_experts = w_gate.shape[0]
    experts = own_experts * n_expert
    capacity = max(2, 2 * rows * expert_ids.shape[1] // experts)
    share = width // n_vocab
    tile = head_weight.shape[1]
    y_at, x_at, c_at = lax.axis_index("y"), lax.axis_index("x"), lax.axis_index("core")
    e_at = y_at * ZN + lax.axis_index("z")
    v_at = x_at * CN + c_at

    order = jnp.stack(
        [((x_at + k) % XN) * CN + (c_at + c) % CN for c in range(CN) for k in range(XN)]
    )
    head_turned, pair_turned, down_turned = turned_weights(
        order, head_weight, w_gate, w_up, w_down
    )

    values = layer_out.astype(f32)
    row_scale = jnp.sqrt(jnp.mean(values * values, axis=1, keepdims=True) + epsilon)
    unit_share = (
        lax.dynamic_slice_in_dim(layer_out, v_at * share, share, 1).astype(f32) / row_scale
    )
    gain_share = lax.dynamic_slice_in_dim(final_gain, v_at * share, share, 0)[None, :]
    normed_share = (unit_share * gain_share).astype(bf16)

    labels = jnp.arange(experts, dtype=jnp.int32)
    hits = expert_ids[:, :, None] == labels
    naming = jnp.sum(hits.astype(f32), axis=1)
    before = (jnp.arange(rows)[:, None] > jnp.arange(rows)[None, :]).astype(f32)
    earlier = wide_dot(before, naming, ((1,), (0,)))
    gates = jnp.sum(jnp.where(hits, gate_weights[:, :, None], 0.0), axis=1)
    slots = jnp.arange(capacity, dtype=f32)
    taken = (earlier.T[:, None, :] == slots[None, :, None]) & (naming.T[:, None, :] > 0)
    slot_gate = jnp.sum(jnp.where(taken, gates.T[:, None, :], 0.0), axis=2)
    pick = taken.astype(f32).reshape(experts * capacity, rows)
    slot_gate = slot_gate.reshape(experts * capacity, 1)

    def by_expert(a):
        a = a.reshape(n_expert, own_experts, capacity, a.shape[-1])
        return a.transpose(1, 0, 2, 3).reshape(own_experts, n_expert * capacity, a.shape[-1])

    moe_share = lax.dynamic_slice_in_dim(moe_input, v_at * share, share, 1)
    inputs = wide_dot(pick.astype(bf16), moe_share, ((1,), (0,))).astype(bf16)
    inputs = inputs.reshape(n_expert, own_experts * capacity, share)

    code = clean_ids * ratio_table.shape[0] + levels
    digits = jnp.stack([code % 256, code // 256 % 256, code // 65536]).astype(bf16)
    digits = jnp.pad(digits, ((0, 8 - digits.shape[0]), (0, share - rows)))
    spread = jnp.broadcast_to(
        jnp.concatenate([normed_share, digits], axis=0)[None], (n_expert, rows + 8, share)
    )
    spread = exchanged(spread, ("y", "z"))
    spread, head_turned, pair_turned, down_turned, inputs, pick, slot_gate = (
        lax.optimization_barrier(
            (spread, head_turned, pair_turned, down_turned, inputs, pick, slot_gate)
        )
    )
    numbers = spread[:, rows:]
    normed_near = in_ring_order(spread[:, :rows].reshape(all_rows, share), along_x, XN)
    inputs = exchanged(inputs, ("y", "z"))
    normed_near, inputs = lax.optimization_barrier((normed_near, inputs))
    normed_near = jnp.concatenate(normed_near, axis=1)
    normed_far = across_core(normed_near)

    inputs = lax.all_gather(by_expert(inputs), ("x", "core"), axis=2, tiled=True)

    side = width // 2
    numbers = numbers[:, :3, :rows].astype(jnp.int32)
    code_all = numbers[:, 0] + 256 * numbers[:, 1] + 65536 * numbers[:, 2]
    code_all = code_all.reshape(all_rows, 1)
    clean_all = code_all // ratio_table.shape[0]
    level_all = code_all % ratio_table.shape[0]
    level_labels = jnp.arange(ratio_table.shape[0], dtype=jnp.int32)
    ratio_rows = jnp.sum(
        jnp.where(level_all == level_labels[None, :], ratio_table[None, :], 0.0),
        axis=1,
        keepdims=True,
    )
    columns = (e_at * n_vocab + v_at) * tile + jnp.arange(tile, dtype=jnp.int32)
    scores = wide_dot(normed_near, head_turned[:side], ((1,), (0,))) + wide_dot(
        normed_far, head_turned[side:], ((1,), (0,))
    )
    target_hit = (clean_all == columns[None, :]).astype(f32)
    loss_scale = 1.0 / math.sqrt(all_rows)
    score_grad = lax.optimization_barrier(
        ((jnp.exp(scores) - ratio_rows * target_hit) * loss_scale).astype(bf16)
    )
    far = wide_dot(score_grad, head_turned[side:], ((1,), (1,))).astype(bf16)
    far = across_core(far)
    kept, *sent = near_gradient(score_grad, head_turned[:side], far)
    kept, sent, score_grad = lax.optimization_barrier((kept, sent, score_grad))
    sent = [along_x(a, k + 1) for k, a in enumerate(sent)]
    head_grad = head_gradient(order, normed_near, normed_far, score_grad)
    inputs, head_grad = lax.optimization_barrier((inputs, head_grad))
    gate_pre = jnp.einsum("esd,edf->esf", inputs, w_gate, preferred_element_type=f32)
    up_pre = jnp.einsum("esd,edf->esf", inputs, w_up, preferred_element_type=f32)
    sent, head_grad, gate_pre, up_pre = lax.optimization_barrier(
        (sent, head_grad, gate_pre, up_pre)
    )
    kept = kept + sum(a.astype(f32) for a in sent)
    kept = exchanged(kept.reshape(n_expert, rows, share), ("y", "z"))
    normed_grad = jnp.sum(kept, axis=0)

    gained = gain_share * normed_grad
    total = jnp.sum(unit_share * gained, axis=1)
    total = total + across_core(total)
    total = total + sum(along_x(total, k) for k in range(1, XN))
    residual_grad = (gained - unit_share * (total / width)[:, None]) / row_scale

    routed = wide_dot(pick, residual_grad, ((1,), (0,)), lax.Precision.HIGHEST)
    routed = (slot_gate * routed).astype(bf16).reshape(n_expert, own_experts * capacity, share)
    routed = lax.all_to_all(routed, ("y", "z"), 0, 0, tiled=True)
    grads = jnp.concatenate(in_ring_order(by_expert(routed), along_x, XN), axis=2)
    grads_far = across_core(grads)

    act_grad = jnp.einsum(
        "esd,efd->esf", grads, down_turned[:, :, :side], preferred_element_type=f32
    ) + jnp.einsum(
        "esd,efd->esf", grads_far, down_turned[:, :, side:], preferred_element_type=f32
    )
    sigmoid_gate = jax.nn.sigmoid(gate_pre)
    gate_grad = (
        act_grad * up_pre * sigmoid_gate * (1.0 + gate_pre * (1.0 - sigmoid_gate))
    ).astype(bf16)
    up_grad = (act_grad * gate_pre * sigmoid_gate).astype(bf16)
    pair_grad = jnp.concatenate([gate_grad, up_grad], axis=2)

    far = jnp.einsum("esf,edf->esd", pair_grad, pair_turned[:, side:], preferred_element_type=f32)
    far = across_core(far.astype(bf16))
    near = jnp.einsum("esf,edf->esd", pair_grad, pair_turned[:, :side], preferred_element_type=f32)
    near = near + far.astype(f32)
    near = near[:, :, :share] + sum(
        along_x(near[:, :, k * share:(k + 1) * share].astype(bf16), k).astype(f32)
        for k in range(1, XN)
    )
    near = near.reshape(own_experts, n_expert, capacity, share)
    near = near.transpose(1, 0, 2, 3).reshape(n_expert, own_experts * capacity, share)
    returned = lax.all_to_all(near, ("y", "z"), 0, 0, tiled=True)
    input_grad = wide_dot(
        pick,
        returned.reshape(experts * capacity, share),
        ((0,), (0,)),
        lax.Precision.HIGHEST,
    )
    return (head_grad, residual_grad, input_grad)


def solution(mesh):
    fine = Mesh(mesh.devices.reshape(YN, ZN, XN, CN), ("y", "z", "x", "core"))
    expert, vocab = ("y", "z"), ("x", "core")
    everywhere = expert + vocab
    in_specs = (
        P(expert, None),
        P(expert, None),
        P(),
        P(None, everywhere),
        P(expert),
        P(expert),
        P(),
        P(expert, None),
        P(expert, None),
        P(expert, None, vocab),
        P(expert, None, vocab),
        P(expert, vocab, None),
    )
    out_specs = (P(None, everywhere), P(expert, vocab), P(expert, vocab))
    return jax.shard_map(
        on_device, mesh=fine, in_specs=in_specs, out_specs=out_specs, check_vma=False
    )
```

profile of v0, /device:TPU:32, one launch (start us, length us, event | category | flops | bytes accessed | tf_op | source)
XLA Modules:
  0.0 258.7 jit_solution(9636953749435652026)
XLA Ops:
  11.5 11.4 %all-to-all-start = ((bf16[32,40,256]{2,1,0:T(8,128)(2,1)}), bf16[32,40,256]{2,1,0:T(8,128)(2,1)S(1)}, u32[]{:S(2)}, u32[]{:S(2)}) async-start(bf16[32,40,256]{2,1,0:T(8,128)(2,1)} %broadcast_in_dim.34), calls=%async_computation | async-start | bytes 1310720 | tf_op jit(solution)/shard_map/all_to_all | solution.py:35
  24.7 7.8 %turned_weights.1 = (bf16[2048,384]{1,0:T(8,128)(2,1)}, bf16[2,2048,256]{2,1,0:T(8,128)(2,1)}, bf16[2,128,2048]{2,1,0:T(8,128)(2,1)}) custom-call(s32[8]{0:T(128)} %stack.55.order_ref, bf16[2048,384]{1,0:T(8,128)(2,1)} %head_ref.1, bf16[2,2048,128]{2,1,0:T(8,128)(2,1)} %gate_ref.1, bf16[2,2048,128]{2,1,0:T(8,128)(2,1)} %up_ref.1, bf16[2,128,2048]{2,1,0:T(8,128)(2,1)} %down_ref.1), custom_call_target="tpu_custom_call" | custom-call | bytes 9437184 | tf_op jit(solution)/shard_map/turned_weights/pallas_call | solution.py:55
  32.9 10.2 %all-to-all-done = bf16[32,40,256]{2,1,0:T(8,128)(2,1)S(1)} async-done(((bf16[32,40,256]{2,1,0:T(8,128)(2,1)}), bf16[32,40,256]{2,1,0:T(8,128)(2,1)S(1)}, u32[]{:S(2)}, u32[]{:S(2)}) %all-to-all-start) | async-done | bytes 655392 | tf_op jit(solution)/shard_map/all_to_all | solution.py:35
  43.2 2.8 %collective-permute-start = (bf16[1024,256]{1,0:T(8,128)(2,1)S(1)}, bf16[1024,256]{1,0:T(8,128)(2,1)S(1)}, u32[]{:S(2)}, u32[]{:S(2)}) collective-permute-start(bf16[1024,256]{1,0:T(8,128)(2,1)S(1)} %bitcast.72), channel_id=1, source_target_pairs={{0,6},{2,0},{4,2},{6,4},{1,7},{3,1},{5,3},{7,5},{8,14},{10,8},{12,... | collective-permute-start | bytes 1572872 | tf_op jit(solution)/shard_map/ppermute | solution.py:27
  47.7 16.0 %all_to_all.25 = bf16[32,16,256]{2,1,0:T(8,128)(2,1)S(1)} all-to-all(bf16[32,16,256]{2,1,0:T(8,128)(2,1)S(1)} %bitcast.77), channel_id=1, replica_groups=mesh['y'=4,'z'=8,'x'=4,'core'=2] {'y','z'}, dimensions={0} | all-to-all | bytes 524288 | tf_op jit(solution)/shard_map/all_to_all | solution.py:35
  63.7 2.5 collective-permute-done
  66.1 3.7 %collective-permute-done.2 = bf16[1024,256]{1,0:T(8,128)(2,1)S(1)} collective-permute-done((bf16[1024,256]{1,0:T(8,128)(2,1)S(1)}, bf16[1024,256]{1,0:T(8,128)(2,1)S(1)}, u32[]{:S(2)}, u32[]{:S(2)}) %collective-permute-start.2) | collective-permute-done | bytes 524320 | tf_op jit(solution)/shard_map/ppermute | solution.py:27
  71.6 2.9 %collective-permute-done.3.far_ref = bf16[1024,1024]{1,0:T(8,128)(2,1)} collective-permute-done((bf16[1024,1024]{1,0:T(8,128)(2,1)S(1)}, bf16[1024,1024]{1,0:T(8,128)(2,1)}, u32[]{:S(2)}, u32[]{:S(2)}) %collective-permute-start.3) | collective-permute-done | bytes 2097184 | tf_op jit(solution)/shard_map/ppermute | solution.py:31
  74.5 3.0 %fusion.7 = f32[1024,384]{1,0:T(8,128)S(1)} fusion(bf16[1024,1024]{1,0:T(8,128)(2,1)} %collective-permute-done.3.far_ref, bf16[2048,384]{1,0:T(8,128)(2,1)} %get-tuple-element.44), kind=kOutput, calls=%fused_computation.14 | convolution fusion | flops 805306368 | bytes 4456448 | tf_op jit(solution)/shard_map/dot_general | solution.py:17
  77.5 1.5 multiply_convert_fusion.grad_ref
  80.6 3.9 %collective-permute-done.4.far_ref = bf16[1024,1024]{1,0:T(8,128)(2,1)S(1)} collective-permute-done((bf16[1024,1024]{1,0:T(8,128)(2,1)S(1)}, bf16[1024,1024]{1,0:T(8,128)(2,1)S(1)}, u32[]{:S(2)}, u32[]{:S(2)}) %collective-permute-start.4) | collective-permute-done | bytes 2097184 | tf_op jit(solution)/shard_map/ppermute | solution.py:31
  84.5 1.3 near_gradient.1
  85.8 9.2 %head_gradient.1 = f32[2048,384]{1,0:T(8,128)} custom-call(s32[8]{0:T(128)} %stack.55.order_ref, bf16[1024,1024]{1,0:T(8,128)(2,1)} %copy-done.4, bf16[1024,1024]{1,0:T(8,128)(2,1)} %collective-permute-done.3.far_ref, bf16[1024,384]{1,0:T(8,128)(2,1)} %copy-done.1), custom_call_target="tpu_custom_call" | custom-call | flops 1610612736 | bytes 8126464 | tf_op jit(solution)/shard_map/head_gradient/pallas_call | solution.py:101
  95.0 2.3 all-gather.2.cloned.1.call-done
  98.2 2.6 collective-permute-start.6
  100.8 1.8 collective-permute-start.7
  102.6 2.5 fusion.45
  105.9 7.1 %collective-permute-done.5 = bf16[1024,256]{1,0:T(8,128)(2,1)S(1)} collective-permute-done((bf16[1024,256]{1,0:T(8,128)(2,1)S(1)}, bf16[1024,256]{1,0:T(8,128)(2,1)S(1)}, u32[]{:S(2)}, u32[]{:S(2)}) %collective-permute-start.5) | collective-permute-done | bytes 524320 | tf_op jit(solution)/shard_map/ppermute | solution.py:27
  113.0 11.1 %collective-permute-done.6 = bf16[1024,256]{1,0:T(8,128)(2,1)S(1)} collective-permute-done((bf16[1024,256]{1,0:T(8,128)(2,1)S(1)}, bf16[1024,256]{1,0:T(8,128)(2,1)S(1)}, u32[]{:S(2)}, u32[]{:S(2)}) %collective-permute-start.6) | collective-permute-done | bytes 524320 | tf_op jit(solution)/shard_map/ppermute | solution.py:27
  124.6 37.7 %all_to_all.26 = f32[32,32,256]{2,1,0:T(8,128)S(1)} all-to-all(f32[32,32,256]{2,1,0:T(8,128)S(1)} %bitcast.71), channel_id=1, replica_groups=mesh['y'=4,'z'=8,'x'=4,'core'=2] {'y','z'}, dimensions={0} | all-to-all | bytes 2097152 | tf_op jit(solution)/shard_map/all_to_all | solution.py:35
  164.6 2.8 %collective-permute-start.10 = (f32[32]{0:T(128)S(1)}, f32[32]{0:T(128)S(1)}, u32[]{:S(2)}, u32[]{:S(2)}) collective-permute-start(f32[32]{0:T(128)S(1)} %add.274), channel_id=1, source_target_pairs={{0,4},{2,6},{4,0},{6,2},{1,5},{3,7},{5,1},{7,3},{8,12},{10,14},{12... | collective-permute-start | bytes 392 | tf_op jit(solution)/shard_map/ppermute | solution.py:27
  167.4 2.1 collective-permute-start.11
  170.9 3.3 %collective-permute-done.9 = f32[32]{0:T(128)S(1)} collective-permute-done((f32[32]{0:T(128)S(1)}, f32[32]{0:T(128)S(1)}, u32[]{:S(2)}, u32[]{:S(2)}) %collective-permute-start.9) | collective-permute-done | bytes 160 | tf_op jit(solution)/shard_map/ppermute | solution.py:27
  175.6 16.1 %all_to_all.27 = bf16[32,16,256]{2,1,0:T(8,128)(2,1)S(1)} all-to-all(bf16[32,16,256]{2,1,0:T(8,128)(2,1)S(1)} %bitcast.78), channel_id=1, replica_groups=mesh['y'=4,'z'=8,'x'=4,'core'=2] {'y','z'}, dimensions={0} | all-to-all | bytes 524288 | tf_op jit(solution)/shard_map/all_to_all | solution.py:283
  193.9 6.0 %collective-permute-done.12 = bf16[2,256,256]{2,1,0:T(8,128)(2,1)S(1)} collective-permute-done((bf16[2,256,256]{2,1,0:T(8,128)(2,1)S(1)}, bf16[2,256,256]{2,1,0:T(8,128)(2,1)S(1)}, u32[]{:S(2)}, u32[]{:S(2)}) %collective-permute-start.12) | collective-permute-done | bytes 262176 | tf_op jit(solution)/shard_map/ppermute | solution.py:27
  199.8 1.7 collective-permute-done.13
  201.6 2.7 %collective-permute-done.14 = bf16[2,256,256]{2,1,0:T(8,128)(2,1)S(1)} collective-permute-done((bf16[2,256,256]{2,1,0:T(8,128)(2,1)S(1)}, bf16[2,256,256]{2,1,0:T(8,128)(2,1)S(1)}, u32[]{:S(2)}, u32[]{:S(2)}) %collective-permute-start.14) | collective-permute-done | bytes 262176 | tf_op jit(solution)/shard_map/ppermute | solution.py:27
  204.5 2.6 %collective-permute-done.15 = bf16[2,256,1024]{2,1,0:T(8,128)(2,1)S(1)} collective-permute-done((bf16[2,256,1024]{2,1,0:T(8,128)(2,1)S(1)}, bf16[2,256,1024]{2,1,0:T(8,128)(2,1)S(1)}, u32[]{:S(2)}, u32[]{:S(2)}) %collective-permute-start.15) | collective-permute-done | bytes 1048608 | tf_op jit(solution)/shard_map/ppermute | solution.py:31
  209.9 2.5 collective-permute-done.16
  213.0 2.6 collective-permute-start.18
  216.4 11.8 %collective-permute-done.17 = bf16[2,256,256]{2,1,0:T(8,128)(2,1)S(1)} collective-permute-done((bf16[2,256,256]{2,1,0:T(8,128)(2,1)S(1)}, bf16[2,256,256]{2,1,0:T(8,128)(2,1)S(1)}, u32[]{:S(2)}, u32[]{:S(2)}) %collective-permute-start.17) | collective-permute-done | bytes 262176 | tf_op jit(solution)/shard_map/ppermute | solution.py:27
  228.9 21.7 %all_to_all.28 = f32[32,16,256]{2,1,0:T(8,128)S(1)} all-to-all(f32[32,16,256]{2,1,0:T(8,128)S(1)} %copy_bitcast_fusion), channel_id=1, replica_groups=mesh['y'=4,'z'=8,'x'=4,'core'=2] {'y','z'}, dimensions={0} | all-to-all | bytes 1048576 | tf_op jit(solution)/shard_map/all_to_all | solution.py:309
  (101 shorter events, 27.1 us)
Async XLA Ops:
  7.2 25.4 %copy-start = (bf16[32,2048]{1,0:T(8,128)(2,1)S(1)}, bf16[32,2048]{1,0:T(8,128)(2,1)}, u32[]{:S(2)}) copy-start(bf16[32,2048]{1,0:T(8,128)(2,1)} %param.13) | copy-start | bytes 393220
  7.2 15.8 %copy-start.8 = (s32[32,8]{0,1:T(8,128)S(1)}, s32[32,8]{0,1:T(8,128)}, u32[]{:S(2)}) copy-start(s32[32,8]{0,1:T(8,128)} %param.20) | copy-start | bytes 3076
  7.2 15.9 %copy-start.9 = (f32[32,8]{0,1:T(8,128)S(1)}, f32[32,8]{0,1:T(8,128)}, u32[]{:S(2)}) copy-start(f32[32,8]{0,1:T(8,128)} %param.19) | copy-start | bytes 3076
  11.5 31.6 %all-to-all-start = ((bf16[32,40,256]{2,1,0:T(8,128)(2,1)}), bf16[32,40,256]{2,1,0:T(8,128)(2,1)S(1)}, u32[]{:S(2)}, u32[]{:S(2)}) async-start(bf16[32,40,256]{2,1,0:T(8,128)(2,1)} %broadcast_in_dim.34), calls=%async_computation | async-start | bytes 1310720 | tf_op jit(solution)/shard_map/all_to_all | solution.py:35
  22.8 74.4 %all-gather.2.cloned.1.call-start = ((), (), s32[]{:S(2)}) async-start(), calls=%async_computation.5 | async-start | bytes 2359296 | tf_op jit(solution)/shard_map/all_gather | solution.py:236
  43.2 23.0 %collective-permute-start = (bf16[1024,256]{1,0:T(8,128)(2,1)S(1)}, bf16[1024,256]{1,0:T(8,128)(2,1)S(1)}, u32[]{:S(2)}, u32[]{:S(2)}) collective-permute-start(bf16[1024,256]{1,0:T(8,128)(2,1)S(1)} %bitcast.72), channel_id=1, source_target_pairs={{0,6},{2,0},{4,2},{6,4},{1,7},{3,1},{5,3},{7,5},{8,14},{10,8},{12,... | collective-permute-start | bytes 1572872 | tf_op jit(solution)/shard_map/ppermute | solution.py:27
  46.0 20.1 %collective-permute-start.1 = (bf16[1024,256]{1,0:T(8,128)(2,1)S(1)}, bf16[1024,256]{1,0:T(8,128)(2,1)S(1)}, u32[]{:S(2)}, u32[]{:S(2)}) collective-permute-start(bf16[1024,256]{1,0:T(8,128)(2,1)S(1)} %bitcast.73), channel_id=1, source_target_pairs={{0,4},{2,6},{4,0},{6,2},{1,5},{3,7},{5,1},{7,3},{8,12},{10,14},{12... | collective-permute-start | bytes 1572872 | tf_op jit(solution)/shard_map/ppermute | solution.py:27
  46.8 23.0 %collective-permute-start.2 = (bf16[1024,256]{1,0:T(8,128)(2,1)S(1)}, bf16[1024,256]{1,0:T(8,128)(2,1)S(1)}, u32[]{:S(2)}, u32[]{:S(2)}) collective-permute-start(bf16[1024,256]{1,0:T(8,128)(2,1)S(1)} %bitcast.74), channel_id=1, source_target_pairs={{0,2},{2,4},{4,6},{6,0},{1,3},{3,5},{5,7},{7,1},{8,10},{10,12},{12... | collective-permute-start | bytes 1572872 | tf_op jit(solution)/shard_map/ppermute | solution.py:27
  70.1 7.4 %copy-start.4 = (bf16[1024,1024]{1,0:T(8,128)(2,1)}, bf16[1024,1024]{1,0:T(8,128)(2,1)S(1)}, u32[]{:S(2)}) copy-start(bf16[1024,1024]{1,0:T(8,128)(2,1)S(1)} %constant_dynamic-update-slice_fusion.near_ref) | copy-start | bytes 6291460
  70.1 4.4 %collective-permute-start.3 = (bf16[1024,1024]{1,0:T(8,128)(2,1)S(1)}, bf16[1024,1024]{1,0:T(8,128)(2,1)}, u32[]{:S(2)}, u32[]{:S(2)}) collective-permute-start(bf16[1024,1024]{1,0:T(8,128)(2,1)S(1)} %constant_dynamic-update-slice_fusion.near_ref), channel_id=1, source_target_pairs={{0,1},{1,0},{2,3},{3,2},{4,5},{5,4},{6,7},{7,6},{8,9},{9,8},{10,11... | collective-permute-start | bytes 6291464 | tf_op jit(solution)/shard_map/ppermute | solution.py:31
  71.6 5.9 %copy-start.6 = (bf16[2048,384]{1,0:T(8,128)(2,1)S(1)}, bf16[2048,384]{1,0:T(8,128)(2,1)}, u32[]{:S(2)}) copy-start(bf16[2048,384]{1,0:T(8,128)(2,1)} %get-tuple-element.44) | copy-start | bytes 4718596
  79.0 5.6 %copy-start.1 = (bf16[1024,384]{1,0:T(8,128)(2,1)}, bf16[1024,384]{1,0:T(8,128)(2,1)S(1)}, u32[]{:S(2)}) copy-start(bf16[1024,384]{1,0:T(8,128)(2,1)S(1)} %multiply_convert_fusion.grad_ref) | copy-start | bytes 2359300
  80.3 4.2 %collective-permute-start.4 = (bf16[1024,1024]{1,0:T(8,128)(2,1)S(1)}, bf16[1024,1024]{1,0:T(8,128)(2,1)S(1)}, u32[]{:S(2)}, u32[]{:S(2)}) collective-permute-start(bf16[1024,1024]{1,0:T(8,128)(2,1)S(1)} %convolution_convert_fusion), channel_id=1, source_target_pairs={{0,1},{1,0},{2,3},{3,2},{4,5},{5,4},{6,7},{7,6},{8,9},{9,8},{10,11... | collective-permute-start | bytes 6291464 | tf_op jit(solution)/shard_map/ppermute | solution.py:31
  97.3 7.9 %copy-start.2 = (bf16[2,256,2048]{2,1,0:T(8,128)(2,1)S(1)}, bf16[2,256,2048]{2,1,0:T(8,128)(2,1)}, u32[]{:S(2)}) copy-start(bf16[2,256,2048]{2,1,0:T(8,128)(2,1)} %all-gather.2.cloned.1.call-done) | copy-start | bytes 6291460
  97.3 7.9 %copy-start.3 = (bf16[2,2048,128]{2,1,0:T(8,128)(2,1)S(1)}, bf16[2,2048,128]{2,1,0:T(8,128)(2,1)}, u32[]{:S(2)}) copy-start(bf16[2,2048,128]{2,1,0:T(8,128)(2,1)} %up_ref.1) | copy-start | bytes 3145732
  97.3 15.7 %collective-permute-start.5 = (bf16[1024,256]{1,0:T(8,128)(2,1)S(1)}, bf16[1024,256]{1,0:T(8,128)(2,1)S(1)}, u32[]{:S(2)}, u32[]{:S(2)}) collective-permute-start(bf16[1024,256]{1,0:T(8,128)(2,1)S(1)} %get-tuple-element.49), channel_id=1, source_target_pairs={{0,2},{2,4},{4,6},{6,0},{1,3},{3,5},{5,7},{7,1},{8,10},{10,12},{12... | collective-permute-start | bytes 1572872 | tf_op jit(solution)/shard_map/ppermute | solution.py:27
  98.2 25.8 %collective-permute-start.6 = (bf16[1024,256]{1,0:T(8,128)(2,1)S(1)}, bf16[1024,256]{1,0:T(8,128)(2,1)S(1)}, u32[]{:S(2)}, u32[]{:S(2)}) collective-permute-start(bf16[1024,256]{1,0:T(8,128)(2,1)S(1)} %get-tuple-element.50), channel_id=1, source_target_pairs={{0,4},{2,6},{4,0},{6,2},{1,5},{3,7},{5,1},{7,3},{8,12},{10,14},{12... | collective-permute-start | bytes 1572872 | tf_op jit(solution)/shard_map/ppermute | solution.py:27
  100.8 23.6 %collective-permute-start.7 = (bf16[1024,256]{1,0:T(8,128)(2,1)S(1)}, bf16[1024,256]{1,0:T(8,128)(2,1)S(1)}, u32[]{:S(2)}, u32[]{:S(2)}) collective-permute-start(bf16[1024,256]{1,0:T(8,128)(2,1)S(1)} %get-tuple-element.51), channel_id=1, source_target_pairs={{0,6},{2,0},{4,2},{6,4},{1,7},{3,1},{5,3},{7,5},{8,14},{10,8},{12,... | collective-permute-start | bytes 1572872 | tf_op jit(solution)/shard_map/ppermute | solution.py:27
  162.4 44.7 %copy-start.11 = (bf16[2,128,2048]{2,1,0:T(8,128)(2,1)S(1)}, bf16[2,128,2048]{2,1,0:T(8,128)(2,1)}, u32[]{:S(2)}) copy-start(bf16[2,128,2048]{2,1,0:T(8,128)(2,1)} %get-tuple-element.63) | copy-start | bytes 3145732
  163.4 1.2 collective-permute-start.8
  164.6 5.0 %collective-permute-start.10 = (f32[32]{0:T(128)S(1)}, f32[32]{0:T(128)S(1)}, u32[]{:S(2)}, u32[]{:S(2)}) collective-permute-start(f32[32]{0:T(128)S(1)} %add.274), channel_id=1, source_target_pairs={{0,4},{2,6},{4,0},{6,2},{1,5},{3,7},{5,1},{7,3},{8,12},{10,14},{12... | collective-permute-start | bytes 392 | tf_op jit(solution)/shard_map/ppermute | solution.py:27
  167.4 3.5 %collective-permute-start.11 = (f32[32]{0:T(128)S(1)}, f32[32]{0:T(128)S(1)}, u32[]{:S(2)}, u32[]{:S(2)}) collective-permute-start(f32[32]{0:T(128)S(1)} %add.274), channel_id=1, source_target_pairs={{0,6},{2,0},{4,2},{6,4},{1,7},{3,1},{5,3},{7,5},{8,14},{10,8},{12,... | collective-permute-start | bytes 392 | tf_op jit(solution)/shard_map/ppermute | solution.py:27
  169.5 4.8 %collective-permute-start.9 = (f32[32]{0:T(128)S(1)}, f32[32]{0:T(128)S(1)}, u32[]{:S(2)}, u32[]{:S(2)}) collective-permute-start(f32[32]{0:T(128)S(1)} %add.274), channel_id=1, source_target_pairs={{0,2},{2,4},{4,6},{6,0},{1,3},{3,5},{5,7},{7,1},{8,10},{10,12},{12... | collective-permute-start | bytes 392 | tf_op jit(solution)/shard_map/ppermute | solution.py:27
  175.0 32.6 %copy-start.7 = (f32[32,256]{1,0:T(8,128)}, f32[32,256]{1,0:T(8,128)S(1)}, u32[]{:S(2)}) copy-start(f32[32,256]{1,0:T(8,128)S(1)} %subtract_divide_fusion) | copy-start | bytes 98308
  191.8 8.1 %collective-permute-start.12 = (bf16[2,256,256]{2,1,0:T(8,128)(2,1)S(1)}, bf16[2,256,256]{2,1,0:T(8,128)(2,1)S(1)}, u32[]{:S(2)}, u32[]{:S(2)}) collective-permute-start(bf16[2,256,256]{2,1,0:T(8,128)(2,1)S(1)} %copy_bitcast_fusion.1), channel_id=1, source_target_pairs={{0,6},{2,0},{4,2},{6,4},{1,7},{3,1},{5,3},{7,5},{8,14},{10,8},{12,... | collective-permute-start | bytes 786440 | tf_op jit(solution)/shard_map/ppermute | solution.py:27
  191.9 9.6 %collective-permute-start.13 = (bf16[2,256,256]{2,1,0:T(8,128)(2,1)S(1)}, bf16[2,256,256]{2,1,0:T(8,128)(2,1)S(1)}, u32[]{:S(2)}, u32[]{:S(2)}) collective-permute-start(bf16[2,256,256]{2,1,0:T(8,128)(2,1)S(1)} %copy_bitcast_fusion.1), channel_id=1, source_target_pairs={{0,4},{2,6},{4,0},{6,2},{1,5},{3,7},{5,1},{7,3},{8,12},{10,14},{12... | collective-permute-start | bytes 786440 | tf_op jit(solution)/shard_map/ppermute | solution.py:27
  192.8 11.4 %collective-permute-start.14 = (bf16[2,256,256]{2,1,0:T(8,128)(2,1)S(1)}, bf16[2,256,256]{2,1,0:T(8,128)(2,1)S(1)}, u32[]{:S(2)}, u32[]{:S(2)}) collective-permute-start(bf16[2,256,256]{2,1,0:T(8,128)(2,1)S(1)} %copy_bitcast_fusion.1), channel_id=1, source_target_pairs={{0,2},{2,4},{4,6},{6,0},{1,3},{3,5},{5,7},{7,1},{8,10},{10,12},{12... | collective-permute-start | bytes 786440 | tf_op jit(solution)/shard_map/ppermute | solution.py:27
  204.4 2.7 %collective-permute-start.15 = (bf16[2,256,1024]{2,1,0:T(8,128)(2,1)S(1)}, bf16[2,256,1024]{2,1,0:T(8,128)(2,1)S(1)}, u32[]{:S(2)}, u32[]{:S(2)}) collective-permute-start(bf16[2,256,1024]{2,1,0:T(8,128)(2,1)S(1)} %pad_maximum_fusion), channel_id=1, source_target_pairs={{0,1},{1,0},{2,3},{3,2},{4,5},{5,4},{6,7},{7,6},{8,9},{9,8},{10,11... | collective-permute-start | bytes 3145736 | tf_op jit(solution)/shard_map/ppermute | solution.py:31
  209.7 2.7 %collective-permute-start.16 = (bf16[2,256,1024]{2,1,0:T(8,128)(2,1)S(1)}, bf16[2,256,1024]{2,1,0:T(8,128)(2,1)S(1)}, u32[]{:S(2)}, u32[]{:S(2)}) collective-permute-start(bf16[2,256,1024]{2,1,0:T(8,128)(2,1)S(1)} %convolution_convert_fusion.1), channel_id=1, source_target_pairs={{0,1},{1,0},{2,3},{3,2},{4,5},{5,4},{6,7},{7,6},{8,9},{9,8},{10,11... | collective-permute-start | bytes 3145736 | tf_op jit(solution)/shard_map/ppermute | solution.py:31
  212.9 15.3 %collective-permute-start.17 = (bf16[2,256,256]{2,1,0:T(8,128)(2,1)S(1)}, bf16[2,256,256]{2,1,0:T(8,128)(2,1)S(1)}, u32[]{:S(2)}, u32[]{:S(2)}) collective-permute-start(bf16[2,256,256]{2,1,0:T(8,128)(2,1)S(1)} %get-tuple-element.69), channel_id=1, source_target_pairs={{0,2},{2,4},{4,6},{6,0},{1,3},{3,5},{5,7},{7,1},{8,10},{10,12},{12... | collective-permute-start | bytes 786440 | tf_op jit(solution)/shard_map/ppermute | solution.py:27
  213.0 15.2 %collective-permute-start.18 = (bf16[2,256,256]{2,1,0:T(8,128)(2,1)S(1)}, bf16[2,256,256]{2,1,0:T(8,128)(2,1)S(1)}, u32[]{:S(2)}, u32[]{:S(2)}) collective-permute-start(bf16[2,256,256]{2,1,0:T(8,128)(2,1)S(1)} %get-tuple-element.71), channel_id=1, source_target_pairs={{0,4},{2,6},{4,0},{6,2},{1,5},{3,7},{5,1},{7,3},{8,12},{10,14},{12... | collective-permute-start | bytes 786440 | tf_op jit(solution)/shard_map/ppermute | solution.py:27
  215.6 13.2 %collective-permute-start.19 = (bf16[2,256,256]{2,1,0:T(8,128)(2,1)S(1)}, bf16[2,256,256]{2,1,0:T(8,128)(2,1)S(1)}, u32[]{:S(2)}, u32[]{:S(2)}) collective-permute-start(bf16[2,256,256]{2,1,0:T(8,128)(2,1)S(1)} %get-tuple-element.70), channel_id=1, source_target_pairs={{0,6},{2,0},{4,2},{6,4},{1,7},{3,1},{5,3},{7,5},{8,14},{10,8},{12,... | collective-permute-start | bytes 786440 | tf_op jit(solution)/shard_map/ppermute | solution.py:27
  (2 other events, 3.2 us)
Sparse Core Ops, SparseCore 0:
  71.6 25.6 all-gather.1
where the time goes:
time: 260 us; the launch traced here: 259 us
  blocking collectives  91.6 us (35%)
  waiting for transfers between devices  77.9 us (30%)
  starting transfers between devices  32.3 us (12%)
  Pallas kernels  18.2 us (7%)
  between operations  14.6 us (6%)
  matrix products  13 us (5%)
  other arithmetic  5.71 us (2%)
  local copies, waits for them, and re-layouts  5.45 us (2%)
    all_to_all x2, blocking collectives, exchanged(): return lax.all_to_all(a, axes, 0, 0, tiled=True)  53.7 us
    ppermute x15, waiting for transfers between devices, along_x(): return lax.ppermute(a, 'x', [(p, (p + step) % XN) for p in range(XN)])  52.2 us
    all_to_all x1, blocking collectives, on_device(): returned = lax.all_to_all(near, ('y', 'z'), 0, 0, tiled=True)  21.7 us
    ppermute x15, starting transfers between devices, along_x(): return lax.ppermute(a, 'x', [(p, (p + step) % XN) for p in range(XN)])  20.2 us
    all_to_all x1, blocking collectives, on_device(): routed = lax.all_to_all(routed, ('y', 'z'), 0, 0, tiled=True)  16.1 us
    ppermute x5, waiting for transfers between devices, across_core(): return lax.ppermute(a, 'core', [(p, CN - 1 - p) for p in range(CN)])  13.1 us
    all_to_all x1, starting transfers between devices, exchanged(): return lax.all_to_all(a, axes, 0, 0, tiled=True)  11.4 us
    all_to_all x1, waiting for transfers between devices, exchanged(): return lax.all_to_all(a, axes, 0, 0, tiled=True)  10.2 us
  transfers between devices with their start and end apart: 22, of which 20 were waited for; matrix products, arithmetic and copies ran while one was open for 5% of the time, Pallas kernels for 7%

commit v1 on v0

--- a/solution.py
+++ b/solution.py
@@ -111,11 +111,7 @@
             out_specs=pl.BlockSpec((share, tile), lambda i, s: (s[i], 0)),
         ),
         out_shape=jax.ShapeDtypeStruct((2 * side, tile), f32),
-        cost_estimate=pl.CostEstimate(
-            flops=4 * rows * side * tile,
-            bytes_accessed=4 * rows * side + 2 * rows * tile + 8 * side * tile,
-            transcendentals=0,
-        ),
+        cost_estimate=pl.CostEstimate(flops=1024, bytes_accessed=1024, transcendentals=0),
         name="head_gradient",
     )(order, near, far, score_grad)
 
@@ -253,35 +249,38 @@
     )
     target_hit = (clean_all == columns[None, :]).astype(f32)
     loss_scale = 1.0 / math.sqrt(all_rows)
-    score_grad = lax.optimization_barrier(
-        ((jnp.exp(scores) - ratio_rows * target_hit) * loss_scale).astype(bf16)
-    )
+    score_grad = ((jnp.exp(scores) - ratio_rows * target_hit) * loss_scale).astype(bf16)
+    along = jnp.sum(score_grad.astype(f32) * scores, axis=1)
+    score_grad, along = lax.optimization_barrier((score_grad, along))
     far = wide_dot(score_grad, head_turned[side:], ((1,), (1,))).astype(bf16)
     far = across_core(far)
     kept, *sent = near_gradient(score_grad, head_turned[:side], far)
-    kept, sent, score_grad = lax.optimization_barrier((kept, sent, score_grad))
+    kept, sent, score_grad, along = lax.optimization_barrier((kept, sent, score_grad, along))
     sent = [along_x(a, k + 1) for k, a in enumerate(sent)]
+    along = jnp.pad(along.reshape(n_expert, 1, rows), ((0, 0), (0, 7), (0, 128 - rows)))
+    along = jnp.sum(exchanged(along, ("y", "z")), axis=0)
+    along = along + across_core(along)
+    along = along + sum(along_x(along, k) for k in range(1, XN))
+    along, score_grad = lax.optimization_barrier((along, score_grad))
     head_grad = head_gradient(order, normed_near, normed_far, score_grad)
-    inputs, head_grad = lax.optimization_barrier((inputs, head_grad))
+    sent, head_grad, along = lax.optimization_barrier((sent, head_grad, along))
+    kept = (kept + sum(a.astype(f32) for a in sent)).astype(bf16)
+    kept = exchanged(kept.reshape(n_expert, rows, share), ("y", "z"))
+    normed_grad = jnp.sum(kept.astype(f32), axis=0)
+
+    residual_grad = (
+        gain_share * normed_grad - unit_share * (along[0, :rows] / width)[:, None]
+    ) / row_scale
+
+    routed = wide_dot(pick, residual_grad, ((1,), (0,)), lax.Precision.HIGHEST)
+    routed = (slot_gate * routed).astype(bf16).reshape(n_expert, own_experts * capacity, share)
+    routed = exchanged(routed, ("y", "z"))
+    routed, inputs = lax.optimization_barrier((routed, inputs))
     gate_pre = jnp.einsum("esd,edf->esf", inputs, w_gate, preferred_element_type=f32)
     up_pre = jnp.einsum("esd,edf->esf", inputs, w_up, preferred_element_type=f32)
-    sent, head_grad, gate_pre, up_pre = lax.optimization_barrier(
-        (sent, head_grad, gate_pre, up_pre)
-    )
-    kept = kept + sum(a.astype(f32) for a in sent)
-    kept = exchanged(kept.reshape(n_expert, rows, share), ("y", "z"))
-    normed_grad = jnp.sum(kept, axis=0)
-
-    gained = gain_share * normed_grad
-    total = jnp.sum(unit_share * gained, axis=1)
-    total = total + across_core(total)
-    total = total + sum(along_x(total, k) for k in range(1, XN))
-    residual_grad = (gained - unit_share * (total / width)[:, None]) / row_scale
-
-    routed = wide_dot(pick, residual_grad, ((1,), (0,)), lax.Precision.HIGHEST)
-    routed = (slot_gate * routed).astype(bf16).reshape(n_expert, own_experts * capacity, share)
-    routed = lax.all_to_all(routed, ("y", "z"), 0, 0, tiled=True)
-    grads = jnp.concatenate(in_ring_order(by_expert(routed), along_x, XN), axis=2)
+    grads = in_ring_order(by_expert(routed), along_x, XN)
+    grads, gate_pre, up_pre = lax.optimization_barrier((grads, gate_pre, up_pre))
+    grads = jnp.concatenate(grads, axis=2)
     grads_far = across_core(grads)
 
     act_grad = jnp.einsum(

time: 260 us -> 248 us (0.954)
  blocking collectives: 91.6 us -> 54.5 us
  waiting for transfers between devices: 77.9 us -> 91.6 us
  starting transfers between devices: 32.3 us -> 40.3 us
    all_to_all x1 -> x3, waiting for transfers between devices: 10.2 us -> 36.6 us  [exchanged(): return lax.all_to_all(a, axes, 0, 0, tiled=True)]
    all_to_all x2, blocking collectives: 53.7 us -> 32.3 us  [exchanged(): return lax.all_to_all(a, axes, 0, 0, tiled=True)]
    all_to_all x1 -> x0, blocking collectives: 16.1 us -> none  [on_device(): routed = lax.all_to_all(routed, ('y', 'z'), 0, 0, tiled=True)]
    all_to_all x1 -> x3, starting transfers between devices: 11.4 us -> 23.5 us  [exchanged(): return lax.all_to_all(a, axes, 0, 0, tiled=True)]
    ppermute x15, waiting for transfers between devices: 52.2 us -> 42.4 us  [along_x(): return lax.ppermute(a, 'x', [(p, (p + step) % XN) for p in range(XN)])]
    ppermute x15, starting transfers between devices: 20.2 us -> 15.9 us  [along_x(): return lax.ppermute(a, 'x', [(p, (p + step) % XN) for p in range(XN)])]
  transfers between devices with their start and end apart: 22 -> 24, of which waited for: 20 -> 18; matrix products, arithmetic and copies ran while one was open for 5% -> 5% of each run, Pallas kernels for 7% -> 8%
where the time goes in v1:
time: 248 us; the launch traced here: 247 us
  waiting for transfers between devices  91.6 us (37%)
  blocking collectives  54.5 us (22%)
  starting transfers between devices  40.3 us (16%)
  Pallas kernels  18.8 us (8%)
  matrix products  14.9 us (6%)
  between operations  14.6 us (6%)
  local copies, waits for them, and re-layouts  6.52 us (3%)
  other arithmetic  6.19 us (2%)
    ppermute x15, waiting for transfers between devices, along_x(): return lax.ppermute(a, 'x', [(p, (p + step) % XN) for p in range(XN)])  42.4 us
    all_to_all x3, waiting for transfers between devices, exchanged(): return lax.all_to_all(a, axes, 0, 0, tiled=True)  36.6 us
    all_to_all x2, blocking collectives, exchanged(): return lax.all_to_all(a, axes, 0, 0, tiled=True)  32.3 us
    all_to_all x3, starting transfers between devices, exchanged(): return lax.all_to_all(a, axes, 0, 0, tiled=True)  23.5 us
    all_to_all x1, blocking collectives, on_device(): returned = lax.all_to_all(near, ('y', 'z'), 0, 0, tiled=True)  22.3 us
    ppermute x15, starting transfers between devices, along_x(): return lax.ppermute(a, 'x', [(p, (p + step) % XN) for p in range(XN)])  15.9 us
    ppermute x5, waiting for transfers between devices, across_core(): return lax.ppermute(a, 'core', [(p, CN - 1 - p) for p in range(CN)])  12.5 us
    dot_general x7, matrix products, wide_dot(): lax.dot_general(a, b, (dims, ((), ())), preferred_element_type=f32, preci...  10.1 us
  transfers between devices with their start and end apart: 24, of which 18 were waited for; matrix products, arithmetic and copies ran while one was open for 5% of the time, Pallas kernels for 8%

profile of v1, /device:TPU:32, one launch (start us, length us, event | category | flops | bytes accessed | tf_op | source)
XLA Modules:
  0.0 247.4 jit_solution(14922158276948121620)
XLA Ops:
  11.5 11.4 %all-to-all-start = ((bf16[32,40,256]{2,1,0:T(8,128)(2,1)}), bf16[32,40,256]{2,1,0:T(8,128)(2,1)S(1)}, u32[]{:S(2)}, u32[]{:S(2)}) async-start(bf16[32,40,256]{2,1,0:T(8,128)(2,1)} %broadcast_in_dim.34), calls=%async_computation | async-start | bytes 1310720 | tf_op jit(solution)/shard_map/all_to_all | solution.py:35
  24.6 7.8 %turned_weights.1 = (bf16[2048,384]{1,0:T(8,128)(2,1)}, bf16[2,2048,256]{2,1,0:T(8,128)(2,1)}, bf16[2,128,2048]{2,1,0:T(8,128)(2,1)}) custom-call(s32[8]{0:T(128)} %stack.55.order_ref, bf16[2048,384]{1,0:T(8,128)(2,1)} %head_ref.1, bf16[2,2048,128]{2,1,0:T(8,128)(2,1)} %gate_ref.1, bf16[2,2048,128]{2,1,0:T(8,128)(2,1)} %up_ref.1, bf16[2,128,2048]{2,1,0:T(8,128)(2,1)} %down_ref.1), custom_call_target="tpu_custom_call" | custom-call | bytes 9437184 | tf_op jit(solution)/shard_map/turned_weights/pallas_call | solution.py:55
  33.5 9.6 %all-to-all-done = bf16[32,40,256]{2,1,0:T(8,128)(2,1)S(1)} async-done(((bf16[32,40,256]{2,1,0:T(8,128)(2,1)}), bf16[32,40,256]{2,1,0:T(8,128)(2,1)S(1)}, u32[]{:S(2)}, u32[]{:S(2)}) %all-to-all-start) | async-done | bytes 655392 | tf_op jit(solution)/shard_map/all_to_all | solution.py:35
  43.2 2.8 %collective-permute-start = (bf16[1024,256]{1,0:T(8,128)(2,1)S(1)}, bf16[1024,256]{1,0:T(8,128)(2,1)S(1)}, u32[]{:S(2)}, u32[]{:S(2)}) collective-permute-start(bf16[1024,256]{1,0:T(8,128)(2,1)S(1)} %bitcast.74), channel_id=1, source_target_pairs={{0,6},{2,0},{4,2},{6,4},{1,7},{3,1},{5,3},{7,5},{8,14},{10,8},{12,... | collective-permute-start | bytes 1572872 | tf_op jit(solution)/shard_map/ppermute | solution.py:27
  47.7 16.0 %all_to_all.30 = bf16[32,16,256]{2,1,0:T(8,128)(2,1)S(1)} all-to-all(bf16[32,16,256]{2,1,0:T(8,128)(2,1)S(1)} %bitcast.80), channel_id=1, replica_groups=mesh['y'=4,'z'=8,'x'=4,'core'=2] {'y','z'}, dimensions={0} | all-to-all | bytes 524288 | tf_op jit(solution)/shard_map/all_to_all | solution.py:35
  63.7 2.5 collective-permute-done
  66.1 3.7 %collective-permute-done.2 = bf16[1024,256]{1,0:T(8,128)(2,1)S(1)} collective-permute-done((bf16[1024,256]{1,0:T(8,128)(2,1)S(1)}, bf16[1024,256]{1,0:T(8,128)(2,1)S(1)}, u32[]{:S(2)}, u32[]{:S(2)}) %collective-permute-start.2) | collective-permute-done | bytes 524320 | tf_op jit(solution)/shard_map/ppermute | solution.py:27
  70.5 4.0 %collective-permute-done.3.far_ref = bf16[1024,1024]{1,0:T(8,128)(2,1)} collective-permute-done((bf16[1024,1024]{1,0:T(8,128)(2,1)S(1)}, bf16[1024,1024]{1,0:T(8,128)(2,1)}, u32[]{:S(2)}, u32[]{:S(2)}) %collective-permute-start.3) | collective-permute-done | bytes 2097184 | tf_op jit(solution)/shard_map/ppermute | solution.py:31
  74.5 3.0 %fusion.7 = f32[1024,384]{1,0:T(8,128)S(1)} fusion(bf16[1024,1024]{1,0:T(8,128)(2,1)} %collective-permute-done.3.far_ref, bf16[2048,384]{1,0:T(8,128)(2,1)} %get-tuple-element.54), kind=kOutput, calls=%fused_computation.16 | convolution fusion | flops 805306368 | bytes 4456448 | tf_op jit(solution)/shard_map/dot_general | solution.py:17
  77.5 1.6 multiply_reduce_fusion
  79.1 2.6 %convolution_convert_fusion = bf16[1024,1024]{1,0:T(8,128)(2,1)} fusion(bf16[1024,384]{1,0:T(8,128)(2,1)S(1)} %get-tuple-element.66.grad_ref, bf16[2048,384]{1,0:T(8,128)(2,1)S(1)} %copy-done.11), kind=kOutput, calls=%fused_computation.1 | convolution fusion | flops 806354944 | bytes 3670016 | tf_op jit(solution)/shard_map/dot_general | solution.py:17
  83.8 2.3 collective-permute-done.4.far_ref
  86.1 1.8 near_gradient.1
  89.0 2.1 collective-permute-start.6
  92.5 16.3 %all_to_all.31 = f32[32,8,128]{2,1,0:T(8,128)S(1)} all-to-all(f32[32,8,128]{2,1,0:T(8,128)S(1)} %pad.9), channel_id=1, replica_groups=mesh['y'=4,'z'=8,'x'=4,'core'=2] {'y','z'}, dimensions={0} | all-to-all | bytes 262144 | tf_op jit(solution)/shard_map/all_to_all | solution.py:35
  112.1 12.3 %collective-permute-done.11 = f32[8,128]{1,0:T(8,128)S(1)} collective-permute-done((f32[8,128]{1,0:T(8,128)S(1)}, f32[8,128]{1,0:T(8,128)S(1)}, u32[]{:S(2)}, u32[]{:S(2)}) %collective-permute-start.11) | collective-permute-done | bytes 4128 | tf_op jit(solution)/shard_map/ppermute | solution.py:27
  125.6 4.0 %collective-permute-done.10 = f32[8,128]{1,0:T(8,128)S(1)} collective-permute-done((f32[8,128]{1,0:T(8,128)S(1)}, f32[8,128]{1,0:T(8,128)S(1)}, u32[]{:S(2)}, u32[]{:S(2)}) %collective-permute-start.10) | collective-permute-done | bytes 4128 | tf_op jit(solution)/shard_map/ppermute | solution.py:27
  129.6 9.2 %head_gradient.1 = f32[2048,384]{1,0:T(8,128)} custom-call(s32[8]{0:T(128)} %stack.55.order_ref, bf16[1024,1024]{1,0:T(8,128)(2,1)} %copy-done.7, bf16[1024,1024]{1,0:T(8,128)(2,1)} %collective-permute-done.3.far_ref, bf16[1024,384]{1,0:T(8,128)(2,1)} %copy-done.1), custom_call_target="tpu_custom_call" | custom-call | flops 1024 | bytes 1024 | tf_op jit(solution)/shard_map/head_gradient/pallas_call | solution.py:101
  139.8 7.2 %all-to-all-start.3 = ((bf16[32,32,256]{2,1,0:T(8,128)(2,1)}), bf16[32,32,256]{2,1,0:T(8,128)(2,1)S(1)}, u32[]{:S(2)}, u32[]{:S(2)}) async-start(bf16[32,32,256]{2,1,0:T(8,128)(2,1)} %bitcast.79), calls=%async_computation.3 | async-start | bytes 1048576 | tf_op jit(solution)/shard_map/all_to_all | solution.py:35
  147.1 16.0 %all-to-all-done.3 = bf16[32,32,256]{2,1,0:T(8,128)(2,1)S(1)} async-done(((bf16[32,32,256]{2,1,0:T(8,128)(2,1)}), bf16[32,32,256]{2,1,0:T(8,128)(2,1)S(1)}, u32[]{:S(2)}, u32[]{:S(2)}) %all-to-all-start.3) | async-done | bytes 524320 | tf_op jit(solution)/shard_map/all_to_all | solution.py:35
  165.3 4.9 %all-to-all-start.4 = ((bf16[32,16,256]{2,1,0:T(8,128)(2,1)}), bf16[32,16,256]{2,1,0:T(8,128)(2,1)S(1)}, u32[]{:S(2)}, u32[]{:S(2)}) async-start(bf16[32,16,256]{2,1,0:T(8,128)(2,1)} %bitcast.20), calls=%async_computation.4 | async-start | bytes 524288 | tf_op jit(solution)/shard_map/all_to_all | solution.py:35
  170.2 11.0 %all-to-all-done.4 = bf16[32,16,256]{2,1,0:T(8,128)(2,1)S(1)} async-done(((bf16[32,16,256]{2,1,0:T(8,128)(2,1)}), bf16[32,16,256]{2,1,0:T(8,128)(2,1)S(1)}, u32[]{:S(2)}, u32[]{:S(2)}) %all-to-all-start.4) | async-done | bytes 262176 | tf_op jit(solution)/shard_map/all_to_all | solution.py:35
  183.3 2.3 fusion.45
  186.3 1.9 collective-permute-done.12
  188.3 1.8 collective-permute-done.13
  190.0 2.7 %collective-permute-done.14 = bf16[2,256,256]{2,1,0:T(8,128)(2,1)S(1)} collective-permute-done((bf16[2,256,256]{2,1,0:T(8,128)(2,1)S(1)}, bf16[2,256,256]{2,1,0:T(8,128)(2,1)S(1)}, u32[]{:S(2)}, u32[]{:S(2)}) %collective-permute-start.14) | collective-permute-done | bytes 262176 | tf_op jit(solution)/shard_map/ppermute | solution.py:27
  193.0 2.6 %collective-permute-done.15 = bf16[2,256,1024]{2,1,0:T(8,128)(2,1)S(1)} collective-permute-done((bf16[2,256,1024]{2,1,0:T(8,128)(2,1)S(1)}, bf16[2,256,1024]{2,1,0:T(8,128)(2,1)S(1)}, u32[]{:S(2)}, u32[]{:S(2)}) %collective-permute-start.15) | collective-permute-done | bytes 1048608 | tf_op jit(solution)/shard_map/ppermute | solution.py:31
  197.6 2.5 %collective-permute-done.16 = bf16[2,256,1024]{2,1,0:T(8,128)(2,1)S(1)} collective-permute-done((bf16[2,256,1024]{2,1,0:T(8,128)(2,1)S(1)}, bf16[2,256,1024]{2,1,0:T(8,128)(2,1)S(1)}, u32[]{:S(2)}, u32[]{:S(2)}) %collective-permute-start.16) | collective-permute-done | bytes 1048608 | tf_op jit(solution)/shard_map/ppermute | solution.py:31
  203.4 6.5 %collective-permute-done.19 = bf16[2,256,256]{2,1,0:T(8,128)(2,1)S(1)} collective-permute-done((bf16[2,256,256]{2,1,0:T(8,128)(2,1)S(1)}, bf16[2,256,256]{2,1,0:T(8,128)(2,1)S(1)}, u32[]{:S(2)}, u32[]{:S(2)}) %collective-permute-start.19) | collective-permute-done | bytes 262176 | tf_op jit(solution)/shard_map/ppermute | solution.py:27
  209.9 2.6 %collective-permute-done.18 = bf16[2,256,256]{2,1,0:T(8,128)(2,1)S(1)} collective-permute-done((bf16[2,256,256]{2,1,0:T(8,128)(2,1)S(1)}, bf16[2,256,256]{2,1,0:T(8,128)(2,1)S(1)}, u32[]{:S(2)}, u32[]{:S(2)}) %collective-permute-start.18) | collective-permute-done | bytes 262176 | tf_op jit(solution)/shard_map/ppermute | solution.py:27
  212.5 4.4 %collective-permute-done.17 = bf16[2,256,256]{2,1,0:T(8,128)(2,1)S(1)} collective-permute-done((bf16[2,256,256]{2,1,0:T(8,128)(2,1)S(1)}, bf16[2,256,256]{2,1,0:T(8,128)(2,1)S(1)}, u32[]{:S(2)}, u32[]{:S(2)}) %collective-permute-start.17) | collective-permute-done | bytes 262176 | tf_op jit(solution)/shard_map/ppermute | solution.py:27
  217.1 22.3 %all_to_all.32 = f32[32,16,256]{2,1,0:T(8,128)S(1)} all-to-all(f32[32,16,256]{2,1,0:T(8,128)S(1)} %copy_bitcast_fusion), channel_id=1, replica_groups=mesh['y'=4,'z'=8,'x'=4,'core'=2] {'y','z'}, dimensions={0} | all-to-all | bytes 1048576 | tf_op jit(solution)/shard_map/all_to_all | solution.py:308
  (120 shorter events, 31.2 us)
Async XLA Ops:
  7.2 26.0 %copy-start = (bf16[32,2048]{1,0:T(8,128)(2,1)S(1)}, bf16[32,2048]{1,0:T(8,128)(2,1)}, u32[]{:S(2)}) copy-start(bf16[32,2048]{1,0:T(8,128)(2,1)} %param.13) | copy-start | bytes 393220
  7.2 15.9 %copy-start.14 = (f32[32,8]{0,1:T(8,128)S(1)}, f32[32,8]{0,1:T(8,128)}, u32[]{:S(2)}) copy-start(f32[32,8]{0,1:T(8,128)} %param.19) | copy-start | bytes 3076
  7.2 15.9 %copy-start.15 = (s32[32,8]{0,1:T(8,128)S(1)}, s32[32,8]{0,1:T(8,128)}, u32[]{:S(2)}) copy-start(s32[32,8]{0,1:T(8,128)} %param.20) | copy-start | bytes 3076
  11.5 31.6 %all-to-all-start = ((bf16[32,40,256]{2,1,0:T(8,128)(2,1)}), bf16[32,40,256]{2,1,0:T(8,128)(2,1)S(1)}, u32[]{:S(2)}, u32[]{:S(2)}) async-start(bf16[32,40,256]{2,1,0:T(8,128)(2,1)} %broadcast_in_dim.34), calls=%async_computation | async-start | bytes 1310720 | tf_op jit(solution)/shard_map/all_to_all | solution.py:35
  22.8 147.3 %all-gather.2.cloned.1.call-start = ((), (), s32[]{:S(2)}) async-start(), calls=%async_computation.6 | async-start | bytes 2359296 | tf_op jit(solution)/shard_map/all_gather | solution.py:232
  43.2 23.0 %collective-permute-start = (bf16[1024,256]{1,0:T(8,128)(2,1)S(1)}, bf16[1024,256]{1,0:T(8,128)(2,1)S(1)}, u32[]{:S(2)}, u32[]{:S(2)}) collective-permute-start(bf16[1024,256]{1,0:T(8,128)(2,1)S(1)} %bitcast.74), channel_id=1, source_target_pairs={{0,6},{2,0},{4,2},{6,4},{1,7},{3,1},{5,3},{7,5},{8,14},{10,8},{12,... | collective-permute-start | bytes 1572872 | tf_op jit(solution)/shard_map/ppermute | solution.py:27
  46.0 20.1 %collective-permute-start.1 = (bf16[1024,256]{1,0:T(8,128)(2,1)S(1)}, bf16[1024,256]{1,0:T(8,128)(2,1)S(1)}, u32[]{:S(2)}, u32[]{:S(2)}) collective-permute-start(bf16[1024,256]{1,0:T(8,128)(2,1)S(1)} %bitcast.75), channel_id=1, source_target_pairs={{0,4},{2,6},{4,0},{6,2},{1,5},{3,7},{5,1},{7,3},{8,12},{10,14},{12... | collective-permute-start | bytes 1572872 | tf_op jit(solution)/shard_map/ppermute | solution.py:27
  46.8 23.0 %collective-permute-start.2 = (bf16[1024,256]{1,0:T(8,128)(2,1)S(1)}, bf16[1024,256]{1,0:T(8,128)(2,1)S(1)}, u32[]{:S(2)}, u32[]{:S(2)}) collective-permute-start(bf16[1024,256]{1,0:T(8,128)(2,1)S(1)} %bitcast.76), channel_id=1, source_target_pairs={{0,2},{2,4},{4,6},{6,0},{1,3},{3,5},{5,7},{7,1},{8,10},{10,12},{12... | collective-permute-start | bytes 1572872 | tf_op jit(solution)/shard_map/ppermute | solution.py:27
  70.1 4.4 %collective-permute-start.3 = (bf16[1024,1024]{1,0:T(8,128)(2,1)S(1)}, bf16[1024,1024]{1,0:T(8,128)(2,1)}, u32[]{:S(2)}, u32[]{:S(2)}) collective-permute-start(bf16[1024,1024]{1,0:T(8,128)(2,1)S(1)} %constant_dynamic-update-slice_fusion.near_ref), channel_id=1, source_target_pairs={{0,1},{1,0},{2,3},{3,2},{4,5},{5,4},{6,7},{7,6},{8,9},{9,8},{10,11... | collective-permute-start | bytes 6291464 | tf_op jit(solution)/shard_map/ppermute | solution.py:31
  81.7 4.4 %collective-permute-start.4 = (bf16[1024,1024]{1,0:T(8,128)(2,1)}, bf16[1024,1024]{1,0:T(8,128)(2,1)S(1)}, u32[]{:S(2)}, u32[]{:S(2)}) collective-permute-start(bf16[1024,1024]{1,0:T(8,128)(2,1)} %convolution_convert_fusion), channel_id=1, source_target_pairs={{0,1},{1,0},{2,3},{3,2},{4,5},{5,4},{6,7},{7,6},{8,9},{9,8},{10,11... | collective-permute-start | bytes 6291464 | tf_op jit(solution)/shard_map/ppermute | solution.py:31
  89.0 49.8 %collective-permute-start.5 = (bf16[1024,256]{1,0:T(8,128)(2,1)}, bf16[1024,256]{1,0:T(8,128)(2,1)S(1)}, u32[]{:S(2)}, u32[]{:S(2)}) collective-permute-start(bf16[1024,256]{1,0:T(8,128)(2,1)} %get-tuple-element.61), channel_id=1, source_target_pairs={{0,2},{2,4},{4,6},{6,0},{1,3},{3,5},{5,7},{7,1},{8,10},{10,12},{12... | collective-permute-start | bytes 1572872 | tf_op jit(solution)/shard_map/ppermute | solution.py:27
  89.0 49.8 %collective-permute-start.6 = (bf16[1024,256]{1,0:T(8,128)(2,1)}, bf16[1024,256]{1,0:T(8,128)(2,1)S(1)}, u32[]{:S(2)}, u32[]{:S(2)}) collective-permute-start(bf16[1024,256]{1,0:T(8,128)(2,1)} %get-tuple-element.62), channel_id=1, source_target_pairs={{0,4},{2,6},{4,0},{6,2},{1,5},{3,7},{5,1},{7,3},{8,12},{10,14},{12... | collective-permute-start | bytes 1572872 | tf_op jit(solution)/shard_map/ppermute | solution.py:27
  91.0 47.7 %collective-permute-start.7 = (bf16[1024,256]{1,0:T(8,128)(2,1)S(1)}, bf16[1024,256]{1,0:T(8,128)(2,1)S(1)}, u32[]{:S(2)}, u32[]{:S(2)}) collective-permute-start(bf16[1024,256]{1,0:T(8,128)(2,1)S(1)} %get-tuple-element.63), channel_id=1, source_target_pairs={{0,6},{2,0},{4,2},{6,4},{1,7},{3,1},{5,3},{7,5},{8,14},{10,8},{12,... | collective-permute-start | bytes 1572872 | tf_op jit(solution)/shard_map/ppermute | solution.py:27
  108.9 1.2 collective-permute-start.8
  110.1 14.4 %collective-permute-start.11 = (f32[8,128]{1,0:T(8,128)S(1)}, f32[8,128]{1,0:T(8,128)S(1)}, u32[]{:S(2)}, u32[]{:S(2)}) collective-permute-start(f32[8,128]{1,0:T(8,128)S(1)} %add.273), channel_id=1, source_target_pairs={{0,6},{2,0},{4,2},{6,4},{1,7},{3,1},{5,3},{7,5},{8,14},{10,8},{12,... | collective-permute-start | bytes 12296 | tf_op jit(solution)/shard_map/ppermute | solution.py:27
  110.8 14.8 %collective-permute-start.9 = (f32[8,128]{1,0:T(8,128)S(1)}, f32[8,128]{1,0:T(8,128)S(1)}, u32[]{:S(2)}, u32[]{:S(2)}) collective-permute-start(f32[8,128]{1,0:T(8,128)S(1)} %add.273), channel_id=1, source_target_pairs={{0,2},{2,4},{4,6},{6,0},{1,3},{3,5},{5,7},{7,1},{8,10},{10,12},{12... | collective-permute-start | bytes 12296 | tf_op jit(solution)/shard_map/ppermute | solution.py:27
  124.5 5.1 %collective-permute-start.10 = (f32[8,128]{1,0:T(8,128)S(1)}, f32[8,128]{1,0:T(8,128)S(1)}, u32[]{:S(2)}, u32[]{:S(2)}) collective-permute-start(f32[8,128]{1,0:T(8,128)S(1)} %add.273), channel_id=1, source_target_pairs={{0,4},{2,6},{4,0},{6,2},{1,5},{3,7},{5,1},{7,3},{8,12},{10,14},{12... | collective-permute-start | bytes 12296 | tf_op jit(solution)/shard_map/ppermute | solution.py:27
  138.8 25.2 %copy-start.8 = (f32[512,32]{1,0:T(8,128)S(1)}, f32[512,32]{1,0:T(8,128)}, u32[]{:S(2)}) copy-start(f32[512,32]{1,0:T(8,128)} %fusion.15) | copy-start | bytes 196612
  139.8 43.5 %copy-start.5 = (bf16[2,2048,128]{2,1,0:T(8,128)(2,1)S(1)}, bf16[2,2048,128]{2,1,0:T(8,128)(2,1)}, u32[]{:S(2)}) copy-start(bf16[2,2048,128]{2,1,0:T(8,128)(2,1)} %gate_ref.1) | copy-start | bytes 3145732
  139.8 23.3 %all-to-all-start.3 = ((bf16[32,32,256]{2,1,0:T(8,128)(2,1)}), bf16[32,32,256]{2,1,0:T(8,128)(2,1)S(1)}, u32[]{:S(2)}, u32[]{:S(2)}) async-start(bf16[32,32,256]{2,1,0:T(8,128)(2,1)} %bitcast.79), calls=%async_computation.3 | async-start | bytes 1048576 | tf_op jit(solution)/shard_map/all_to_all | solution.py:35
  165.3 15.9 %all-to-all-start.4 = ((bf16[32,16,256]{2,1,0:T(8,128)(2,1)}), bf16[32,16,256]{2,1,0:T(8,128)(2,1)S(1)}, u32[]{:S(2)}, u32[]{:S(2)}) async-start(bf16[32,16,256]{2,1,0:T(8,128)(2,1)} %bitcast.20), calls=%async_computation.4 | async-start | bytes 524288 | tf_op jit(solution)/shard_map/all_to_all | solution.py:35
  170.2 15.4 %copy-start.4 = (bf16[2,256,2048]{2,1,0:T(8,128)(2,1)S(1)}, bf16[2,256,2048]{2,1,0:T(8,128)(2,1)}, u32[]{:S(2)}) copy-start(bf16[2,256,2048]{2,1,0:T(8,128)(2,1)} %all-gather.2.cloned.1.call-done) | copy-start | bytes 6291460
  181.2 7.1 %collective-permute-start.12 = (bf16[2,256,256]{2,1,0:T(8,128)(2,1)S(1)}, bf16[2,256,256]{2,1,0:T(8,128)(2,1)S(1)}, u32[]{:S(2)}, u32[]{:S(2)}) collective-permute-start(bf16[2,256,256]{2,1,0:T(8,128)(2,1)S(1)} %copy_bitcast_fusion.1), channel_id=1, source_target_pairs={{0,6},{2,0},{4,2},{6,4},{1,7},{3,1},{5,3},{7,5},{8,14},{10,8},{12,... | collective-permute-start | bytes 786440 | tf_op jit(solution)/shard_map/ppermute | solution.py:27
  182.0 8.1 %collective-permute-start.13 = (bf16[2,256,256]{2,1,0:T(8,128)(2,1)S(1)}, bf16[2,256,256]{2,1,0:T(8,128)(2,1)S(1)}, u32[]{:S(2)}, u32[]{:S(2)}) collective-permute-start(bf16[2,256,256]{2,1,0:T(8,128)(2,1)S(1)} %copy_bitcast_fusion.1), channel_id=1, source_target_pairs={{0,4},{2,6},{4,0},{6,2},{1,5},{3,7},{5,1},{7,3},{8,12},{10,14},{12... | collective-permute-start | bytes 786440 | tf_op jit(solution)/shard_map/ppermute | solution.py:27
  182.9 9.9 %collective-permute-start.14 = (bf16[2,256,256]{2,1,0:T(8,128)(2,1)S(1)}, bf16[2,256,256]{2,1,0:T(8,128)(2,1)S(1)}, u32[]{:S(2)}, u32[]{:S(2)}) collective-permute-start(bf16[2,256,256]{2,1,0:T(8,128)(2,1)S(1)} %copy_bitcast_fusion.1), channel_id=1, source_target_pairs={{0,2},{2,4},{4,6},{6,0},{1,3},{3,5},{5,7},{7,1},{8,10},{10,12},{12... | collective-permute-start | bytes 786440 | tf_op jit(solution)/shard_map/ppermute | solution.py:27
  185.6 10.0 %copy-start.12 = (bf16[2,128,2048]{2,1,0:T(8,128)(2,1)S(1)}, bf16[2,128,2048]{2,1,0:T(8,128)(2,1)}, u32[]{:S(2)}) copy-start(bf16[2,128,2048]{2,1,0:T(8,128)(2,1)} %get-tuple-element.83) | copy-start | bytes 3145732
  192.9 2.7 %collective-permute-start.15 = (bf16[2,256,1024]{2,1,0:T(8,128)(2,1)S(1)}, bf16[2,256,1024]{2,1,0:T(8,128)(2,1)S(1)}, u32[]{:S(2)}, u32[]{:S(2)}) collective-permute-start(bf16[2,256,1024]{2,1,0:T(8,128)(2,1)S(1)} %constant_dynamic-update-slice_fusion.4), channel_id=1, source_target_pairs={{0,1},{1,0},{2,3},{3,2},{4,5},{5,4},{6,7},{7,6},{8,9},{9,8},{10,11... | collective-permute-start | bytes 3145736 | tf_op jit(solution)/shard_map/ppermute | solution.py:31
  197.1 3.0 %collective-permute-start.16 = (bf16[2,256,1024]{2,1,0:T(8,128)(2,1)S(1)}, bf16[2,256,1024]{2,1,0:T(8,128)(2,1)S(1)}, u32[]{:S(2)}, u32[]{:S(2)}) collective-permute-start(bf16[2,256,1024]{2,1,0:T(8,128)(2,1)S(1)} %convolution_convert_fusion.1), channel_id=1, source_target_pairs={{0,1},{1,0},{2,3},{3,2},{4,5},{5,4},{6,7},{7,6},{8,9},{9,8},{10,11... | collective-permute-start | bytes 3145736 | tf_op jit(solution)/shard_map/ppermute | solution.py:31
  200.6 38.8 %copy-start.9 = (f32[512,32]{1,0:T(8,128)S(1)}, f32[512,32]{1,0:T(8,128)}, u32[]{:S(2)}) copy-start(f32[512,32]{1,0:T(8,128)} %fusion.15) | copy-start | bytes 196612
  200.7 9.2 %collective-permute-start.19 = (bf16[2,256,256]{2,1,0:T(8,128)(2,1)S(1)}, bf16[2,256,256]{2,1,0:T(8,128)(2,1)S(1)}, u32[]{:S(2)}, u32[]{:S(2)}) collective-permute-start(bf16[2,256,256]{2,1,0:T(8,128)(2,1)S(1)} %get-tuple-element.92), channel_id=1, source_target_pairs={{0,6},{2,0},{4,2},{6,4},{1,7},{3,1},{5,3},{7,5},{8,14},{10,8},{12,... | collective-permute-start | bytes 786440 | tf_op jit(solution)/shard_map/ppermute | solution.py:27
  201.8 10.7 %collective-permute-start.18 = (bf16[2,256,256]{2,1,0:T(8,128)(2,1)S(1)}, bf16[2,256,256]{2,1,0:T(8,128)(2,1)S(1)}, u32[]{:S(2)}, u32[]{:S(2)}) collective-permute-start(bf16[2,256,256]{2,1,0:T(8,128)(2,1)S(1)} %get-tuple-element.93), channel_id=1, source_target_pairs={{0,4},{2,6},{4,0},{6,2},{1,5},{3,7},{5,1},{7,3},{8,12},{10,14},{12... | collective-permute-start | bytes 786440 | tf_op jit(solution)/shard_map/ppermute | solution.py:27
  202.6 14.4 %collective-permute-start.17 = (bf16[2,256,256]{2,1,0:T(8,128)(2,1)S(1)}, bf16[2,256,256]{2,1,0:T(8,128)(2,1)S(1)}, u32[]{:S(2)}, u32[]{:S(2)}) collective-permute-start(bf16[2,256,256]{2,1,0:T(8,128)(2,1)S(1)} %get-tuple-element.91), channel_id=1, source_target_pairs={{0,2},{2,4},{4,6},{6,0},{1,3},{3,5},{5,7},{7,1},{8,10},{10,12},{12... | collective-permute-start | bytes 786440 | tf_op jit(solution)/shard_map/ppermute | solution.py:27
  (9 other events, 52.8 us)
Sparse Core Ops, SparseCore 0:
  82.7 43.1 all-gather.1

commit v2 on v1

--- a/solution.py
+++ b/solution.py
@@ -45,8 +45,19 @@
     count = order.shape[0]
     share = width // count
 
-    def body(order_ref, head_ref, gate_ref, up_ref, down_ref, head_out, pair_out, down_out):
-        head_out[...] = head_ref[...]
+    lead = count // 2
+
+    def body(
+        order_ref, head_ref, gate_ref, up_ref, down_ref, near_out, far_out, pair_out, down_out
+    ):
+        @pl.when(pl.program_id(0) < lead)
+        def _():
+            near_out[...] = head_ref[...]
+
+        @pl.when(pl.program_id(0) >= lead)
+        def _():
+            far_out[...] = head_ref[...]
+
         pair_out[:, :, :hidden] = gate_ref[...]
         pair_out[:, :, hidden:] = up_ref[...]
         down_out[...] = down_ref[...]
@@ -64,13 +75,15 @@
                 pl.BlockSpec((own, hidden, share), lambda i, s: (0, 0, s[i])),
             ],
             out_specs=[
-                pl.BlockSpec((share, tile), lambda i, s: (i, 0)),
+                pl.BlockSpec((share, tile), lambda i, s: (jnp.minimum(i, lead - 1), 0)),
+                pl.BlockSpec((share, tile), lambda i, s: (jnp.maximum(i - lead, 0), 0)),
                 pl.BlockSpec((own, share, 2 * hidden), lambda i, s: (0, i, 0)),
                 pl.BlockSpec((own, hidden, share), lambda i, s: (0, 0, i)),
             ],
         ),
         out_shape=[
-            jax.ShapeDtypeStruct((width, tile), bf16),
+            jax.ShapeDtypeStruct((width // 2, tile), bf16),
+            jax.ShapeDtypeStruct((width // 2, tile), bf16),
             jax.ShapeDtypeStruct((own, width, 2 * hidden), bf16),
             jax.ShapeDtypeStruct((own, hidden, width), bf16),
         ],
@@ -178,7 +191,7 @@
     order = jnp.stack(
         [((x_at + k) % XN) * CN + (c_at + c) % CN for c in range(CN) for k in range(XN)]
     )
-    head_turned, pair_turned, down_turned = turned_weights(
+    head_near, head_far, pair_turned, down_turned = turned_weights(
         order, head_weight, w_gate, w_up, w_down
     )
 
@@ -217,9 +230,9 @@
         jnp.concatenate([normed_share, digits], axis=0)[None], (n_expert, rows + 8, share)
     )
     spread = exchanged(spread, ("y", "z"))
-    spread, head_turned, pair_turned, down_turned, inputs, pick, slot_gate = (
+    spread, head_near, head_far, pair_turned, down_turned, inputs, pick, slot_gate = (
         lax.optimization_barrier(
-            (spread, head_turned, pair_turned, down_turned, inputs, pick, slot_gate)
+            (spread, head_near, head_far, pair_turned, down_turned, inputs, pick, slot_gate)
         )
     )
     numbers = spread[:, rows:]
@@ -244,24 +257,25 @@
         keepdims=True,
     )
     columns = (e_at * n_vocab + v_at) * tile + jnp.arange(tile, dtype=jnp.int32)
-    scores = wide_dot(normed_near, head_turned[:side], ((1,), (0,))) + wide_dot(
-        normed_far, head_turned[side:], ((1,), (0,))
-    )
+    scores = wide_dot(normed_near, head_near, ((1,), (0,)))
+    scores, normed_far = lax.optimization_barrier((scores, normed_far))
+    scores = scores + wide_dot(normed_far, head_far, ((1,), (0,)))
     target_hit = (clean_all == columns[None, :]).astype(f32)
     loss_scale = 1.0 / math.sqrt(all_rows)
     score_grad = ((jnp.exp(scores) - ratio_rows * target_hit) * loss_scale).astype(bf16)
     along = jnp.sum(score_grad.astype(f32) * scores, axis=1)
     score_grad, along = lax.optimization_barrier((score_grad, along))
-    far = wide_dot(score_grad, head_turned[side:], ((1,), (1,))).astype(bf16)
+    far = wide_dot(score_grad, head_far, ((1,), (1,))).astype(bf16)
     far = across_core(far)
-    kept, *sent = near_gradient(score_grad, head_turned[:side], far)
+    along = along.reshape(8, all_rows // 8)
+    along = along + across_core(along)
+    along = along + sum(along_x(along, k) for k in range(1, XN))
+    along, far = lax.optimization_barrier((along, far))
+    kept, *sent = near_gradient(score_grad, head_near, far)
     kept, sent, score_grad, along = lax.optimization_barrier((kept, sent, score_grad, along))
     sent = [along_x(a, k + 1) for k, a in enumerate(sent)]
     along = jnp.pad(along.reshape(n_expert, 1, rows), ((0, 0), (0, 7), (0, 128 - rows)))
     along = jnp.sum(exchanged(along, ("y", "z")), axis=0)
-    along = along + across_core(along)
-    along = along + sum(along_x(along, k) for k in range(1, XN))
-    along, score_grad = lax.optimization_barrier((along, score_grad))
     head_grad = head_gradient(order, normed_near, normed_far, score_grad)
     sent, head_grad, along = lax.optimization_barrier((sent, head_grad, along))
     kept = (kept + sum(a.astype(f32) for a in sent)).astype(bf16)

time: 248 us -> 242 us (0.976)
  blocking collectives: 54.5 us -> 38.6 us
  starting transfers between devices: 40.3 us -> 51.5 us
  waiting for transfers between devices: 91.6 us -> 87.6 us
    all_to_all x2 -> x1, blocking collectives: 32.3 us -> 16 us  [exchanged(): return lax.all_to_all(a, axes, 0, 0, tiled=True)]
    all_to_all x3 -> x4, starting transfers between devices: 23.5 us -> 31.6 us  [exchanged(): return lax.all_to_all(a, axes, 0, 0, tiled=True)]
    ppermute x15, waiting for transfers between devices: 42.4 us -> 38.8 us  [along_x(): return lax.ppermute(a, 'x', [(p, (p + step) % XN) for p in range(XN)])]
    ppermute x5, waiting for transfers between devices: 12.5 us -> 9.75 us  [across_core(): return lax.ppermute(a, 'core', [(p, CN - 1 - p) for p in range(CN)])]
    ppermute x15, starting transfers between devices: 15.9 us -> 18.6 us  [along_x(): return lax.ppermute(a, 'x', [(p, (p + step) % XN) for p in range(XN)])]
    all_to_all x3 -> x4, waiting for transfers between devices: 36.6 us -> 39.1 us  [exchanged(): return lax.all_to_all(a, axes, 0, 0, tiled=True)]
  transfers between devices with their start and end apart: 24 -> 25, of which waited for: 18 -> 20; matrix products, arithmetic and copies ran while one was open for 5% -> 5% of each run, Pallas kernels for 8% -> 8%
where the time goes in v2:
time: 242 us; the launch traced here: 241 us
  waiting for transfers between devices  87.6 us (36%)
  starting transfers between devices  51.5 us (21%)
  blocking collectives  38.6 us (16%)
  Pallas kernels  19 us (8%)
  between operations  14.6 us (6%)
  matrix products  14.4 us (6%)
  other arithmetic  7.79 us (3%)
  local copies, waits for them, and re-layouts  7.08 us (3%)
    all_to_all x4, waiting for transfers between devices, exchanged(): return lax.all_to_all(a, axes, 0, 0, tiled=True)  39.1 us
    ppermute x15, waiting for transfers between devices, along_x(): return lax.ppermute(a, 'x', [(p, (p + step) % XN) for p in range(XN)])  38.8 us
    all_to_all x4, starting transfers between devices, exchanged(): return lax.all_to_all(a, axes, 0, 0, tiled=True)  31.6 us
    all_to_all x1, blocking collectives, on_device(): returned = lax.all_to_all(near, ('y', 'z'), 0, 0, tiled=True)  22.6 us
    ppermute x15, starting transfers between devices, along_x(): return lax.ppermute(a, 'x', [(p, (p + step) % XN) for p in range(XN)])  18.6 us
    all_to_all x1, blocking collectives, exchanged(): return lax.all_to_all(a, axes, 0, 0, tiled=True)  16 us
    ppermute x5, waiting for transfers between devices, across_core(): return lax.ppermute(a, 'core', [(p, CN - 1 - p) for p in range(CN)])  9.75 us
    dot_general x7, matrix products, wide_dot(): lax.dot_general(a, b, (dims, ((), ())), preferred_element_type=f32, preci...  9.61 us
  transfers between devices with their start and end apart: 25, of which 20 were waited for; matrix products, arithmetic and copies ran while one was open for 5% of the time, Pallas kernels for 8%

profile of v2, /device:TPU:32, one launch (start us, length us, event | category | flops | bytes accessed | tf_op | source)
XLA Modules:
  0.0 240.7 jit_solution(5359003850346440391)
XLA Ops:
  11.5 11.4 %all-to-all-start = ((bf16[32,40,256]{2,1,0:T(8,128)(2,1)}), bf16[32,40,256]{2,1,0:T(8,128)(2,1)S(1)}, u32[]{:S(2)}, u32[]{:S(2)}) async-start(bf16[32,40,256]{2,1,0:T(8,128)(2,1)} %broadcast_in_dim.34), calls=%async_computation | async-start | bytes 1310720 | tf_op jit(solution)/shard_map/all_to_all | solution.py:35
  24.6 7.8 %turned_weights.1 = (bf16[1024,384]{1,0:T(8,128)(2,1)}, bf16[1024,384]{1,0:T(8,128)(2,1)}, bf16[2,2048,256]{2,1,0:T(8,128)(2,1)}, bf16[2,128,2048]{2,1,0:T(8,128)(2,1)}) custom-call(s32[8]{0:T(128)} %stack.55.order_ref, bf16[2048,384]{1,0:T(8,128)(2,1)} %head_ref.1, bf16[2,2048,128]{2,1,0:T(8,128)(2,1)} %gate_ref.1, bf16[2,2048,128]{2,1,0:T(8,128)(2,1)} %up_ref.1, ...), custom_call_target="tpu_custom_call" | custom-call | bytes 9437184 | tf_op jit(solution)/shard_map/turned_weights/pallas_call | solution.py:66
  33.5 9.6 %all-to-all-done = bf16[32,40,256]{2,1,0:T(8,128)(2,1)S(1)} async-done(((bf16[32,40,256]{2,1,0:T(8,128)(2,1)}), bf16[32,40,256]{2,1,0:T(8,128)(2,1)S(1)}, u32[]{:S(2)}, u32[]{:S(2)}) %all-to-all-start) | async-done | bytes 655392 | tf_op jit(solution)/shard_map/all_to_all | solution.py:35
  43.2 2.8 %collective-permute-start = (bf16[1024,256]{1,0:T(8,128)(2,1)S(1)}, bf16[1024,256]{1,0:T(8,128)(2,1)S(1)}, u32[]{:S(2)}, u32[]{:S(2)}) collective-permute-start(bf16[1024,256]{1,0:T(8,128)(2,1)S(1)} %bitcast.81), channel_id=1, source_target_pairs={{0,6},{2,0},{4,2},{6,4},{1,7},{3,1},{5,3},{7,5},{8,14},{10,8},{12,... | collective-permute-start | bytes 1572872 | tf_op jit(solution)/shard_map/ppermute | solution.py:27
  47.7 16.0 %all_to_all.30 = bf16[32,16,256]{2,1,0:T(8,128)(2,1)S(1)} all-to-all(bf16[32,16,256]{2,1,0:T(8,128)(2,1)S(1)} %bitcast.86), channel_id=1, replica_groups=mesh['y'=4,'z'=8,'x'=4,'core'=2] {'y','z'}, dimensions={0} | all-to-all | bytes 524288 | tf_op jit(solution)/shard_map/all_to_all | solution.py:35
  63.7 2.5 %collective-permute-done = bf16[1024,256]{1,0:T(8,128)(2,1)S(1)} collective-permute-done((bf16[1024,256]{1,0:T(8,128)(2,1)S(1)}, bf16[1024,256]{1,0:T(8,128)(2,1)S(1)}, u32[]{:S(2)}, u32[]{:S(2)}) %collective-permute-start) | collective-permute-done | bytes 524320 | tf_op jit(solution)/shard_map/ppermute | solution.py:27
  66.1 3.7 %collective-permute-done.2 = bf16[1024,256]{1,0:T(8,128)(2,1)S(1)} collective-permute-done((bf16[1024,256]{1,0:T(8,128)(2,1)S(1)}, bf16[1024,256]{1,0:T(8,128)(2,1)S(1)}, u32[]{:S(2)}, u32[]{:S(2)}) %collective-permute-start.2) | collective-permute-done | bytes 524320 | tf_op jit(solution)/shard_map/ppermute | solution.py:27
  72.7 1.8 collective-permute-done.3.far_ref
  74.5 2.8 %fusion.42 = f32[1024,384]{1,0:T(8,128)S(1)} fusion(bf16[1024,1024]{1,0:T(8,128)(2,1)} %collective-permute-done.3.far_ref, bf16[1024,384]{1,0:T(8,128)(2,1)S(1)} %copy-done.19), kind=kOutput, calls=%fused_computation.110 | convolution fusion | flops 805306368 | bytes 4456448 | tf_op jit(solution)/shard_map/dot_general | solution.py:17
  78.0 2.6 %convolution_convert_fusion = bf16[1024,1024]{1,0:T(8,128)(2,1)} fusion(bf16[1024,384]{1,0:T(8,128)(2,1)S(1)} %get-tuple-element.74.grad_ref, bf16[1024,384]{1,0:T(8,128)(2,1)S(1)} %copy-done.19), kind=kOutput, calls=%fused_computation.1 | convolution fusion | flops 806354944 | bytes 3670016 | tf_op jit(solution)/shard_map/dot_general | solution.py:17
  82.0 2.8 %collective-permute-done.4 = f32[8,128]{1,0:T(8,128)S(1)} collective-permute-done((f32[8,128]{1,0:T(8,128)S(1)}, f32[8,128]{1,0:T(8,128)S(1)}, u32[]{:S(2)}, u32[]{:S(2)}) %collective-permute-start.4) | collective-permute-done | bytes 4128 | tf_op jit(solution)/shard_map/ppermute | solution.py:31
  84.8 2.1 collective-permute-start.6
  91.7 2.1 near_gradient.1
  94.8 1.8 collective-permute-start.10
  96.6 2.9 %collective-permute-start.11 = (bf16[1024,256]{1,0:T(8,128)(2,1)}, bf16[1024,256]{1,0:T(8,128)(2,1)S(1)}, u32[]{:S(2)}, u32[]{:S(2)}) collective-permute-start(bf16[1024,256]{1,0:T(8,128)(2,1)} %get-tuple-element.73), channel_id=1, source_target_pairs={{0,6},{2,0},{4,2},{6,4},{1,7},{3,1},{5,3},{7,5},{8,14},{10,8},{12,... | collective-permute-start | bytes 1572872 | tf_op jit(solution)/shard_map/ppermute | solution.py:27
  100.2 6.9 %all-to-all-start.2 = ((f32[32,8,128]{2,1,0:T(8,128)}), f32[32,8,128]{2,1,0:T(8,128)S(1)}, u32[]{:S(2)}, u32[]{:S(2)}) async-start(f32[32,8,128]{2,1,0:T(8,128)} %pad.9), calls=%async_computation.2 | async-start | bytes 262144 | tf_op jit(solution)/shard_map/all_to_all | solution.py:35
  107.1 9.2 %head_gradient.1 = f32[2048,384]{1,0:T(8,128)} custom-call(s32[8]{0:T(128)} %stack.55.order_ref, bf16[1024,1024]{1,0:T(8,128)(2,1)} %copy-done.9, bf16[1024,1024]{1,0:T(8,128)(2,1)} %collective-permute-done.3.far_ref, bf16[1024,384]{1,0:T(8,128)(2,1)} %copy-done.1), custom_call_target="tpu_custom_call" | custom-call | flops 1024 | bytes 1024 | tf_op jit(solution)/shard_map/head_gradient/pallas_call | solution.py:114
  116.8 9.1 %collective-permute-done.11 = bf16[1024,256]{1,0:T(8,128)(2,1)S(1)} collective-permute-done((bf16[1024,256]{1,0:T(8,128)(2,1)}, bf16[1024,256]{1,0:T(8,128)(2,1)S(1)}, u32[]{:S(2)}, u32[]{:S(2)}) %collective-permute-start.11) | collective-permute-done | bytes 524320 | tf_op jit(solution)/shard_map/ppermute | solution.py:27
  127.2 8.6 %all-to-all-start.3 = ((bf16[32,32,256]{2,1,0:T(8,128)(2,1)}), bf16[32,32,256]{2,1,0:T(8,128)(2,1)S(1)}, u32[]{:S(2)}, u32[]{:S(2)}) async-start(bf16[32,32,256]{2,1,0:T(8,128)(2,1)} %bitcast.18), calls=%async_computation.3 | async-start | bytes 1048576 | tf_op jit(solution)/shard_map/all_to_all | solution.py:35
  135.8 17.3 %all-to-all-done.3 = bf16[32,32,256]{2,1,0:T(8,128)(2,1)S(1)} async-done(((bf16[32,32,256]{2,1,0:T(8,128)(2,1)}), bf16[32,32,256]{2,1,0:T(8,128)(2,1)S(1)}, u32[]{:S(2)}, u32[]{:S(2)}) %all-to-all-start.3) | async-done | bytes 524320 | tf_op jit(solution)/shard_map/all_to_all | solution.py:35
  155.3 4.8 %all-to-all-start.4 = ((bf16[32,16,256]{2,1,0:T(8,128)(2,1)}), bf16[32,16,256]{2,1,0:T(8,128)(2,1)S(1)}, u32[]{:S(2)}, u32[]{:S(2)}) async-start(bf16[32,16,256]{2,1,0:T(8,128)(2,1)} %bitcast.21), calls=%async_computation.4 | async-start | bytes 524288 | tf_op jit(solution)/shard_map/all_to_all | solution.py:35
  160.2 11.8 %all-to-all-done.4 = bf16[32,16,256]{2,1,0:T(8,128)(2,1)S(1)} async-done(((bf16[32,16,256]{2,1,0:T(8,128)(2,1)}), bf16[32,16,256]{2,1,0:T(8,128)(2,1)S(1)}, u32[]{:S(2)}, u32[]{:S(2)}) %all-to-all-start.4) | async-done | bytes 262176 | tf_op jit(solution)/shard_map/all_to_all | solution.py:35
  172.0 1.7 collective-permute-start.12
  174.6 2.3 fusion.43
  177.7 3.1 %collective-permute-done.12 = bf16[2,256,256]{2,1,0:T(8,128)(2,1)S(1)} collective-permute-done((bf16[2,256,256]{2,1,0:T(8,128)(2,1)S(1)}, bf16[2,256,256]{2,1,0:T(8,128)(2,1)S(1)}, u32[]{:S(2)}, u32[]{:S(2)}) %collective-permute-start.12) | collective-permute-done | bytes 262176 | tf_op jit(solution)/shard_map/ppermute | solution.py:27
  180.7 2.8 %collective-permute-done.13 = bf16[2,256,256]{2,1,0:T(8,128)(2,1)S(1)} collective-permute-done((bf16[2,256,256]{2,1,0:T(8,128)(2,1)S(1)}, bf16[2,256,256]{2,1,0:T(8,128)(2,1)S(1)}, u32[]{:S(2)}, u32[]{:S(2)}) %collective-permute-start.13) | collective-permute-done | bytes 262176 | tf_op jit(solution)/shard_map/ppermute | solution.py:27
  183.5 2.6 %collective-permute-done.14 = bf16[2,256,256]{2,1,0:T(8,128)(2,1)S(1)} collective-permute-done((bf16[2,256,256]{2,1,0:T(8,128)(2,1)S(1)}, bf16[2,256,256]{2,1,0:T(8,128)(2,1)S(1)}, u32[]{:S(2)}, u32[]{:S(2)}) %collective-permute-start.14) | collective-permute-done | bytes 262176 | tf_op jit(solution)/shard_map/ppermute | solution.py:27
  186.3 2.6 %collective-permute-done.15 = bf16[2,256,1024]{2,1,0:T(8,128)(2,1)S(1)} collective-permute-done((bf16[2,256,1024]{2,1,0:T(8,128)(2,1)S(1)}, bf16[2,256,1024]{2,1,0:T(8,128)(2,1)S(1)}, u32[]{:S(2)}, u32[]{:S(2)}) %collective-permute-start.15) | collective-permute-done | bytes 1048608 | tf_op jit(solution)/shard_map/ppermute | solution.py:31
  190.9 2.5 %collective-permute-done.16 = bf16[2,256,1024]{2,1,0:T(8,128)(2,1)S(1)} collective-permute-done((bf16[2,256,1024]{2,1,0:T(8,128)(2,1)S(1)}, bf16[2,256,1024]{2,1,0:T(8,128)(2,1)S(1)}, u32[]{:S(2)}, u32[]{:S(2)}) %collective-permute-start.16) | collective-permute-done | bytes 1048608 | tf_op jit(solution)/shard_map/ppermute | solution.py:31
  194.1 2.2 collective-permute-start.18
  197.3 11.9 %collective-permute-done.17 = bf16[2,256,256]{2,1,0:T(8,128)(2,1)S(1)} collective-permute-done((bf16[2,256,256]{2,1,0:T(8,128)(2,1)S(1)}, bf16[2,256,256]{2,1,0:T(8,128)(2,1)S(1)}, u32[]{:S(2)}, u32[]{:S(2)}) %collective-permute-start.17) | collective-permute-done | bytes 262176 | tf_op jit(solution)/shard_map/ppermute | solution.py:27
  210.0 22.6 %all_to_all.31 = f32[32,16,256]{2,1,0:T(8,128)S(1)} all-to-all(f32[32,16,256]{2,1,0:T(8,128)S(1)} %copy_bitcast_fusion), channel_id=1, replica_groups=mesh['y'=4,'z'=8,'x'=4,'core'=2] {'y','z'}, dimensions={0} | all-to-all | bytes 1048576 | tf_op jit(solution)/shard_map/all_to_all | solution.py:322
  (127 shorter events, 31.7 us)
Async XLA Ops:
  7.2 26.1 %copy-start = (bf16[32,2048]{1,0:T(8,128)(2,1)S(1)}, bf16[32,2048]{1,0:T(8,128)(2,1)}, u32[]{:S(2)}) copy-start(bf16[32,2048]{1,0:T(8,128)(2,1)} %param.13) | copy-start | bytes 393220
  7.2 15.8 %copy-start.17 = (f32[32,8]{0,1:T(8,128)S(1)}, f32[32,8]{0,1:T(8,128)}, u32[]{:S(2)}) copy-start(f32[32,8]{0,1:T(8,128)} %param.19) | copy-start | bytes 3076
  11.5 31.6 %all-to-all-start = ((bf16[32,40,256]{2,1,0:T(8,128)(2,1)}), bf16[32,40,256]{2,1,0:T(8,128)(2,1)S(1)}, u32[]{:S(2)}, u32[]{:S(2)}) async-start(bf16[32,40,256]{2,1,0:T(8,128)(2,1)} %broadcast_in_dim.34), calls=%async_computation | async-start | bytes 1310720 | tf_op jit(solution)/shard_map/all_to_all | solution.py:35
  22.8 137.3 %all-gather.2.cloned.1.call-start = ((), (), s32[]{:S(2)}) async-start(), calls=%async_computation.6 | async-start | bytes 2359296 | tf_op jit(solution)/shard_map/all_gather | solution.py:245
  43.2 23.0 %collective-permute-start = (bf16[1024,256]{1,0:T(8,128)(2,1)S(1)}, bf16[1024,256]{1,0:T(8,128)(2,1)S(1)}, u32[]{:S(2)}, u32[]{:S(2)}) collective-permute-start(bf16[1024,256]{1,0:T(8,128)(2,1)S(1)} %bitcast.81), channel_id=1, source_target_pairs={{0,6},{2,0},{4,2},{6,4},{1,7},{3,1},{5,3},{7,5},{8,14},{10,8},{12,... | collective-permute-start | bytes 1572872 | tf_op jit(solution)/shard_map/ppermute | solution.py:27
  46.0 20.1 %collective-permute-start.1 = (bf16[1024,256]{1,0:T(8,128)(2,1)S(1)}, bf16[1024,256]{1,0:T(8,128)(2,1)S(1)}, u32[]{:S(2)}, u32[]{:S(2)}) collective-permute-start(bf16[1024,256]{1,0:T(8,128)(2,1)S(1)} %bitcast.82), channel_id=1, source_target_pairs={{0,4},{2,6},{4,0},{6,2},{1,5},{3,7},{5,1},{7,3},{8,12},{10,14},{12... | collective-permute-start | bytes 1572872 | tf_op jit(solution)/shard_map/ppermute | solution.py:27
  46.8 23.0 %collective-permute-start.2 = (bf16[1024,256]{1,0:T(8,128)(2,1)S(1)}, bf16[1024,256]{1,0:T(8,128)(2,1)S(1)}, u32[]{:S(2)}, u32[]{:S(2)}) collective-permute-start(bf16[1024,256]{1,0:T(8,128)(2,1)S(1)} %bitcast.83), channel_id=1, source_target_pairs={{0,2},{2,4},{4,6},{6,0},{1,3},{3,5},{5,7},{7,1},{8,10},{10,12},{12... | collective-permute-start | bytes 1572872 | tf_op jit(solution)/shard_map/ppermute | solution.py:27
  70.1 4.4 %collective-permute-start.3 = (bf16[1024,1024]{1,0:T(8,128)(2,1)S(1)}, bf16[1024,1024]{1,0:T(8,128)(2,1)}, u32[]{:S(2)}, u32[]{:S(2)}) collective-permute-start(bf16[1024,1024]{1,0:T(8,128)(2,1)S(1)} %constant_dynamic-update-slice_fusion.near_ref), channel_id=1, source_target_pairs={{0,1},{1,0},{2,3},{3,2},{4,5},{5,4},{6,7},{7,6},{8,9},{9,8},{10,11... | collective-permute-start | bytes 6291464 | tf_op jit(solution)/shard_map/ppermute | solution.py:31
  80.6 9.9 %collective-permute-start.8 = (bf16[1024,1024]{1,0:T(8,128)(2,1)}, bf16[1024,1024]{1,0:T(8,128)(2,1)S(1)}, u32[]{:S(2)}, u32[]{:S(2)}) collective-permute-start(bf16[1024,1024]{1,0:T(8,128)(2,1)} %convolution_convert_fusion), channel_id=1, source_target_pairs={{0,1},{1,0},{2,3},{3,2},{4,5},{5,4},{6,7},{7,6},{8,9},{9,8},{10,11... | collective-permute-start | bytes 6291464 | tf_op jit(solution)/shard_map/ppermute | solution.py:31
  81.5 3.3 %collective-permute-start.4 = (f32[8,128]{1,0:T(8,128)S(1)}, f32[8,128]{1,0:T(8,128)S(1)}, u32[]{:S(2)}, u32[]{:S(2)}) collective-permute-start(f32[8,128]{1,0:T(8,128)S(1)} %bitcast.88), channel_id=1, source_target_pairs={{0,1},{1,0},{2,3},{3,2},{4,5},{5,4},{6,7},{7,6},{8,9},{9,8},{10,11... | collective-permute-start | bytes 12296 | tf_op jit(solution)/shard_map/ppermute | solution.py:31
  84.8 4.8 %collective-permute-start.5 = (f32[8,128]{1,0:T(8,128)S(1)}, f32[8,128]{1,0:T(8,128)S(1)}, u32[]{:S(2)}, u32[]{:S(2)}) collective-permute-start(f32[8,128]{1,0:T(8,128)S(1)} %bitcast_add_fusion), channel_id=1, source_target_pairs={{0,2},{2,4},{4,6},{6,0},{1,3},{3,5},{5,7},{7,1},{8,10},{10,12},{12... | collective-permute-start | bytes 12296 | tf_op jit(solution)/shard_map/ppermute | solution.py:27
  84.8 5.1 %collective-permute-start.6 = (f32[8,128]{1,0:T(8,128)S(1)}, f32[8,128]{1,0:T(8,128)S(1)}, u32[]{:S(2)}, u32[]{:S(2)}) collective-permute-start(f32[8,128]{1,0:T(8,128)S(1)} %bitcast_add_fusion), channel_id=1, source_target_pairs={{0,4},{2,6},{4,0},{6,2},{1,5},{3,7},{5,1},{7,3},{8,12},{10,14},{12... | collective-permute-start | bytes 12296 | tf_op jit(solution)/shard_map/ppermute | solution.py:27
  86.9 3.6 %collective-permute-start.7 = (f32[8,128]{1,0:T(8,128)S(1)}, f32[8,128]{1,0:T(8,128)S(1)}, u32[]{:S(2)}, u32[]{:S(2)}) collective-permute-start(f32[8,128]{1,0:T(8,128)S(1)} %bitcast_add_fusion), channel_id=1, source_target_pairs={{0,6},{2,0},{4,2},{6,4},{1,7},{3,1},{5,3},{7,5},{8,14},{10,8},{12,... | collective-permute-start | bytes 12296 | tf_op jit(solution)/shard_map/ppermute | solution.py:27
  94.8 22.0 %collective-permute-start.10 = (bf16[1024,256]{1,0:T(8,128)(2,1)}, bf16[1024,256]{1,0:T(8,128)(2,1)S(1)}, u32[]{:S(2)}, u32[]{:S(2)}) collective-permute-start(bf16[1024,256]{1,0:T(8,128)(2,1)} %get-tuple-element.72), channel_id=1, source_target_pairs={{0,4},{2,6},{4,0},{6,2},{1,5},{3,7},{5,1},{7,3},{8,12},{10,14},{12... | collective-permute-start | bytes 1572872 | tf_op jit(solution)/shard_map/ppermute | solution.py:27
  96.6 29.3 %collective-permute-start.11 = (bf16[1024,256]{1,0:T(8,128)(2,1)}, bf16[1024,256]{1,0:T(8,128)(2,1)S(1)}, u32[]{:S(2)}, u32[]{:S(2)}) collective-permute-start(bf16[1024,256]{1,0:T(8,128)(2,1)} %get-tuple-element.73), channel_id=1, source_target_pairs={{0,6},{2,0},{4,2},{6,4},{1,7},{3,1},{5,3},{7,5},{8,14},{10,8},{12,... | collective-permute-start | bytes 1572872 | tf_op jit(solution)/shard_map/ppermute | solution.py:27
  99.4 26.8 %collective-permute-start.9 = (bf16[1024,256]{1,0:T(8,128)(2,1)S(1)}, bf16[1024,256]{1,0:T(8,128)(2,1)S(1)}, u32[]{:S(2)}, u32[]{:S(2)}) collective-permute-start(bf16[1024,256]{1,0:T(8,128)(2,1)S(1)} %get-tuple-element.71), channel_id=1, source_target_pairs={{0,2},{2,4},{4,6},{6,0},{1,3},{3,5},{5,7},{7,1},{8,10},{10,12},{12... | collective-permute-start | bytes 1572872 | tf_op jit(solution)/shard_map/ppermute | solution.py:27
  100.2 16.5 %all-to-all-start.2 = ((f32[32,8,128]{2,1,0:T(8,128)}), f32[32,8,128]{2,1,0:T(8,128)S(1)}, u32[]{:S(2)}, u32[]{:S(2)}) async-start(f32[32,8,128]{2,1,0:T(8,128)} %pad.9), calls=%async_computation.2 | async-start | bytes 262144 | tf_op jit(solution)/shard_map/all_to_all | solution.py:35
  107.1 19.1 %copy-start.3 = (f32[1024,256]{1,0:T(8,128)S(1)}, f32[1024,256]{1,0:T(8,128)}, u32[]{:S(2)}) copy-start(f32[1024,256]{1,0:T(8,128)} %copy-done.2) | copy-start | bytes 3145732
  116.8 37.2 %copy-start.10 = (f32[512,32]{1,0:T(8,128)S(1)}, f32[512,32]{1,0:T(8,128)}, u32[]{:S(2)}) copy-start(f32[512,32]{1,0:T(8,128)} %fusion.12) | copy-start | bytes 196612
  127.2 47.4 %copy-start.7 = (bf16[2,2048,128]{2,1,0:T(8,128)(2,1)S(1)}, bf16[2,2048,128]{2,1,0:T(8,128)(2,1)}, u32[]{:S(2)}) copy-start(bf16[2,2048,128]{2,1,0:T(8,128)(2,1)} %gate_ref.1) | copy-start | bytes 3145732
  127.2 25.8 %all-to-all-start.3 = ((bf16[32,32,256]{2,1,0:T(8,128)(2,1)}), bf16[32,32,256]{2,1,0:T(8,128)(2,1)S(1)}, u32[]{:S(2)}, u32[]{:S(2)}) async-start(bf16[32,32,256]{2,1,0:T(8,128)(2,1)} %bitcast.18), calls=%async_computation.3 | async-start | bytes 1048576 | tf_op jit(solution)/shard_map/all_to_all | solution.py:35
  155.3 16.7 %all-to-all-start.4 = ((bf16[32,16,256]{2,1,0:T(8,128)(2,1)}), bf16[32,16,256]{2,1,0:T(8,128)(2,1)S(1)}, u32[]{:S(2)}, u32[]{:S(2)}) async-start(bf16[32,16,256]{2,1,0:T(8,128)(2,1)} %bitcast.21), calls=%async_computation.4 | async-start | bytes 524288 | tf_op jit(solution)/shard_map/all_to_all | solution.py:35
  160.2 16.8 %copy-start.6 = (bf16[2,256,2048]{2,1,0:T(8,128)(2,1)S(1)}, bf16[2,256,2048]{2,1,0:T(8,128)(2,1)}, u32[]{:S(2)}) copy-start(bf16[2,256,2048]{2,1,0:T(8,128)(2,1)} %all-gather.2.cloned.1.call-done) | copy-start | bytes 6291460
  172.0 8.8 %collective-permute-start.12 = (bf16[2,256,256]{2,1,0:T(8,128)(2,1)S(1)}, bf16[2,256,256]{2,1,0:T(8,128)(2,1)S(1)}, u32[]{:S(2)}, u32[]{:S(2)}) collective-permute-start(bf16[2,256,256]{2,1,0:T(8,128)(2,1)S(1)} %copy_bitcast_fusion.1), channel_id=1, source_target_pairs={{0,6},{2,0},{4,2},{6,4},{1,7},{3,1},{5,3},{7,5},{8,14},{10,8},{12,... | collective-permute-start | bytes 786440 | tf_op jit(solution)/shard_map/ppermute | solution.py:27
  173.7 9.8 %collective-permute-start.13 = (bf16[2,256,256]{2,1,0:T(8,128)(2,1)S(1)}, bf16[2,256,256]{2,1,0:T(8,128)(2,1)S(1)}, u32[]{:S(2)}, u32[]{:S(2)}) collective-permute-start(bf16[2,256,256]{2,1,0:T(8,128)(2,1)S(1)} %copy_bitcast_fusion.1), channel_id=1, source_target_pairs={{0,4},{2,6},{4,0},{6,2},{1,5},{3,7},{5,1},{7,3},{8,12},{10,14},{12... | collective-permute-start | bytes 786440 | tf_op jit(solution)/shard_map/ppermute | solution.py:27
  174.1 12.0 %collective-permute-start.14 = (bf16[2,256,256]{2,1,0:T(8,128)(2,1)S(1)}, bf16[2,256,256]{2,1,0:T(8,128)(2,1)S(1)}, u32[]{:S(2)}, u32[]{:S(2)}) collective-permute-start(bf16[2,256,256]{2,1,0:T(8,128)(2,1)S(1)} %copy_bitcast_fusion.1), channel_id=1, source_target_pairs={{0,2},{2,4},{4,6},{6,0},{1,3},{3,5},{5,7},{7,1},{8,10},{10,12},{12... | collective-permute-start | bytes 786440 | tf_op jit(solution)/shard_map/ppermute | solution.py:27
  186.2 2.7 %collective-permute-start.15 = (bf16[2,256,1024]{2,1,0:T(8,128)(2,1)S(1)}, bf16[2,256,1024]{2,1,0:T(8,128)(2,1)S(1)}, u32[]{:S(2)}, u32[]{:S(2)}) collective-permute-start(bf16[2,256,1024]{2,1,0:T(8,128)(2,1)S(1)} %constant_dynamic-update-slice_fusion.4), channel_id=1, source_target_pairs={{0,1},{1,0},{2,3},{3,2},{4,5},{5,4},{6,7},{7,6},{8,9},{9,8},{10,11... | collective-permute-start | bytes 3145736 | tf_op jit(solution)/shard_map/ppermute | solution.py:31
  190.5 3.0 %collective-permute-start.16 = (bf16[2,256,1024]{2,1,0:T(8,128)(2,1)S(1)}, bf16[2,256,1024]{2,1,0:T(8,128)(2,1)S(1)}, u32[]{:S(2)}, u32[]{:S(2)}) collective-permute-start(bf16[2,256,1024]{2,1,0:T(8,128)(2,1)S(1)} %convolution_convert_fusion.1), channel_id=1, source_target_pairs={{0,1},{1,0},{2,3},{3,2},{4,5},{5,4},{6,7},{7,6},{8,9},{9,8},{10,11... | collective-permute-start | bytes 3145736 | tf_op jit(solution)/shard_map/ppermute | solution.py:31
  193.9 38.7 %copy-start.11 = (f32[512,32]{1,0:T(8,128)S(1)}, f32[512,32]{1,0:T(8,128)}, u32[]{:S(2)}) copy-start(f32[512,32]{1,0:T(8,128)} %fusion.12) | copy-start | bytes 196612
  194.0 15.3 %collective-permute-start.17 = (bf16[2,256,256]{2,1,0:T(8,128)(2,1)S(1)}, bf16[2,256,256]{2,1,0:T(8,128)(2,1)S(1)}, u32[]{:S(2)}, u32[]{:S(2)}) collective-permute-start(bf16[2,256,256]{2,1,0:T(8,128)(2,1)S(1)} %get-tuple-element.99), channel_id=1, source_target_pairs={{0,2},{2,4},{4,6},{6,0},{1,3},{3,5},{5,7},{7,1},{8,10},{10,12},{12... | collective-permute-start | bytes 786440 | tf_op jit(solution)/shard_map/ppermute | solution.py:27
  194.1 15.2 %collective-permute-start.18 = (bf16[2,256,256]{2,1,0:T(8,128)(2,1)S(1)}, bf16[2,256,256]{2,1,0:T(8,128)(2,1)S(1)}, u32[]{:S(2)}, u32[]{:S(2)}) collective-permute-start(bf16[2,256,256]{2,1,0:T(8,128)(2,1)S(1)} %get-tuple-element.101), channel_id=1, source_target_pairs={{0,4},{2,6},{4,0},{6,2},{1,5},{3,7},{5,1},{7,3},{8,12},{10,14},{12... | collective-permute-start | bytes 786440 | tf_op jit(solution)/shard_map/ppermute | solution.py:27
  196.3 13.6 %collective-permute-start.19 = (bf16[2,256,256]{2,1,0:T(8,128)(2,1)S(1)}, bf16[2,256,256]{2,1,0:T(8,128)(2,1)S(1)}, u32[]{:S(2)}, u32[]{:S(2)}) collective-permute-start(bf16[2,256,256]{2,1,0:T(8,128)(2,1)S(1)} %get-tuple-element.100), channel_id=1, source_target_pairs={{0,6},{2,0},{4,2},{6,4},{1,7},{3,1},{5,3},{7,5},{8,14},{10,8},{12,... | collective-permute-start | bytes 786440 | tf_op jit(solution)/shard_map/ppermute | solution.py:27
  (13 other events, 78.3 us)
Sparse Core Ops, SparseCore 0:
  81.7 42.3 all-gather.1

commit v3 on v2

--- a/solution.py
+++ b/solution.py
@@ -37,6 +37,40 @@
 
 def in_ring_order(a, move, ring):
     return [a] + [move(a, ring - k) for k in range(1, ring)]
+
+
+def normed_to_spread(at, layer_out, final_gain, digits, copies):
+    rows, width = layer_out.shape
+    below, share = digits.shape
+
+    def body(at_ref, rows_ref, gain_ref, digits_ref, spread_out, unit_out, scale_out, gain_out):
+        low = pl.multiple_of(at_ref[0] * share, share)
+        values = rows_ref[...].astype(f32)
+        mean = jnp.sum(values * values, axis=1, keepdims=True) / width
+        scale = jnp.sqrt(mean + epsilon)
+        unit = rows_ref[:, pl.ds(low, share)].astype(f32) / scale
+        gain = gain_ref[:, pl.ds(low, share)]
+        normed = (unit * gain).astype(bf16)
+        for k in range(copies):
+            spread_out[k, :rows, :] = normed
+            spread_out[k, rows:, :] = digits_ref[...]
+        unit_out[...] = unit
+        scale_out[...] = scale
+        gain_out[...] = gain
+
+    whole = pl.BlockSpec(memory_space=pltpu.VMEM)
+    return pl.pallas_call(
+        body,
+        in_specs=[pl.BlockSpec(memory_space=pltpu.SMEM)] + [whole] * 3,
+        out_specs=[whole] * 4,
+        out_shape=[
+            jax.ShapeDtypeStruct((copies, rows + below, share), bf16),
+            jax.ShapeDtypeStruct((rows, share), f32),
+            jax.ShapeDtypeStruct((rows, 1), f32),
+            jax.ShapeDtypeStruct((1, share), f32),
+        ],
+        name="normed_to_spread",
+    )(at[None], layer_out, final_gain[None, :], digits)
 
 
 def turned_weights(order, head_weight, w_gate, w_up, w_down):
@@ -195,13 +229,12 @@
         order, head_weight, w_gate, w_up, w_down
     )
 
-    values = layer_out.astype(f32)
-    row_scale = jnp.sqrt(jnp.mean(values * values, axis=1, keepdims=True) + epsilon)
-    unit_share = (
-        lax.dynamic_slice_in_dim(layer_out, v_at * share, share, 1).astype(f32) / row_scale
-    )
-    gain_share = lax.dynamic_slice_in_dim(final_gain, v_at * share, share, 0)[None, :]
-    normed_share = (unit_share * gain_share).astype(bf16)
+    code = clean_ids * ratio_table.shape[0] + levels
+    digits = jnp.stack([code % 256, code // 256 % 256, code // 65536]).astype(bf16)
+    digits = jnp.pad(digits, ((0, 8 - digits.shape[0]), (0, share - rows)))
+    spread, unit_share, row_scale, gain_share = normed_to_spread(
+        v_at, layer_out, final_gain, digits, n_expert
+    )
 
     labels = jnp.arange(experts, dtype=jnp.int32)
     hits = expert_ids[:, :, None] == labels
@@ -223,12 +256,6 @@
     inputs = wide_dot(pick.astype(bf16), moe_share, ((1,), (0,))).astype(bf16)
     inputs = inputs.reshape(n_expert, own_experts * capacity, share)
 
-    code = clean_ids * ratio_table.shape[0] + levels
-    digits = jnp.stack([code % 256, code // 256 % 256, code // 65536]).astype(bf16)
-    digits = jnp.pad(digits, ((0, 8 - digits.shape[0]), (0, share - rows)))
-    spread = jnp.broadcast_to(
-        jnp.concatenate([normed_share, digits], axis=0)[None], (n_expert, rows + 8, share)
-    )
     spread = exchanged(spread, ("y", "z"))
     spread, head_near, head_far, pair_turned, down_turned, inputs, pick, slot_gate = (
         lax.optimization_barrier(
@@ -267,10 +294,6 @@
     score_grad, along = lax.optimization_barrier((score_grad, along))
     far = wide_dot(score_grad, head_far, ((1,), (1,))).astype(bf16)
     far = across_core(far)
-    along = along.reshape(8, all_rows // 8)
-    along = along + across_core(along)
-    along = along + sum(along_x(along, k) for k in range(1, XN))
-    along, far = lax.optimization_barrier((along, far))
     kept, *sent = near_gradient(score_grad, head_near, far)
     kept, sent, score_grad, along = lax.optimization_barrier((kept, sent, score_grad, along))
     sent = [along_x(a, k + 1) for k, a in enumerate(sent)]
@@ -278,6 +301,8 @@
     along = jnp.sum(exchanged(along, ("y", "z")), axis=0)
     head_grad = head_gradient(order, normed_near, normed_far, score_grad)
     sent, head_grad, along = lax.optimization_barrier((sent, head_grad, along))
+    along = along + across_core(along)
+    along = along + sum(along_x(along, k) for k in range(1, XN))
     kept = (kept + sum(a.astype(f32) for a in sent)).astype(bf16)
     kept = exchanged(kept.reshape(n_expert, rows, share), ("y", "z"))
     normed_grad = jnp.sum(kept.astype(f32), axis=0)

time: 242 us -> 237 us (0.979)
  waiting for transfers between devices: 87.6 us -> 81.1 us
    all_to_all x4, waiting for transfers between devices: 39.1 us -> 27.7 us  [exchanged(): return lax.all_to_all(a, axes, 0, 0, tiled=True)]
    ppermute x15, waiting for transfers between devices: 38.8 us -> 41.8 us  [along_x(): return lax.ppermute(a, 'x', [(p, (p + step) % XN) for p in range(XN)])]
  transfers between devices with their start and end apart: 25 -> 25, of which waited for: 20 -> 21; matrix products, arithmetic and copies ran while one was open for 5% -> 6% of each run, Pallas kernels for 8% -> 8%
where the time goes in v3:
time: 237 us; the launch traced here: 234 us
  waiting for transfers between devices  81.1 us (34%)
  starting transfers between devices  50.9 us (21%)
  blocking collectives  38.7 us (16%)
  Pallas kernels  20.8 us (9%)
  between operations  14.6 us (6%)
  matrix products  14.4 us (6%)
  other arithmetic  6.95 us (3%)
  local copies, waits for them, and re-layouts  6.81 us (3%)
    ppermute x15, waiting for transfers between devices, along_x(): return lax.ppermute(a, 'x', [(p, (p + step) % XN) for p in range(XN)])  41.8 us
    all_to_all x4, starting transfers between devices, exchanged(): return lax.all_to_all(a, axes, 0, 0, tiled=True)  31.4 us
    all_to_all x4, waiting for transfers between devices, exchanged(): return lax.all_to_all(a, axes, 0, 0, tiled=True)  27.7 us
    all_to_all x1, blocking collectives, on_device(): returned = lax.all_to_all(near, ('y', 'z'), 0, 0, tiled=True)  22.6 us
    ppermute x15, starting transfers between devices, along_x(): return lax.ppermute(a, 'x', [(p, (p + step) % XN) for p in range(XN)])  18.6 us
    all_to_all x1, blocking collectives, exchanged(): return lax.all_to_all(a, axes, 0, 0, tiled=True)  16.1 us
    ppermute x5, waiting for transfers between devices, across_core(): return lax.ppermute(a, 'core', [(p, CN - 1 - p) for p in range(CN)])  11.6 us
    dot_general x7, matrix products, wide_dot(): lax.dot_general(a, b, (dims, ((), ())), preferred_element_type=f32, preci...  9.59 us
  transfers between devices with their start and end apart: 25, of which 21 were waited for; matrix products, arithmetic and copies ran while one was open for 6% of the time, Pallas kernels for 8%

profile of v3, /device:TPU:32, one launch (start us, length us, event | category | flops | bytes accessed | tf_op | source)
XLA Modules:
  0.0 234.3 jit_solution(12805127735307325914)
XLA Ops:
  8.5 1.9 normed_to_spread.1
  10.5 11.4 %all-to-all-start = ((bf16[32,40,256]{2,1,0:T(8,128)(2,1)}), bf16[32,40,256]{2,1,0:T(8,128)(2,1)S(1)}, u32[]{:S(2)}, u32[]{:S(2)}) async-start(bf16[32,40,256]{2,1,0:T(8,128)(2,1)} %get-tuple-element.51), calls=%async_computation | async-start | bytes 1310720 | tf_op jit(solution)/shard_map/all_to_all | solution.py:35
  25.0 7.8 %turned_weights.1 = (bf16[1024,384]{1,0:T(8,128)(2,1)}, bf16[1024,384]{1,0:T(8,128)(2,1)}, bf16[2,2048,256]{2,1,0:T(8,128)(2,1)}, bf16[2,128,2048]{2,1,0:T(8,128)(2,1)}) custom-call(s32[8]{0:T(128)} %stack.55.order_ref, bf16[2048,384]{1,0:T(8,128)(2,1)} %head_ref.1, bf16[2,2048,128]{2,1,0:T(8,128)(2,1)} %gate_ref.1, bf16[2,2048,128]{2,1,0:T(8,128)(2,1)} %up_ref.1, ...), custom_call_target="tpu_custom_call" | custom-call | bytes 9437184 | tf_op jit(solution)/shard_map/turned_weights/pallas_call | solution.py:100
  34.0 8.1 %all-to-all-done = bf16[32,40,256]{2,1,0:T(8,128)(2,1)S(1)} async-done(((bf16[32,40,256]{2,1,0:T(8,128)(2,1)}), bf16[32,40,256]{2,1,0:T(8,128)(2,1)S(1)}, u32[]{:S(2)}, u32[]{:S(2)}) %all-to-all-start) | async-done | bytes 655392 | tf_op jit(solution)/shard_map/all_to_all | solution.py:35
  42.2 2.8 %collective-permute-start = (bf16[1024,256]{1,0:T(8,128)(2,1)S(1)}, bf16[1024,256]{1,0:T(8,128)(2,1)S(1)}, u32[]{:S(2)}, u32[]{:S(2)}) collective-permute-start(bf16[1024,256]{1,0:T(8,128)(2,1)S(1)} %bitcast.80), channel_id=1, source_target_pairs={{0,6},{2,0},{4,2},{6,4},{1,7},{3,1},{5,3},{7,5},{8,14},{10,8},{12,... | collective-permute-start | bytes 1572872 | tf_op jit(solution)/shard_map/ppermute | solution.py:27
  46.7 16.1 %all_to_all.30 = bf16[32,16,256]{2,1,0:T(8,128)(2,1)} all-to-all(bf16[32,16,256]{2,1,0:T(8,128)(2,1)S(1)} %bitcast.85), channel_id=1, replica_groups=mesh['y'=4,'z'=8,'x'=4,'core'=2] {'y','z'}, dimensions={0} | all-to-all | bytes 524288 | tf_op jit(solution)/shard_map/all_to_all | solution.py:35
  62.8 2.4 %collective-permute-done = bf16[1024,256]{1,0:T(8,128)(2,1)S(1)} collective-permute-done((bf16[1024,256]{1,0:T(8,128)(2,1)S(1)}, bf16[1024,256]{1,0:T(8,128)(2,1)S(1)}, u32[]{:S(2)}, u32[]{:S(2)}) %collective-permute-start) | collective-permute-done | bytes 524320 | tf_op jit(solution)/shard_map/ppermute | solution.py:27
  65.1 3.7 %collective-permute-done.2 = bf16[1024,256]{1,0:T(8,128)(2,1)S(1)} collective-permute-done((bf16[1024,256]{1,0:T(8,128)(2,1)S(1)}, bf16[1024,256]{1,0:T(8,128)(2,1)S(1)}, u32[]{:S(2)}, u32[]{:S(2)}) %collective-permute-start.2) | collective-permute-done | bytes 524320 | tf_op jit(solution)/shard_map/ppermute | solution.py:27
  73.5 2.8 %fusion.42 = f32[1024,384]{1,0:T(8,128)S(1)} fusion(bf16[1024,1024]{1,0:T(8,128)(2,1)} %collective-permute-done.3.far_ref, bf16[1024,384]{1,0:T(8,128)(2,1)S(1)} %copy-done.21), kind=kOutput, calls=%fused_computation.104 | convolution fusion | flops 805306368 | bytes 4456448 | tf_op jit(solution)/shard_map/dot_general | solution.py:17
  77.0 2.6 %convolution_convert_fusion = bf16[1024,1024]{1,0:T(8,128)(2,1)} fusion(bf16[1024,384]{1,0:T(8,128)(2,1)S(1)} %get-tuple-element.75.grad_ref, bf16[1024,384]{1,0:T(8,128)(2,1)S(1)} %copy-done.21), kind=kOutput, calls=%fused_computation.1 | convolution fusion | flops 806354944 | bytes 3670016 | tf_op jit(solution)/shard_map/dot_general | solution.py:17
  80.5 3.5 %collective-permute-done.4.far_ref = bf16[1024,1024]{1,0:T(8,128)(2,1)S(1)} collective-permute-done((bf16[1024,1024]{1,0:T(8,128)(2,1)}, bf16[1024,1024]{1,0:T(8,128)(2,1)S(1)}, u32[]{:S(2)}, u32[]{:S(2)}) %collective-permute-start.4) | collective-permute-done | bytes 2097184 | tf_op jit(solution)/shard_map/ppermute | solution.py:31
  88.0 2.1 collective-permute-start.6
  92.2 6.8 %all-to-all-start.2 = ((f32[32,8,128]{2,1,0:T(8,128)}), f32[32,8,128]{2,1,0:T(8,128)S(1)}, u32[]{:S(2)}, u32[]{:S(2)}) async-start(f32[32,8,128]{2,1,0:T(8,128)} %pad.9), calls=%async_computation.2 | async-start | bytes 262144 | tf_op jit(solution)/shard_map/all_to_all | solution.py:35
  99.0 9.2 %head_gradient.1 = f32[2048,384]{1,0:T(8,128)} custom-call(s32[8]{0:T(128)} %stack.55.order_ref, bf16[1024,1024]{1,0:T(8,128)(2,1)} %copy-done.9, bf16[1024,1024]{1,0:T(8,128)(2,1)} %collective-permute-done.3.far_ref, bf16[1024,384]{1,0:T(8,128)(2,1)} %copy-done.1), custom_call_target="tpu_custom_call" | custom-call | flops 1024 | bytes 1024 | tf_op jit(solution)/shard_map/head_gradient/pallas_call | solution.py:148
  108.8 4.1 %collective-permute-done.5 = bf16[1024,256]{1,0:T(8,128)(2,1)S(1)} collective-permute-done((bf16[1024,256]{1,0:T(8,128)(2,1)}, bf16[1024,256]{1,0:T(8,128)(2,1)S(1)}, u32[]{:S(2)}, u32[]{:S(2)}) %collective-permute-start.5) | collective-permute-done | bytes 524320 | tf_op jit(solution)/shard_map/ppermute | solution.py:27
  112.9 9.0 %collective-permute-done.6 = bf16[1024,256]{1,0:T(8,128)(2,1)S(1)} collective-permute-done((bf16[1024,256]{1,0:T(8,128)(2,1)}, bf16[1024,256]{1,0:T(8,128)(2,1)S(1)}, u32[]{:S(2)}, u32[]{:S(2)}) %collective-permute-start.6) | collective-permute-done | bytes 524320 | tf_op jit(solution)/shard_map/ppermute | solution.py:27
  122.4 2.0 add_convert_fusion
  124.4 8.4 %all-to-all-start.3 = ((bf16[32,32,256]{2,1,0:T(8,128)(2,1)}), bf16[32,32,256]{2,1,0:T(8,128)(2,1)S(1)}, u32[]{:S(2)}, u32[]{:S(2)}) async-start(bf16[32,32,256]{2,1,0:T(8,128)(2,1)} %bitcast.20), calls=%async_computation.3 | async-start | bytes 1048576 | tf_op jit(solution)/shard_map/all_to_all | solution.py:35
  134.6 2.0 collective-permute-start.11
  136.7 2.4 %collective-permute-done.10 = f32[8,128]{1,0:T(8,128)S(1)} collective-permute-done((f32[8,128]{1,0:T(8,128)S(1)}, f32[8,128]{1,0:T(8,128)S(1)}, u32[]{:S(2)}, u32[]{:S(2)}) %collective-permute-start.10) | collective-permute-done | bytes 4128 | tf_op jit(solution)/shard_map/ppermute | solution.py:27
  139.2 2.2 collective-permute-done.9
  141.4 8.0 %all-to-all-done.3 = bf16[32,32,256]{2,1,0:T(8,128)(2,1)S(1)} async-done(((bf16[32,32,256]{2,1,0:T(8,128)(2,1)}), bf16[32,32,256]{2,1,0:T(8,128)(2,1)S(1)}, u32[]{:S(2)}, u32[]{:S(2)}) %all-to-all-start.3) | async-done | bytes 524320 | tf_op jit(solution)/shard_map/all_to_all | solution.py:35
  150.9 4.9 %all-to-all-start.4 = ((bf16[32,16,256]{2,1,0:T(8,128)(2,1)}), bf16[32,16,256]{2,1,0:T(8,128)(2,1)S(1)}, u32[]{:S(2)}, u32[]{:S(2)}) async-start(bf16[32,16,256]{2,1,0:T(8,128)(2,1)} %bitcast.23), calls=%async_computation.4 | async-start | bytes 524288 | tf_op jit(solution)/shard_map/all_to_all | solution.py:35
  155.8 11.1 %all-to-all-done.4 = bf16[32,16,256]{2,1,0:T(8,128)(2,1)S(1)} async-done(((bf16[32,16,256]{2,1,0:T(8,128)(2,1)}), bf16[32,16,256]{2,1,0:T(8,128)(2,1)S(1)}, u32[]{:S(2)}, u32[]{:S(2)}) %all-to-all-start.4) | async-done | bytes 262176 | tf_op jit(solution)/shard_map/all_to_all | solution.py:35
  167.7 2.7 %collective-permute-start.13 = (bf16[2,256,256]{2,1,0:T(8,128)(2,1)S(1)}, bf16[2,256,256]{2,1,0:T(8,128)(2,1)S(1)}, u32[]{:S(2)}, u32[]{:S(2)}) collective-permute-start(bf16[2,256,256]{2,1,0:T(8,128)(2,1)S(1)} %copy_bitcast_fusion.1), channel_id=1, source_target_pairs={{0,4},{2,6},{4,0},{6,2},{1,5},{3,7},{5,1},{7,3},{8,12},{10,14},{12... | collective-permute-start | bytes 786440 | tf_op jit(solution)/shard_map/ppermute | solution.py:27
  170.4 2.3 fusion.43
  177.0 2.7 %collective-permute-done.14 = bf16[2,256,256]{2,1,0:T(8,128)(2,1)S(1)} collective-permute-done((bf16[2,256,256]{2,1,0:T(8,128)(2,1)S(1)}, bf16[2,256,256]{2,1,0:T(8,128)(2,1)S(1)}, u32[]{:S(2)}, u32[]{:S(2)}) %collective-permute-start.14) | collective-permute-done | bytes 262176 | tf_op jit(solution)/shard_map/ppermute | solution.py:27
  179.9 2.6 %collective-permute-done.15 = bf16[2,256,1024]{2,1,0:T(8,128)(2,1)S(1)} collective-permute-done((bf16[2,256,1024]{2,1,0:T(8,128)(2,1)S(1)}, bf16[2,256,1024]{2,1,0:T(8,128)(2,1)S(1)}, u32[]{:S(2)}, u32[]{:S(2)}) %collective-permute-start.15) | collective-permute-done | bytes 1048608 | tf_op jit(solution)/shard_map/ppermute | solution.py:31
  184.6 2.5 %collective-permute-done.16 = bf16[2,256,1024]{2,1,0:T(8,128)(2,1)S(1)} collective-permute-done((bf16[2,256,1024]{2,1,0:T(8,128)(2,1)S(1)}, bf16[2,256,1024]{2,1,0:T(8,128)(2,1)S(1)}, u32[]{:S(2)}, u32[]{:S(2)}) %collective-permute-start.16) | collective-permute-done | bytes 1048608 | tf_op jit(solution)/shard_map/ppermute | solution.py:31
  190.1 2.3 collective-permute-start.19
  192.3 10.6 %collective-permute-done.17 = bf16[2,256,256]{2,1,0:T(8,128)(2,1)S(1)} collective-permute-done((bf16[2,256,256]{2,1,0:T(8,128)(2,1)S(1)}, bf16[2,256,256]{2,1,0:T(8,128)(2,1)S(1)}, u32[]{:S(2)}, u32[]{:S(2)}) %collective-permute-start.17) | collective-permute-done | bytes 262176 | tf_op jit(solution)/shard_map/ppermute | solution.py:27
  203.6 22.6 %all_to_all.31 = f32[32,16,256]{2,1,0:T(8,128)S(1)} all-to-all(f32[32,16,256]{2,1,0:T(8,128)S(1)} %copy_bitcast_fusion), channel_id=1, replica_groups=mesh['y'=4,'z'=8,'x'=4,'core'=2] {'y','z'}, dimensions={0} | all-to-all | bytes 1048576 | tf_op jit(solution)/shard_map/all_to_all | solution.py:347
  (127 shorter events, 36.0 us)
Async XLA Ops:
  7.2 26.5 %copy-start = (bf16[32,2048]{1,0:T(8,128)(2,1)S(1)}, bf16[32,2048]{1,0:T(8,128)(2,1)}, u32[]{:S(2)}) copy-start(bf16[32,2048]{1,0:T(8,128)(2,1)} %param.13) | copy-start | bytes 393220
  10.5 31.6 %all-to-all-start = ((bf16[32,40,256]{2,1,0:T(8,128)(2,1)}), bf16[32,40,256]{2,1,0:T(8,128)(2,1)S(1)}, u32[]{:S(2)}, u32[]{:S(2)}) async-start(bf16[32,40,256]{2,1,0:T(8,128)(2,1)} %get-tuple-element.51), calls=%async_computation | async-start | bytes 1310720 | tf_op jit(solution)/shard_map/all_to_all | solution.py:35
  21.8 134.0 %all-gather.2.cloned.1.call-start = ((), (), s32[]{:S(2)}) async-start(), calls=%async_computation.6 | async-start | bytes 2359296 | tf_op jit(solution)/shard_map/all_gather | solution.py:272
  42.2 23.0 %collective-permute-start = (bf16[1024,256]{1,0:T(8,128)(2,1)S(1)}, bf16[1024,256]{1,0:T(8,128)(2,1)S(1)}, u32[]{:S(2)}, u32[]{:S(2)}) collective-permute-start(bf16[1024,256]{1,0:T(8,128)(2,1)S(1)} %bitcast.80), channel_id=1, source_target_pairs={{0,6},{2,0},{4,2},{6,4},{1,7},{3,1},{5,3},{7,5},{8,14},{10,8},{12,... | collective-permute-start | bytes 1572872 | tf_op jit(solution)/shard_map/ppermute | solution.py:27
  45.0 20.1 %collective-permute-start.1 = (bf16[1024,256]{1,0:T(8,128)(2,1)S(1)}, bf16[1024,256]{1,0:T(8,128)(2,1)S(1)}, u32[]{:S(2)}, u32[]{:S(2)}) collective-permute-start(bf16[1024,256]{1,0:T(8,128)(2,1)S(1)} %bitcast.81), channel_id=1, source_target_pairs={{0,4},{2,6},{4,0},{6,2},{1,5},{3,7},{5,1},{7,3},{8,12},{10,14},{12... | collective-permute-start | bytes 1572872 | tf_op jit(solution)/shard_map/ppermute | solution.py:27
  45.8 23.0 %collective-permute-start.2 = (bf16[1024,256]{1,0:T(8,128)(2,1)S(1)}, bf16[1024,256]{1,0:T(8,128)(2,1)S(1)}, u32[]{:S(2)}, u32[]{:S(2)}) collective-permute-start(bf16[1024,256]{1,0:T(8,128)(2,1)S(1)} %bitcast.82), channel_id=1, source_target_pairs={{0,2},{2,4},{4,6},{6,0},{1,3},{3,5},{5,7},{7,1},{8,10},{10,12},{12... | collective-permute-start | bytes 1572872 | tf_op jit(solution)/shard_map/ppermute | solution.py:27
  69.1 4.4 %collective-permute-start.3 = (bf16[1024,1024]{1,0:T(8,128)(2,1)S(1)}, bf16[1024,1024]{1,0:T(8,128)(2,1)}, u32[]{:S(2)}, u32[]{:S(2)}) collective-permute-start(bf16[1024,1024]{1,0:T(8,128)(2,1)S(1)} %constant_dynamic-update-slice_fusion.near_ref), channel_id=1, source_target_pairs={{0,1},{1,0},{2,3},{3,2},{4,5},{5,4},{6,7},{7,6},{8,9},{9,8},{10,11... | collective-permute-start | bytes 6291464 | tf_op jit(solution)/shard_map/ppermute | solution.py:31
  79.6 4.4 %collective-permute-start.4 = (bf16[1024,1024]{1,0:T(8,128)(2,1)}, bf16[1024,1024]{1,0:T(8,128)(2,1)S(1)}, u32[]{:S(2)}, u32[]{:S(2)}) collective-permute-start(bf16[1024,1024]{1,0:T(8,128)(2,1)} %convolution_convert_fusion), channel_id=1, source_target_pairs={{0,1},{1,0},{2,3},{3,2},{4,5},{5,4},{6,7},{7,6},{8,9},{9,8},{10,11... | collective-permute-start | bytes 6291464 | tf_op jit(solution)/shard_map/ppermute | solution.py:31
  88.0 24.9 %collective-permute-start.5 = (bf16[1024,256]{1,0:T(8,128)(2,1)}, bf16[1024,256]{1,0:T(8,128)(2,1)S(1)}, u32[]{:S(2)}, u32[]{:S(2)}) collective-permute-start(bf16[1024,256]{1,0:T(8,128)(2,1)} %get-tuple-element.72), channel_id=1, source_target_pairs={{0,2},{2,4},{4,6},{6,0},{1,3},{3,5},{5,7},{7,1},{8,10},{10,12},{12... | collective-permute-start | bytes 1572872 | tf_op jit(solution)/shard_map/ppermute | solution.py:27
  88.0 33.9 %collective-permute-start.6 = (bf16[1024,256]{1,0:T(8,128)(2,1)}, bf16[1024,256]{1,0:T(8,128)(2,1)S(1)}, u32[]{:S(2)}, u32[]{:S(2)}) collective-permute-start(bf16[1024,256]{1,0:T(8,128)(2,1)} %get-tuple-element.73), channel_id=1, source_target_pairs={{0,4},{2,6},{4,0},{6,2},{1,5},{3,7},{5,1},{7,3},{8,12},{10,14},{12... | collective-permute-start | bytes 1572872 | tf_op jit(solution)/shard_map/ppermute | solution.py:27
  90.1 32.3 %collective-permute-start.7 = (bf16[1024,256]{1,0:T(8,128)(2,1)S(1)}, bf16[1024,256]{1,0:T(8,128)(2,1)}, u32[]{:S(2)}, u32[]{:S(2)}) collective-permute-start(bf16[1024,256]{1,0:T(8,128)(2,1)S(1)} %get-tuple-element.74), channel_id=1, source_target_pairs={{0,6},{2,0},{4,2},{6,4},{1,7},{3,1},{5,3},{7,5},{8,14},{10,8},{12,... | collective-permute-start | bytes 1572872 | tf_op jit(solution)/shard_map/ppermute | solution.py:27
  92.2 16.5 %all-to-all-start.2 = ((f32[32,8,128]{2,1,0:T(8,128)}), f32[32,8,128]{2,1,0:T(8,128)S(1)}, u32[]{:S(2)}, u32[]{:S(2)}) async-start(f32[32,8,128]{2,1,0:T(8,128)} %pad.9), calls=%async_computation.2 | async-start | bytes 262144 | tf_op jit(solution)/shard_map/all_to_all | solution.py:35
  108.7 27.9 %copy-start.18 = (f32[32,1]{1,0:T(8,128)S(1)}, f32[32,1]{1,0:T(8,128)}, u32[]{:S(2)}) copy-start(f32[32,1]{1,0:T(8,128)} %get-tuple-element.85) | copy-start | bytes 388
  108.7 40.8 %copy-start.17 = (f32[32,256]{1,0:T(8,128)S(1)}, f32[32,256]{1,0:T(8,128)}, u32[]{:S(2)}) copy-start(f32[32,256]{1,0:T(8,128)} %get-tuple-element.83) | copy-start | bytes 98308
  108.8 40.8 %copy-start.19 = (f32[1,256]{1,0:T(1,128)S(1)}, f32[1,256]{1,0:T(1,128)}, u32[]{:S(2)}) copy-start(f32[1,256]{1,0:T(1,128)} %get-tuple-element.78) | copy-start | bytes 3076
  108.8 40.9 %copy-start.10 = (f32[512,32]{1,0:T(8,128)S(1)}, f32[512,32]{1,0:T(8,128)}, u32[]{:S(2)}) copy-start(f32[512,32]{1,0:T(8,128)} %fusion.12) | copy-start | bytes 196612
  124.4 46.0 %copy-start.7 = (bf16[2,2048,128]{2,1,0:T(8,128)(2,1)S(1)}, bf16[2,2048,128]{2,1,0:T(8,128)(2,1)}, u32[]{:S(2)}) copy-start(bf16[2,2048,128]{2,1,0:T(8,128)(2,1)} %gate_ref.1) | copy-start | bytes 3145732
  124.4 25.0 %all-to-all-start.3 = ((bf16[32,32,256]{2,1,0:T(8,128)(2,1)}), bf16[32,32,256]{2,1,0:T(8,128)(2,1)S(1)}, u32[]{:S(2)}, u32[]{:S(2)}) async-start(bf16[32,32,256]{2,1,0:T(8,128)(2,1)} %bitcast.20), calls=%async_computation.3 | async-start | bytes 1048576 | tf_op jit(solution)/shard_map/all_to_all | solution.py:35
  132.8 1.3 collective-permute-start.8
  134.1 5.1 %collective-permute-start.10 = (f32[8,128]{1,0:T(8,128)S(1)}, f32[8,128]{1,0:T(8,128)S(1)}, u32[]{:S(2)}, u32[]{:S(2)}) collective-permute-start(f32[8,128]{1,0:T(8,128)S(1)} %add.261), channel_id=1, source_target_pairs={{0,4},{2,6},{4,0},{6,2},{1,5},{3,7},{5,1},{7,3},{8,12},{10,14},{12... | collective-permute-start | bytes 12296 | tf_op jit(solution)/shard_map/ppermute | solution.py:27
  134.6 4.6 %collective-permute-start.11 = (f32[8,128]{1,0:T(8,128)S(1)}, f32[8,128]{1,0:T(8,128)S(1)}, u32[]{:S(2)}, u32[]{:S(2)}) collective-permute-start(f32[8,128]{1,0:T(8,128)S(1)} %add.261), channel_id=1, source_target_pairs={{0,6},{2,0},{4,2},{6,4},{1,7},{3,1},{5,3},{7,5},{8,14},{10,8},{12,... | collective-permute-start | bytes 12296 | tf_op jit(solution)/shard_map/ppermute | solution.py:27
  136.6 4.8 %collective-permute-start.9 = (f32[8,128]{1,0:T(8,128)S(1)}, f32[8,128]{1,0:T(8,128)S(1)}, u32[]{:S(2)}, u32[]{:S(2)}) collective-permute-start(f32[8,128]{1,0:T(8,128)S(1)} %add.261), channel_id=1, source_target_pairs={{0,2},{2,4},{4,6},{6,0},{1,3},{3,5},{5,7},{7,1},{8,10},{10,12},{12... | collective-permute-start | bytes 12296 | tf_op jit(solution)/shard_map/ppermute | solution.py:27
  150.9 16.0 %all-to-all-start.4 = ((bf16[32,16,256]{2,1,0:T(8,128)(2,1)}), bf16[32,16,256]{2,1,0:T(8,128)(2,1)S(1)}, u32[]{:S(2)}, u32[]{:S(2)}) async-start(bf16[32,16,256]{2,1,0:T(8,128)(2,1)} %bitcast.23), calls=%async_computation.4 | async-start | bytes 524288 | tf_op jit(solution)/shard_map/all_to_all | solution.py:35
  166.9 8.1 %collective-permute-start.12 = (bf16[2,256,256]{2,1,0:T(8,128)(2,1)S(1)}, bf16[2,256,256]{2,1,0:T(8,128)(2,1)S(1)}, u32[]{:S(2)}, u32[]{:S(2)}) collective-permute-start(bf16[2,256,256]{2,1,0:T(8,128)(2,1)S(1)} %copy_bitcast_fusion.1), channel_id=1, source_target_pairs={{0,6},{2,0},{4,2},{6,4},{1,7},{3,1},{5,3},{7,5},{8,14},{10,8},{12,... | collective-permute-start | bytes 786440 | tf_op jit(solution)/shard_map/ppermute | solution.py:27
  167.7 9.3 %collective-permute-start.13 = (bf16[2,256,256]{2,1,0:T(8,128)(2,1)S(1)}, bf16[2,256,256]{2,1,0:T(8,128)(2,1)S(1)}, u32[]{:S(2)}, u32[]{:S(2)}) collective-permute-start(bf16[2,256,256]{2,1,0:T(8,128)(2,1)S(1)} %copy_bitcast_fusion.1), channel_id=1, source_target_pairs={{0,4},{2,6},{4,0},{6,2},{1,5},{3,7},{5,1},{7,3},{8,12},{10,14},{12... | collective-permute-start | bytes 786440 | tf_op jit(solution)/shard_map/ppermute | solution.py:27
  170.4 9.3 %collective-permute-start.14 = (bf16[2,256,256]{2,1,0:T(8,128)(2,1)S(1)}, bf16[2,256,256]{2,1,0:T(8,128)(2,1)S(1)}, u32[]{:S(2)}, u32[]{:S(2)}) collective-permute-start(bf16[2,256,256]{2,1,0:T(8,128)(2,1)S(1)} %copy_bitcast_fusion.1), channel_id=1, source_target_pairs={{0,2},{2,4},{4,6},{6,0},{1,3},{3,5},{5,7},{7,1},{8,10},{10,12},{12... | collective-permute-start | bytes 786440 | tf_op jit(solution)/shard_map/ppermute | solution.py:27
  179.8 2.7 %collective-permute-start.15 = (bf16[2,256,1024]{2,1,0:T(8,128)(2,1)S(1)}, bf16[2,256,1024]{2,1,0:T(8,128)(2,1)S(1)}, u32[]{:S(2)}, u32[]{:S(2)}) collective-permute-start(bf16[2,256,1024]{2,1,0:T(8,128)(2,1)S(1)} %constant_dynamic-update-slice_fusion.4), channel_id=1, source_target_pairs={{0,1},{1,0},{2,3},{3,2},{4,5},{5,4},{6,7},{7,6},{8,9},{9,8},{10,11... | collective-permute-start | bytes 3145736 | tf_op jit(solution)/shard_map/ppermute | solution.py:31
  184.1 3.0 %collective-permute-start.16 = (bf16[2,256,1024]{2,1,0:T(8,128)(2,1)S(1)}, bf16[2,256,1024]{2,1,0:T(8,128)(2,1)S(1)}, u32[]{:S(2)}, u32[]{:S(2)}) collective-permute-start(bf16[2,256,1024]{2,1,0:T(8,128)(2,1)S(1)} %convolution_convert_fusion.1), channel_id=1, source_target_pairs={{0,1},{1,0},{2,3},{3,2},{4,5},{5,4},{6,7},{7,6},{8,9},{9,8},{10,11... | collective-permute-start | bytes 3145736 | tf_op jit(solution)/shard_map/ppermute | solution.py:31
  187.6 38.7 %copy-start.11 = (f32[512,32]{1,0:T(8,128)S(1)}, f32[512,32]{1,0:T(8,128)}, u32[]{:S(2)}) copy-start(f32[512,32]{1,0:T(8,128)} %fusion.12) | copy-start | bytes 196612
  187.6 15.3 %collective-permute-start.17 = (bf16[2,256,256]{2,1,0:T(8,128)(2,1)S(1)}, bf16[2,256,256]{2,1,0:T(8,128)(2,1)S(1)}, u32[]{:S(2)}, u32[]{:S(2)}) collective-permute-start(bf16[2,256,256]{2,1,0:T(8,128)(2,1)S(1)} %get-tuple-element.103), channel_id=1, source_target_pairs={{0,2},{2,4},{4,6},{6,0},{1,3},{3,5},{5,7},{7,1},{8,10},{10,12},{12... | collective-permute-start | bytes 786440 | tf_op jit(solution)/shard_map/ppermute | solution.py:27
  189.5 13.3 %collective-permute-start.18 = (bf16[2,256,256]{2,1,0:T(8,128)(2,1)S(1)}, bf16[2,256,256]{2,1,0:T(8,128)(2,1)S(1)}, u32[]{:S(2)}, u32[]{:S(2)}) collective-permute-start(bf16[2,256,256]{2,1,0:T(8,128)(2,1)S(1)} %get-tuple-element.105), channel_id=1, source_target_pairs={{0,4},{2,6},{4,0},{6,2},{1,5},{3,7},{5,1},{7,3},{8,12},{10,14},{12... | collective-permute-start | bytes 786440 | tf_op jit(solution)/shard_map/ppermute | solution.py:27
  190.1 13.4 %collective-permute-start.19 = (bf16[2,256,256]{2,1,0:T(8,128)(2,1)S(1)}, bf16[2,256,256]{2,1,0:T(8,128)(2,1)S(1)}, u32[]{:S(2)}, u32[]{:S(2)}) collective-permute-start(bf16[2,256,256]{2,1,0:T(8,128)(2,1)S(1)} %get-tuple-element.104), channel_id=1, source_target_pairs={{0,6},{2,0},{4,2},{6,4},{1,7},{3,1},{5,3},{7,5},{8,14},{10,8},{12,... | collective-permute-start | bytes 786440 | tf_op jit(solution)/shard_map/ppermute | solution.py:27
  (15 other events, 98.3 us)
Sparse Core Ops, SparseCore 0:
  80.6 44.2 all-gather.1

commit v4 on v3

--- a/solution.py
+++ b/solution.py
@@ -190,7 +190,7 @@
             bytes_accessed=8 * rows * share * XN,
             transcendentals=0,
         ),
-        compiler_params=pltpu.CompilerParams(vmem_limit_bytes=32 * 1024 * 1024),
+        compiler_params=pltpu.CompilerParams(vmem_limit_bytes=16 * 1024 * 1024),
         name="near_gradient",
     )(score_grad, weight, far)
 
@@ -269,8 +269,6 @@
     normed_near = jnp.concatenate(normed_near, axis=1)
     normed_far = across_core(normed_near)
 
-    inputs = lax.all_gather(by_expert(inputs), ("x", "core"), axis=2, tiled=True)
-
     side = width // 2
     numbers = numbers[:, :3, :rows].astype(jnp.int32)
     code_all = numbers[:, 0] + 256 * numbers[:, 1] + 65536 * numbers[:, 2]
@@ -300,7 +298,9 @@
     along = jnp.pad(along.reshape(n_expert, 1, rows), ((0, 0), (0, 7), (0, 128 - rows)))
     along = jnp.sum(exchanged(along, ("y", "z")), axis=0)
     head_grad = head_gradient(order, normed_near, normed_far, score_grad)
-    sent, head_grad, along = lax.optimization_barrier((sent, head_grad, along))
+    inputs = by_expert(inputs)
+    sent, head_grad, along, inputs = lax.optimization_barrier((sent, head_grad, along, inputs))
+    inputs = lax.all_gather(inputs, ("x", "core"), axis=2, tiled=True)
     along = along + across_core(along)
     along = along + sum(along_x(along, k) for k in range(1, XN))
     kept = (kept + sum(a.astype(f32) for a in sent)).astype(bf16)
@@ -314,7 +314,6 @@
     routed = wide_dot(pick, residual_grad, ((1,), (0,)), lax.Precision.HIGHEST)
     routed = (slot_gate * routed).astype(bf16).reshape(n_expert, own_experts * capacity, share)
     routed = exchanged(routed, ("y", "z"))
-    routed, inputs = lax.optimization_barrier((routed, inputs))
     gate_pre = jnp.einsum("esd,edf->esf", inputs, w_gate, preferred_element_type=f32)
     up_pre = jnp.einsum("esd,edf->esf", inputs, w_up, preferred_element_type=f32)
     grads = in_ring_order(by_expert(routed), along_x, XN)

time: 237 us -> 224 us (0.945)
  waiting for transfers between devices: 81.1 us -> 56.2 us
  blocking collectives: 38.7 us -> 55.3 us
    all_to_all x1 -> x2, blocking collectives: 16.1 us -> 32.6 us  [exchanged(): return lax.all_to_all(a, axes, 0, 0, tiled=True)]
    ppermute x15, waiting for transfers between devices: 41.8 us -> 30 us  [along_x(): return lax.ppermute(a, 'x', [(p, (p + step) % XN) for p in range(XN)])]
    all_to_all x4 -> x3, waiting for transfers between devices: 27.7 us -> 16 us  [exchanged(): return lax.all_to_all(a, axes, 0, 0, tiled=True)]
    all_to_all x4 -> x3, starting transfers between devices: 31.4 us -> 25.2 us  [exchanged(): return lax.all_to_all(a, axes, 0, 0, tiled=True)]
    ppermute x15, starting transfers between devices: 18.6 us -> 23.7 us  [along_x(): return lax.ppermute(a, 'x', [(p, (p + step) % XN) for p in range(XN)])]
  transfers between devices with their start and end apart: 25 -> 24, of which waited for: 21 -> 15; matrix products, arithmetic and copies ran while one was open for 6% -> 7% of each run, Pallas kernels for 8% -> 8%
where the time goes in v4:
time: 224 us; the launch traced here: 223 us
  waiting for transfers between devices  56.2 us (25%)
  blocking collectives  55.3 us (25%)
  starting transfers between devices  50.1 us (22%)
  Pallas kernels  20.7 us (9%)
  between operations  14.6 us (7%)
  matrix products  12.5 us (6%)
  other arithmetic  8.36 us (4%)
  local copies, waits for them, and re-layouts  5.77 us (3%)
    all_to_all x2, blocking collectives, exchanged(): return lax.all_to_all(a, axes, 0, 0, tiled=True)  32.6 us
    ppermute x15, waiting for transfers between devices, along_x(): return lax.ppermute(a, 'x', [(p, (p + step) % XN) for p in range(XN)])  30 us
    all_to_all x3, starting transfers between devices, exchanged(): return lax.all_to_all(a, axes, 0, 0, tiled=True)  25.2 us
    ppermute x15, starting transfers between devices, along_x(): return lax.ppermute(a, 'x', [(p, (p + step) % XN) for p in range(XN)])  23.7 us
    all_to_all x1, blocking collectives, on_device(): returned = lax.all_to_all(near, ('y', 'z'), 0, 0, tiled=True)  22.7 us
    all_to_all x3, waiting for transfers between devices, exchanged(): return lax.all_to_all(a, axes, 0, 0, tiled=True)  16 us
    ppermute x5, waiting for transfers between devices, across_core(): return lax.ppermute(a, 'core', [(p, CN - 1 - p) for p in range(CN)])  10.1 us
    pallas_call x1, Pallas kernels, head_gradient(): pl.pallas_call(body, grid_spec=pltpu.PrefetchScalarGridSpec(num_scalar_pr...  9.04 us
  transfers between devices with their start and end apart: 24, of which 15 were waited for; matrix products, arithmetic and copies ran while one was open for 7% of the time, Pallas kernels for 8%

profile of v4, /device:TPU:32, one launch (start us, length us, event | category | flops | bytes accessed | tf_op | source)
XLA Modules:
  0.0 223.5 jit_solution(15824050667811233906)
XLA Ops:
  8.5 1.9 normed_to_spread.1
  10.4 11.4 %all-to-all-start = ((bf16[32,40,256]{2,1,0:T(8,128)(2,1)}), bf16[32,40,256]{2,1,0:T(8,128)(2,1)S(1)}, u32[]{:S(2)}, u32[]{:S(2)}) async-start(bf16[32,40,256]{2,1,0:T(8,128)(2,1)} %get-tuple-element.50), calls=%async_computation | async-start | bytes 1310720 | tf_op jit(solution)/shard_map/all_to_all | solution.py:35
  25.5 7.8 %turned_weights.1 = (bf16[1024,384]{1,0:T(8,128)(2,1)}, bf16[1024,384]{1,0:T(8,128)(2,1)}, bf16[2,2048,256]{2,1,0:T(8,128)(2,1)}, bf16[2,128,2048]{2,1,0:T(8,128)(2,1)}) custom-call(s32[8]{0:T(128)} %stack.55.order_ref, bf16[2048,384]{1,0:T(8,128)(2,1)} %head_ref.1, bf16[2,2048,128]{2,1,0:T(8,128)(2,1)} %gate_ref.1, bf16[2,2048,128]{2,1,0:T(8,128)(2,1)} %up_ref.1, ...), custom_call_target="tpu_custom_call" | custom-call | bytes 9437184 | tf_op jit(solution)/shard_map/turned_weights/pallas_call | solution.py:100
  33.7 8.4 %all-to-all-done = bf16[32,40,256]{2,1,0:T(8,128)(2,1)S(1)} async-done(((bf16[32,40,256]{2,1,0:T(8,128)(2,1)}), bf16[32,40,256]{2,1,0:T(8,128)(2,1)S(1)}, u32[]{:S(2)}, u32[]{:S(2)}) %all-to-all-start) | async-done | bytes 655392 | tf_op jit(solution)/shard_map/all_to_all | solution.py:35
  42.1 1.6 collective-permute-start.2
  43.7 2.7 %collective-permute-start.1 = (bf16[1024,256]{1,0:T(8,128)(2,1)S(1)}, bf16[1024,256]{1,0:T(8,128)(2,1)S(1)}, u32[]{:S(2)}, u32[]{:S(2)}) collective-permute-start(bf16[1024,256]{1,0:T(8,128)(2,1)S(1)} %bitcast.81), channel_id=1, source_target_pairs={{0,4},{2,6},{4,0},{6,2},{1,5},{3,7},{5,1},{7,3},{8,12},{10,14},{12... | collective-permute-start | bytes 1572872 | tf_op jit(solution)/shard_map/ppermute | solution.py:27
  47.9 16.0 %all_to_all.30 = bf16[32,16,256]{2,1,0:T(8,128)(2,1)S(1)} all-to-all(bf16[32,16,256]{2,1,0:T(8,128)(2,1)S(1)} %bitcast.85), channel_id=1, replica_groups=mesh['y'=4,'z'=8,'x'=4,'core'=2] {'y','z'}, dimensions={0} | all-to-all | bytes 524288 | tf_op jit(solution)/shard_map/all_to_all | solution.py:35
  63.9 3.1 %collective-permute-done.1 = bf16[1024,256]{1,0:T(8,128)(2,1)S(1)} collective-permute-done((bf16[1024,256]{1,0:T(8,128)(2,1)S(1)}, bf16[1024,256]{1,0:T(8,128)(2,1)S(1)}, u32[]{:S(2)}, u32[]{:S(2)}) %collective-permute-start.1) | collective-permute-done | bytes 524320 | tf_op jit(solution)/shard_map/ppermute | solution.py:27
  72.5 2.8 %fusion.42 = f32[1024,384]{1,0:T(8,128)S(1)} fusion(bf16[1024,1024]{1,0:T(8,128)(2,1)} %collective-permute-done.3.far_ref, bf16[1024,384]{1,0:T(8,128)(2,1)S(1)} %copy-done.16), kind=kOutput, calls=%fused_computation.104 | convolution fusion | flops 805306368 | bytes 4456448 | tf_op jit(solution)/shard_map/dot_general | solution.py:17
  77.8 3.8 %collective-permute-done.4.far_ref = bf16[1024,1024]{1,0:T(8,128)(2,1)S(1)} collective-permute-done((bf16[1024,1024]{1,0:T(8,128)(2,1)S(1)}, bf16[1024,1024]{1,0:T(8,128)(2,1)S(1)}, u32[]{:S(2)}, u32[]{:S(2)}) %collective-permute-start.4) | collective-permute-done | bytes 2097184 | tf_op jit(solution)/shard_map/ppermute | solution.py:31
  81.5 1.9 near_gradient.1
  84.8 2.5 %collective-permute-start.6 = (bf16[1024,256]{1,0:T(8,128)(2,1)}, bf16[1024,256]{1,0:T(8,128)(2,1)}, u32[]{:S(2)}, u32[]{:S(2)}) collective-permute-start(bf16[1024,256]{1,0:T(8,128)(2,1)} %get-tuple-element.72), channel_id=1, source_target_pairs={{0,4},{2,6},{4,0},{6,2},{1,5},{3,7},{5,1},{7,3},{8,12},{10,14},{12... | collective-permute-start | bytes 1572872 | tf_op jit(solution)/shard_map/ppermute | solution.py:27
  89.5 6.8 %all-to-all-start.2 = ((f32[32,8,128]{2,1,0:T(8,128)}), f32[32,8,128]{2,1,0:T(8,128)S(1)}, u32[]{:S(2)}, u32[]{:S(2)}) async-start(f32[32,8,128]{2,1,0:T(8,128)} %pad.9), calls=%async_computation.2 | async-start | bytes 262144 | tf_op jit(solution)/shard_map/all_to_all | solution.py:35
  97.1 9.0 %head_gradient.1 = f32[2048,384]{1,0:T(8,128)} custom-call(s32[8]{0:T(128)} %stack.55.order_ref, bf16[1024,1024]{1,0:T(8,128)(2,1)} %copy-done.6, bf16[1024,1024]{1,0:T(8,128)(2,1)} %collective-permute-done.3.far_ref, bf16[1024,384]{1,0:T(8,128)(2,1)} %copy-done.1), custom_call_target="tpu_custom_call" | custom-call | flops 1024 | bytes 1024 | tf_op jit(solution)/shard_map/head_gradient/pallas_call | solution.py:148
  106.2 4.8 %collective-permute-done.6 = bf16[1024,256]{1,0:T(8,128)(2,1)} collective-permute-done((bf16[1024,256]{1,0:T(8,128)(2,1)}, bf16[1024,256]{1,0:T(8,128)(2,1)}, u32[]{:S(2)}, u32[]{:S(2)}) %collective-permute-start.6) | collective-permute-done | bytes 524320 | tf_op jit(solution)/shard_map/ppermute | solution.py:27
  111.1 2.2 add_convert_fusion
  113.3 7.0 %all-to-all-start.3 = ((bf16[32,32,256]{2,1,0:T(8,128)(2,1)}), bf16[32,32,256]{2,1,0:T(8,128)(2,1)S(1)}, u32[]{:S(2)}, u32[]{:S(2)}) async-start(bf16[32,32,256]{2,1,0:T(8,128)(2,1)} %bitcast.23), calls=%async_computation.3 | async-start | bytes 1048576 | tf_op jit(solution)/shard_map/all_to_all | solution.py:35
  121.6 2.6 %collective-permute-start.11 = (f32[8,128]{1,0:T(8,128)S(1)}, f32[8,128]{1,0:T(8,128)S(1)}, u32[]{:S(2)}, u32[]{:S(2)}) collective-permute-start(f32[8,128]{1,0:T(8,128)S(1)} %add.261), channel_id=1, source_target_pairs={{0,6},{2,0},{4,2},{6,4},{1,7},{3,1},{5,3},{7,5},{8,14},{10,8},{12,... | collective-permute-start | bytes 12296 | tf_op jit(solution)/shard_map/ppermute | solution.py:27
  125.8 3.5 %collective-permute-done.10 = f32[8,128]{1,0:T(8,128)S(1)} collective-permute-done((f32[8,128]{1,0:T(8,128)S(1)}, f32[8,128]{1,0:T(8,128)S(1)}, u32[]{:S(2)}, u32[]{:S(2)}) %collective-permute-start.10) | collective-permute-done | bytes 4128 | tf_op jit(solution)/shard_map/ppermute | solution.py:27
  130.0 7.7 %all-to-all-done.3 = bf16[32,32,256]{2,1,0:T(8,128)(2,1)S(1)} async-done(((bf16[32,32,256]{2,1,0:T(8,128)(2,1)}), bf16[32,32,256]{2,1,0:T(8,128)(2,1)S(1)}, u32[]{:S(2)}, u32[]{:S(2)}) %all-to-all-start.3) | async-done | bytes 524320 | tf_op jit(solution)/shard_map/all_to_all | solution.py:35
  138.4 16.6 %all_to_all.31 = bf16[32,16,256]{2,1,0:T(8,128)(2,1)S(1)} all-to-all(bf16[32,16,256]{2,1,0:T(8,128)(2,1)S(1)} %bitcast.86), channel_id=1, replica_groups=mesh['y'=4,'z'=8,'x'=4,'core'=2] {'y','z'}, dimensions={0} | all-to-all | bytes 524288 | tf_op jit(solution)/shard_map/all_to_all | solution.py:35
  155.1 1.5 collective-permute-start.14
  156.6 3.0 %collective-permute-start.13 = (bf16[2,256,256]{2,1,0:T(8,128)(2,1)S(1)}, bf16[2,256,256]{2,1,0:T(8,128)(2,1)S(1)}, u32[]{:S(2)}, u32[]{:S(2)}) collective-permute-start(bf16[2,256,256]{2,1,0:T(8,128)(2,1)S(1)} %copy_bitcast_fusion.1), channel_id=1, source_target_pairs={{0,4},{2,6},{4,0},{6,2},{1,5},{3,7},{5,1},{7,3},{8,12},{10,14},{12... | collective-permute-start | bytes 786440 | tf_op jit(solution)/shard_map/ppermute | solution.py:27
  159.7 2.4 %fusion.44 = f32[2,256,128]{2,1,0:T(8,128)S(1)} fusion(bf16[2,256,2048]{2,1,0:T(8,128)(2,1)} %all-gather.2.cloned.1.call-done, bf16[2,2048,128]{2,1,0:T(8,128)(2,1)S(1)} %copy-done.4), kind=kOutput, calls=%fused_computation.106 | convolution fusion | flops 268435456 | bytes 3407872 | tf_op jit(solution)/shard_map/esd,edf->esf/dot_general | solution.py:318
  162.9 2.6 %collective-permute-done.14 = bf16[2,256,256]{2,1,0:T(8,128)(2,1)S(1)} collective-permute-done((bf16[2,256,256]{2,1,0:T(8,128)(2,1)S(1)}, bf16[2,256,256]{2,1,0:T(8,128)(2,1)S(1)}, u32[]{:S(2)}, u32[]{:S(2)}) %collective-permute-start.14) | collective-permute-done | bytes 262176 | tf_op jit(solution)/shard_map/ppermute | solution.py:27
  165.5 3.3 %collective-permute-done.13 = bf16[2,256,256]{2,1,0:T(8,128)(2,1)S(1)} collective-permute-done((bf16[2,256,256]{2,1,0:T(8,128)(2,1)S(1)}, bf16[2,256,256]{2,1,0:T(8,128)(2,1)S(1)}, u32[]{:S(2)}, u32[]{:S(2)}) %collective-permute-start.13) | collective-permute-done | bytes 262176 | tf_op jit(solution)/shard_map/ppermute | solution.py:27
  169.1 2.6 %collective-permute-done.15 = bf16[2,256,1024]{2,1,0:T(8,128)(2,1)S(1)} collective-permute-done((bf16[2,256,1024]{2,1,0:T(8,128)(2,1)S(1)}, bf16[2,256,1024]{2,1,0:T(8,128)(2,1)S(1)}, u32[]{:S(2)}, u32[]{:S(2)}) %collective-permute-start.15) | collective-permute-done | bytes 1048608 | tf_op jit(solution)/shard_map/ppermute | solution.py:31
  173.7 2.5 %collective-permute-done.16 = bf16[2,256,1024]{2,1,0:T(8,128)(2,1)S(1)} collective-permute-done((bf16[2,256,1024]{2,1,0:T(8,128)(2,1)S(1)}, bf16[2,256,1024]{2,1,0:T(8,128)(2,1)S(1)}, u32[]{:S(2)}, u32[]{:S(2)}) %collective-permute-start.16) | collective-permute-done | bytes 1048608 | tf_op jit(solution)/shard_map/ppermute | solution.py:31
  177.7 2.4 %collective-permute-start.19 = (bf16[2,256,256]{2,1,0:T(8,128)(2,1)S(1)}, bf16[2,256,256]{2,1,0:T(8,128)(2,1)S(1)}, u32[]{:S(2)}, u32[]{:S(2)}) collective-permute-start(bf16[2,256,256]{2,1,0:T(8,128)(2,1)S(1)} %get-tuple-element.102), channel_id=1, source_target_pairs={{0,6},{2,0},{4,2},{6,4},{1,7},{3,1},{5,3},{7,5},{8,14},{10,8},{12,... | collective-permute-start | bytes 786440 | tf_op jit(solution)/shard_map/ppermute | solution.py:27
  180.6 6.0 %collective-permute-done.17 = bf16[2,256,256]{2,1,0:T(8,128)(2,1)S(1)} collective-permute-done((bf16[2,256,256]{2,1,0:T(8,128)(2,1)S(1)}, bf16[2,256,256]{2,1,0:T(8,128)(2,1)S(1)}, u32[]{:S(2)}, u32[]{:S(2)}) %collective-permute-start.17) | collective-permute-done | bytes 262176 | tf_op jit(solution)/shard_map/ppermute | solution.py:27
  186.6 4.7 %collective-permute-done.19 = bf16[2,256,256]{2,1,0:T(8,128)(2,1)S(1)} collective-permute-done((bf16[2,256,256]{2,1,0:T(8,128)(2,1)S(1)}, bf16[2,256,256]{2,1,0:T(8,128)(2,1)S(1)}, u32[]{:S(2)}, u32[]{:S(2)}) %collective-permute-start.19) | collective-permute-done | bytes 262176 | tf_op jit(solution)/shard_map/ppermute | solution.py:27
  192.7 22.7 %all_to_all.32 = f32[32,16,256]{2,1,0:T(8,128)S(1)} all-to-all(f32[32,16,256]{2,1,0:T(8,128)S(1)} %copy_bitcast_fusion), channel_id=1, replica_groups=mesh['y'=4,'z'=8,'x'=4,'core'=2] {'y','z'}, dimensions={0} | all-to-all | bytes 1048576 | tf_op jit(solution)/shard_map/all_to_all | solution.py:346
  (116 shorter events, 30.9 us)
Async XLA Ops:
  7.2 26.3 %copy-start = (bf16[32,2048]{1,0:T(8,128)(2,1)S(1)}, bf16[32,2048]{1,0:T(8,128)(2,1)}, u32[]{:S(2)}) copy-start(bf16[32,2048]{1,0:T(8,128)(2,1)} %param.13) | copy-start | bytes 393220
  10.4 31.6 %all-to-all-start = ((bf16[32,40,256]{2,1,0:T(8,128)(2,1)}), bf16[32,40,256]{2,1,0:T(8,128)(2,1)S(1)}, u32[]{:S(2)}, u32[]{:S(2)}) async-start(bf16[32,40,256]{2,1,0:T(8,128)(2,1)} %get-tuple-element.50), calls=%async_computation | async-start | bytes 1310720 | tf_op jit(solution)/shard_map/all_to_all | solution.py:35
  42.1 21.7 %collective-permute-start.2 = (bf16[1024,256]{1,0:T(8,128)(2,1)S(1)}, bf16[1024,256]{1,0:T(8,128)(2,1)S(1)}, u32[]{:S(2)}, u32[]{:S(2)}) collective-permute-start(bf16[1024,256]{1,0:T(8,128)(2,1)S(1)} %bitcast.80), channel_id=1, source_target_pairs={{0,2},{2,4},{4,6},{6,0},{1,3},{3,5},{5,7},{7,1},{8,10},{10,12},{12... | collective-permute-start | bytes 1572872 | tf_op jit(solution)/shard_map/ppermute | solution.py:27
  43.7 23.3 %collective-permute-start.1 = (bf16[1024,256]{1,0:T(8,128)(2,1)S(1)}, bf16[1024,256]{1,0:T(8,128)(2,1)S(1)}, u32[]{:S(2)}, u32[]{:S(2)}) collective-permute-start(bf16[1024,256]{1,0:T(8,128)(2,1)S(1)} %bitcast.81), channel_id=1, source_target_pairs={{0,4},{2,6},{4,0},{6,2},{1,5},{3,7},{5,1},{7,3},{8,12},{10,14},{12... | collective-permute-start | bytes 1572872 | tf_op jit(solution)/shard_map/ppermute | solution.py:27
  46.4 20.5 %collective-permute-start = (bf16[1024,256]{1,0:T(8,128)(2,1)S(1)}, bf16[1024,256]{1,0:T(8,128)(2,1)S(1)}, u32[]{:S(2)}, u32[]{:S(2)}) collective-permute-start(bf16[1024,256]{1,0:T(8,128)(2,1)S(1)} %bitcast.82), channel_id=1, source_target_pairs={{0,6},{2,0},{4,2},{6,4},{1,7},{3,1},{5,3},{7,5},{8,14},{10,8},{12,... | collective-permute-start | bytes 1572872 | tf_op jit(solution)/shard_map/ppermute | solution.py:27
  67.3 5.1 %collective-permute-start.3 = (bf16[1024,1024]{1,0:T(8,128)(2,1)S(1)}, bf16[1024,1024]{1,0:T(8,128)(2,1)}, u32[]{:S(2)}, u32[]{:S(2)}) collective-permute-start(bf16[1024,1024]{1,0:T(8,128)(2,1)S(1)} %constant_dynamic-update-slice_fusion.near_ref), channel_id=1, source_target_pairs={{0,1},{1,0},{2,3},{3,2},{4,5},{5,4},{6,7},{7,6},{8,9},{9,8},{10,11... | collective-permute-start | bytes 6291464 | tf_op jit(solution)/shard_map/ppermute | solution.py:31
  77.3 4.2 %collective-permute-start.4 = (bf16[1024,1024]{1,0:T(8,128)(2,1)S(1)}, bf16[1024,1024]{1,0:T(8,128)(2,1)S(1)}, u32[]{:S(2)}, u32[]{:S(2)}) collective-permute-start(bf16[1024,1024]{1,0:T(8,128)(2,1)S(1)} %convolution_convert_fusion), channel_id=1, source_target_pairs={{0,1},{1,0},{2,3},{3,2},{4,5},{5,4},{6,7},{7,6},{8,9},{9,8},{10,11... | collective-permute-start | bytes 6291464 | tf_op jit(solution)/shard_map/ppermute | solution.py:31
  83.5 22.8 %collective-permute-start.5 = (bf16[1024,256]{1,0:T(8,128)(2,1)}, bf16[1024,256]{1,0:T(8,128)(2,1)S(1)}, u32[]{:S(2)}, u32[]{:S(2)}) collective-permute-start(bf16[1024,256]{1,0:T(8,128)(2,1)} %get-tuple-element.71), channel_id=1, source_target_pairs={{0,2},{2,4},{4,6},{6,0},{1,3},{3,5},{5,7},{7,1},{8,10},{10,12},{12... | collective-permute-start | bytes 1572872 | tf_op jit(solution)/shard_map/ppermute | solution.py:27
  84.8 26.2 %collective-permute-start.6 = (bf16[1024,256]{1,0:T(8,128)(2,1)}, bf16[1024,256]{1,0:T(8,128)(2,1)}, u32[]{:S(2)}, u32[]{:S(2)}) collective-permute-start(bf16[1024,256]{1,0:T(8,128)(2,1)} %get-tuple-element.72), channel_id=1, source_target_pairs={{0,4},{2,6},{4,0},{6,2},{1,5},{3,7},{5,1},{7,3},{8,12},{10,14},{12... | collective-permute-start | bytes 1572872 | tf_op jit(solution)/shard_map/ppermute | solution.py:27
  87.3 23.7 %collective-permute-start.7 = (bf16[1024,256]{1,0:T(8,128)(2,1)S(1)}, bf16[1024,256]{1,0:T(8,128)(2,1)}, u32[]{:S(2)}, u32[]{:S(2)}) collective-permute-start(bf16[1024,256]{1,0:T(8,128)(2,1)S(1)} %get-tuple-element.73), channel_id=1, source_target_pairs={{0,6},{2,0},{4,2},{6,4},{1,7},{3,1},{5,3},{7,5},{8,14},{10,8},{12,... | collective-permute-start | bytes 1572872 | tf_op jit(solution)/shard_map/ppermute | solution.py:27
  89.5 16.7 %all-to-all-start.2 = ((f32[32,8,128]{2,1,0:T(8,128)}), f32[32,8,128]{2,1,0:T(8,128)S(1)}, u32[]{:S(2)}, u32[]{:S(2)}) async-start(f32[32,8,128]{2,1,0:T(8,128)} %pad.9), calls=%async_computation.2 | async-start | bytes 262144 | tf_op jit(solution)/shard_map/all_to_all | solution.py:35
  96.4 63.4 %all-gather.2.cloned.1.call-start = ((), (), s32[]{:S(2)}) async-start(), calls=%async_computation.6 | async-start | bytes 2359296 | tf_op jit(solution)/shard_map/all_gather | solution.py:303
  111.1 14.6 %copy-start.12 = (f32[32,1]{1,0:T(8,128)S(1)}, f32[32,1]{1,0:T(8,128)}, u32[]{:S(2)}) copy-start(f32[32,1]{1,0:T(8,128)} %get-tuple-element.85) | copy-start | bytes 388
  111.1 26.7 %copy-start.11 = (f32[32,256]{1,0:T(8,128)S(1)}, f32[32,256]{1,0:T(8,128)}, u32[]{:S(2)}) copy-start(f32[32,256]{1,0:T(8,128)} %get-tuple-element.83) | copy-start | bytes 98308
  111.1 26.7 %copy-start.15 = (f32[1,256]{1,0:T(1,128)S(1)}, f32[1,256]{1,0:T(1,128)}, u32[]{:S(2)}) copy-start(f32[1,256]{1,0:T(1,128)} %get-tuple-element.78) | copy-start | bytes 3076
  111.1 26.8 %copy-start.13 = (f32[512,1]{0,1:T(1,128)S(1)}, f32[512,1]{0,1:T(1,128)}, u32[]{:S(2)}) copy-start(f32[512,1]{0,1:T(1,128)} %reshape.201) | copy-start | bytes 6148
  113.3 46.4 %copy-start.4 = (bf16[2,2048,128]{2,1,0:T(8,128)(2,1)S(1)}, bf16[2,2048,128]{2,1,0:T(8,128)(2,1)}, u32[]{:S(2)}) copy-start(bf16[2,2048,128]{2,1,0:T(8,128)(2,1)} %up_ref.1) | copy-start | bytes 3145732
  113.3 24.3 %all-to-all-start.3 = ((bf16[32,32,256]{2,1,0:T(8,128)(2,1)}), bf16[32,32,256]{2,1,0:T(8,128)(2,1)S(1)}, u32[]{:S(2)}, u32[]{:S(2)}) async-start(bf16[32,32,256]{2,1,0:T(8,128)(2,1)} %bitcast.23), calls=%async_computation.3 | async-start | bytes 1048576 | tf_op jit(solution)/shard_map/all_to_all | solution.py:35
  120.3 1.3 collective-permute-start.8
  121.6 4.2 %collective-permute-start.11 = (f32[8,128]{1,0:T(8,128)S(1)}, f32[8,128]{1,0:T(8,128)S(1)}, u32[]{:S(2)}, u32[]{:S(2)}) collective-permute-start(f32[8,128]{1,0:T(8,128)S(1)} %add.261), channel_id=1, source_target_pairs={{0,6},{2,0},{4,2},{6,4},{1,7},{3,1},{5,3},{7,5},{8,14},{10,8},{12,... | collective-permute-start | bytes 12296 | tf_op jit(solution)/shard_map/ppermute | solution.py:27
  124.2 5.1 %collective-permute-start.10 = (f32[8,128]{1,0:T(8,128)S(1)}, f32[8,128]{1,0:T(8,128)S(1)}, u32[]{:S(2)}, u32[]{:S(2)}) collective-permute-start(f32[8,128]{1,0:T(8,128)S(1)} %add.261), channel_id=1, source_target_pairs={{0,4},{2,6},{4,0},{6,2},{1,5},{3,7},{5,1},{7,3},{8,12},{10,14},{12... | collective-permute-start | bytes 12296 | tf_op jit(solution)/shard_map/ppermute | solution.py:27
  125.1 4.8 %collective-permute-start.9 = (f32[8,128]{1,0:T(8,128)S(1)}, f32[8,128]{1,0:T(8,128)S(1)}, u32[]{:S(2)}, u32[]{:S(2)}) collective-permute-start(f32[8,128]{1,0:T(8,128)S(1)} %add.261), channel_id=1, source_target_pairs={{0,2},{2,4},{4,6},{6,0},{1,3},{3,5},{5,7},{7,1},{8,10},{10,12},{12... | collective-permute-start | bytes 12296 | tf_op jit(solution)/shard_map/ppermute | solution.py:27
  137.8 18.7 %copy-start.10 = (f32[32,256]{1,0:T(8,128)}, f32[32,256]{1,0:T(8,128)S(1)}, u32[]{:S(2)}) copy-start(f32[32,256]{1,0:T(8,128)S(1)} %subtract_divide_fusion) | copy-start | bytes 98308
  138.4 23.8 %copy-start.5 = (bf16[2,2048,128]{2,1,0:T(8,128)(2,1)S(1)}, bf16[2,2048,128]{2,1,0:T(8,128)(2,1)}, u32[]{:S(2)}) copy-start(bf16[2,2048,128]{2,1,0:T(8,128)(2,1)} %gate_ref.1) | copy-start | bytes 3145732
  155.1 10.5 %collective-permute-start.14 = (bf16[2,256,256]{2,1,0:T(8,128)(2,1)S(1)}, bf16[2,256,256]{2,1,0:T(8,128)(2,1)S(1)}, u32[]{:S(2)}, u32[]{:S(2)}) collective-permute-start(bf16[2,256,256]{2,1,0:T(8,128)(2,1)S(1)} %copy_bitcast_fusion.1), channel_id=1, source_target_pairs={{0,2},{2,4},{4,6},{6,0},{1,3},{3,5},{5,7},{7,1},{8,10},{10,12},{12... | collective-permute-start | bytes 786440 | tf_op jit(solution)/shard_map/ppermute | solution.py:27
  156.6 12.3 %collective-permute-start.13 = (bf16[2,256,256]{2,1,0:T(8,128)(2,1)S(1)}, bf16[2,256,256]{2,1,0:T(8,128)(2,1)S(1)}, u32[]{:S(2)}, u32[]{:S(2)}) collective-permute-start(bf16[2,256,256]{2,1,0:T(8,128)(2,1)S(1)} %copy_bitcast_fusion.1), channel_id=1, source_target_pairs={{0,4},{2,6},{4,0},{6,2},{1,5},{3,7},{5,1},{7,3},{8,12},{10,14},{12... | collective-permute-start | bytes 786440 | tf_op jit(solution)/shard_map/ppermute | solution.py:27
  159.5 9.3 %collective-permute-start.12 = (bf16[2,256,256]{2,1,0:T(8,128)(2,1)S(1)}, bf16[2,256,256]{2,1,0:T(8,128)(2,1)S(1)}, u32[]{:S(2)}, u32[]{:S(2)}) collective-permute-start(bf16[2,256,256]{2,1,0:T(8,128)(2,1)S(1)} %copy_bitcast_fusion.1), channel_id=1, source_target_pairs={{0,6},{2,0},{4,2},{6,4},{1,7},{3,1},{5,3},{7,5},{8,14},{10,8},{12,... | collective-permute-start | bytes 786440 | tf_op jit(solution)/shard_map/ppermute | solution.py:27
  169.0 2.7 %collective-permute-start.15 = (bf16[2,256,1024]{2,1,0:T(8,128)(2,1)S(1)}, bf16[2,256,1024]{2,1,0:T(8,128)(2,1)S(1)}, u32[]{:S(2)}, u32[]{:S(2)}) collective-permute-start(bf16[2,256,1024]{2,1,0:T(8,128)(2,1)S(1)} %constant_dynamic-update-slice_fusion.4), channel_id=1, source_target_pairs={{0,1},{1,0},{2,3},{3,2},{4,5},{5,4},{6,7},{7,6},{8,9},{9,8},{10,11... | collective-permute-start | bytes 3145736 | tf_op jit(solution)/shard_map/ppermute | solution.py:31
  173.2 3.0 %collective-permute-start.16 = (bf16[2,256,1024]{2,1,0:T(8,128)(2,1)S(1)}, bf16[2,256,1024]{2,1,0:T(8,128)(2,1)S(1)}, u32[]{:S(2)}, u32[]{:S(2)}) collective-permute-start(bf16[2,256,1024]{2,1,0:T(8,128)(2,1)S(1)} %convolution_convert_fusion.1), channel_id=1, source_target_pairs={{0,1},{1,0},{2,3},{3,2},{4,5},{5,4},{6,7},{7,6},{8,9},{9,8},{10,11... | collective-permute-start | bytes 3145736 | tf_op jit(solution)/shard_map/ppermute | solution.py:31
  176.7 9.9 %collective-permute-start.17 = (bf16[2,256,256]{2,1,0:T(8,128)(2,1)S(1)}, bf16[2,256,256]{2,1,0:T(8,128)(2,1)S(1)}, u32[]{:S(2)}, u32[]{:S(2)}) collective-permute-start(bf16[2,256,256]{2,1,0:T(8,128)(2,1)S(1)} %get-tuple-element.101), channel_id=1, source_target_pairs={{0,2},{2,4},{4,6},{6,0},{1,3},{3,5},{5,7},{7,1},{8,10},{10,12},{12... | collective-permute-start | bytes 786440 | tf_op jit(solution)/shard_map/ppermute | solution.py:27
  177.7 13.6 %collective-permute-start.19 = (bf16[2,256,256]{2,1,0:T(8,128)(2,1)S(1)}, bf16[2,256,256]{2,1,0:T(8,128)(2,1)S(1)}, u32[]{:S(2)}, u32[]{:S(2)}) collective-permute-start(bf16[2,256,256]{2,1,0:T(8,128)(2,1)S(1)} %get-tuple-element.102), channel_id=1, source_target_pairs={{0,6},{2,0},{4,2},{6,4},{1,7},{3,1},{5,3},{7,5},{8,14},{10,8},{12,... | collective-permute-start | bytes 786440 | tf_op jit(solution)/shard_map/ppermute | solution.py:27
  180.0 12.5 %collective-permute-start.18 = (bf16[2,256,256]{2,1,0:T(8,128)(2,1)S(1)}, bf16[2,256,256]{2,1,0:T(8,128)(2,1)S(1)}, u32[]{:S(2)}, u32[]{:S(2)}) collective-permute-start(bf16[2,256,256]{2,1,0:T(8,128)(2,1)S(1)} %get-tuple-element.103), channel_id=1, source_target_pairs={{0,4},{2,6},{4,0},{6,2},{1,5},{3,7},{5,1},{7,3},{8,12},{10,14},{12... | collective-permute-start | bytes 786440 | tf_op jit(solution)/shard_map/ppermute | solution.py:27
  (9 other events, 45.6 us)
Sparse Core Ops, SparseCore 0:
  111.2 27.4 all-gather.1

commit v5 on v4

--- a/solution.py
+++ b/solution.py
@@ -39,11 +39,19 @@
     return [a] + [move(a, ring - k) for k in range(1, ring)]
 
 
-def normed_to_spread(at, layer_out, final_gain, digits, copies):
+def normed_to_spread(
+    at, layer_out, final_gain, clean_ids, levels, level_count, copies, share
+):
     rows, width = layer_out.shape
-    below, share = digits.shape
-
-    def body(at_ref, rows_ref, gain_ref, digits_ref, spread_out, unit_out, scale_out, gain_out):
+    below = 8
+
+    def body(
+        at_ref, rows_ref, gain_ref, clean_ref, level_ref, spread_out, unit_out, scale_out, gain_out
+    ):
+        code = jnp.broadcast_to(clean_ref[...] * level_count + level_ref[...], (below, rows))
+        line = lax.broadcasted_iota(jnp.int32, (below, rows), 0)
+        digits = jnp.where(line == 0, code, jnp.where(line == 1, code >> 8, code >> 16)) & 255
+        digits = digits.astype(f32).astype(bf16)
         low = pl.multiple_of(at_ref[0] * share, share)
         values = rows_ref[...].astype(f32)
         mean = jnp.sum(values * values, axis=1, keepdims=True) / width
@@ -53,7 +61,8 @@
         normed = (unit * gain).astype(bf16)
         for k in range(copies):
             spread_out[k, :rows, :] = normed
-            spread_out[k, rows:, :] = digits_ref[...]
+            spread_out[k, rows:, :] = jnp.zeros((below, share), bf16)
+            spread_out[k, rows:, :rows] = digits
         unit_out[...] = unit
         scale_out[...] = scale
         gain_out[...] = gain
@@ -61,7 +70,7 @@
     whole = pl.BlockSpec(memory_space=pltpu.VMEM)
     return pl.pallas_call(
         body,
-        in_specs=[pl.BlockSpec(memory_space=pltpu.SMEM)] + [whole] * 3,
+        in_specs=[pl.BlockSpec(memory_space=pltpu.SMEM)] + [whole] * 4,
         out_specs=[whole] * 4,
         out_shape=[
             jax.ShapeDtypeStruct((copies, rows + below, share), bf16),
@@ -70,7 +79,7 @@
             jax.ShapeDtypeStruct((1, share), f32),
         ],
         name="normed_to_spread",
-    )(at[None], layer_out, final_gain[None, :], digits)
+    )(at[None], layer_out, final_gain[None, :], clean_ids[None, :], levels[None, :])
 
 
 def turned_weights(order, head_weight, w_gate, w_up, w_down):
@@ -229,11 +238,8 @@
         order, head_weight, w_gate, w_up, w_down
     )
 
-    code = clean_ids * ratio_table.shape[0] + levels
-    digits = jnp.stack([code % 256, code // 256 % 256, code // 65536]).astype(bf16)
-    digits = jnp.pad(digits, ((0, 8 - digits.shape[0]), (0, share - rows)))
     spread, unit_share, row_scale, gain_share = normed_to_spread(
-        v_at, layer_out, final_gain, digits, n_expert
+        v_at, layer_out, final_gain, clean_ids, levels, ratio_table.shape[0], n_expert, share
     )
 
     labels = jnp.arange(experts, dtype=jnp.int32)
@@ -323,7 +329,9 @@
 
     act_grad = jnp.einsum(
         "esd,efd->esf", grads, down_turned[:, :, :side], preferred_element_type=f32
-    ) + jnp.einsum(
+    )
+    act_grad, grads_far = lax.optimization_barrier((act_grad, grads_far))
+    act_grad = act_grad + jnp.einsum(
         "esd,efd->esf", grads_far, down_turned[:, :, side:], preferred_element_type=f32
     )
     sigmoid_gate = jax.nn.sigmoid(gate_pre)
@@ -336,6 +344,7 @@
     far = jnp.einsum("esf,edf->esd", pair_grad, pair_turned[:, side:], preferred_element_type=f32)
     far = across_core(far.astype(bf16))
     near = jnp.einsum("esf,edf->esd", pair_grad, pair_turned[:, :side], preferred_element_type=f32)
+    near, far = lax.optimization_barrier((near, far))
     near = near + far.astype(f32)
     near = near[:, :, :share] + sum(
         along_x(near[:, :, k * share:(k + 1) * share].astype(bf16), k).astype(f32)

time: 224 us -> 223 us (level)
  transfers between devices with their start and end apart: 24 -> 24, of which waited for: 15 -> 16; matrix products, arithmetic and copies ran while one was open for 7% -> 8% of each run, Pallas kernels for 8% -> 8%
where the time goes in v5:
time: 223 us; the launch traced here: 222 us
  blocking collectives  55.4 us (25%)
  waiting for transfers between devices  55.2 us (25%)
  starting transfers between devices  49.9 us (22%)
  Pallas kernels  20.7 us (9%)
  between operations  14.6 us (7%)
  matrix products  12.6 us (6%)
  other arithmetic  7.63 us (3%)
  local copies, waits for them, and re-layouts  5.78 us (3%)
    all_to_all x2, blocking collectives, exchanged(): return lax.all_to_all(a, axes, 0, 0, tiled=True)  32.5 us
    ppermute x15, waiting for transfers between devices, along_x(): return lax.ppermute(a, 'x', [(p, (p + step) % XN) for p in range(XN)])  29.9 us
    all_to_all x3, starting transfers between devices, exchanged(): return lax.all_to_all(a, axes, 0, 0, tiled=True)  25.2 us
    ppermute x15, starting transfers between devices, along_x(): return lax.ppermute(a, 'x', [(p, (p + step) % XN) for p in range(XN)])  23.6 us
    all_to_all x1, blocking collectives, on_device(): returned = lax.all_to_all(near, ('y', 'z'), 0, 0, tiled=True)  22.9 us
    all_to_all x3, waiting for transfers between devices, exchanged(): return lax.all_to_all(a, axes, 0, 0, tiled=True)  16 us
    ppermute x5, waiting for transfers between devices, across_core(): return lax.ppermute(a, 'core', [(p, CN - 1 - p) for p in range(CN)])  9.2 us
    pallas_call x1, Pallas kernels, head_gradient(): pl.pallas_call(body, grid_spec=pltpu.PrefetchScalarGridSpec(num_scalar_pr...  9.04 us
  transfers between devices with their start and end apart: 24, of which 16 were waited for; matrix products, arithmetic and copies ran while one was open for 8% of the time, Pallas kernels for 8%

profile of v5, /device:TPU:32, one launch (start us, length us, event | category | flops | bytes accessed | tf_op | source)
XLA Modules:
  0.0 221.8 jit_solution(11071215352482741253)
XLA Ops:
  7.2 2.0 normed_to_spread.1
  9.2 11.4 %all-to-all-start = ((bf16[32,40,256]{2,1,0:T(8,128)(2,1)}), bf16[32,40,256]{2,1,0:T(8,128)(2,1)S(1)}, u32[]{:S(2)}, u32[]{:S(2)}) async-start(bf16[32,40,256]{2,1,0:T(8,128)(2,1)} %get-tuple-element.54), calls=%async_computation | async-start | bytes 1310720 | tf_op jit(solution)/shard_map/all_to_all | solution.py:35
  24.2 7.8 %turned_weights.1 = (bf16[1024,384]{1,0:T(8,128)(2,1)}, bf16[1024,384]{1,0:T(8,128)(2,1)}, bf16[2,2048,256]{2,1,0:T(8,128)(2,1)}, bf16[2,128,2048]{2,1,0:T(8,128)(2,1)}) custom-call(s32[8]{0:T(128)} %stack.35.order_ref, bf16[2048,384]{1,0:T(8,128)(2,1)} %head_ref.1, bf16[2,2048,128]{2,1,0:T(8,128)(2,1)} %gate_ref.1, bf16[2,2048,128]{2,1,0:T(8,128)(2,1)} %up_ref.1, ...), custom_call_target="tpu_custom_call" | custom-call | bytes 9437184 | tf_op jit(solution)/shard_map/turned_weights/pallas_call | solution.py:109
  32.4 8.4 %all-to-all-done = bf16[32,40,256]{2,1,0:T(8,128)(2,1)S(1)} async-done(((bf16[32,40,256]{2,1,0:T(8,128)(2,1)}), bf16[32,40,256]{2,1,0:T(8,128)(2,1)S(1)}, u32[]{:S(2)}, u32[]{:S(2)}) %all-to-all-start) | async-done | bytes 655392 | tf_op jit(solution)/shard_map/all_to_all | solution.py:35
  40.9 1.6 collective-permute-start.2
  42.4 2.7 %collective-permute-start.1 = (bf16[1024,256]{1,0:T(8,128)(2,1)S(1)}, bf16[1024,256]{1,0:T(8,128)(2,1)S(1)}, u32[]{:S(2)}, u32[]{:S(2)}) collective-permute-start(bf16[1024,256]{1,0:T(8,128)(2,1)S(1)} %bitcast.77), channel_id=1, source_target_pairs={{0,4},{2,6},{4,0},{6,2},{1,5},{3,7},{5,1},{7,3},{8,12},{10,14},{12... | collective-permute-start | bytes 1572872 | tf_op jit(solution)/shard_map/ppermute | solution.py:27
  46.6 16.0 %all_to_all.30 = bf16[32,16,256]{2,1,0:T(8,128)(2,1)S(1)} all-to-all(bf16[32,16,256]{2,1,0:T(8,128)(2,1)S(1)} %bitcast.81), channel_id=1, replica_groups=mesh['y'=4,'z'=8,'x'=4,'core'=2] {'y','z'}, dimensions={0} | all-to-all | bytes 524288 | tf_op jit(solution)/shard_map/all_to_all | solution.py:35
  62.6 3.1 %collective-permute-done.1 = bf16[1024,256]{1,0:T(8,128)(2,1)S(1)} collective-permute-done((bf16[1024,256]{1,0:T(8,128)(2,1)S(1)}, bf16[1024,256]{1,0:T(8,128)(2,1)S(1)}, u32[]{:S(2)}, u32[]{:S(2)}) %collective-permute-start.1) | collective-permute-done | bytes 524320 | tf_op jit(solution)/shard_map/ppermute | solution.py:27
  71.2 2.8 %fusion.27 = f32[1024,384]{1,0:T(8,128)S(1)} fusion(bf16[1024,1024]{1,0:T(8,128)(2,1)} %collective-permute-done.3.far_ref, bf16[1024,384]{1,0:T(8,128)(2,1)S(1)} %copy-done.16), kind=kOutput, calls=%fused_computation.74 | convolution fusion | flops 805306368 | bytes 4456448 | tf_op jit(solution)/shard_map/dot_general | solution.py:17
  76.5 3.8 %collective-permute-done.4.far_ref = bf16[1024,1024]{1,0:T(8,128)(2,1)S(1)} collective-permute-done((bf16[1024,1024]{1,0:T(8,128)(2,1)S(1)}, bf16[1024,1024]{1,0:T(8,128)(2,1)S(1)}, u32[]{:S(2)}, u32[]{:S(2)}) %collective-permute-start.4) | collective-permute-done | bytes 2097184 | tf_op jit(solution)/shard_map/ppermute | solution.py:31
  80.3 1.9 near_gradient.1
  83.5 2.4 %collective-permute-start.6 = (bf16[1024,256]{1,0:T(8,128)(2,1)}, bf16[1024,256]{1,0:T(8,128)(2,1)}, u32[]{:S(2)}, u32[]{:S(2)}) collective-permute-start(bf16[1024,256]{1,0:T(8,128)(2,1)} %get-tuple-element.76), channel_id=1, source_target_pairs={{0,4},{2,6},{4,0},{6,2},{1,5},{3,7},{5,1},{7,3},{8,12},{10,14},{12... | collective-permute-start | bytes 1572872 | tf_op jit(solution)/shard_map/ppermute | solution.py:27
  86.0 1.5 collective-permute-start.7
  88.2 6.8 %all-to-all-start.2 = ((f32[32,8,128]{2,1,0:T(8,128)}), f32[32,8,128]{2,1,0:T(8,128)S(1)}, u32[]{:S(2)}, u32[]{:S(2)}) async-start(f32[32,8,128]{2,1,0:T(8,128)} %pad.4), calls=%async_computation.2 | async-start | bytes 262144 | tf_op jit(solution)/shard_map/all_to_all | solution.py:35
  95.9 9.0 %head_gradient.1 = f32[2048,384]{1,0:T(8,128)} custom-call(s32[8]{0:T(128)} %stack.35.order_ref, bf16[1024,1024]{1,0:T(8,128)(2,1)} %copy-done.6, bf16[1024,1024]{1,0:T(8,128)(2,1)} %collective-permute-done.3.far_ref, bf16[1024,384]{1,0:T(8,128)(2,1)} %copy-done.1), custom_call_target="tpu_custom_call" | custom-call | flops 1024 | bytes 1024 | tf_op jit(solution)/shard_map/head_gradient/pallas_call | solution.py:157
  105.0 4.7 %collective-permute-done.6 = bf16[1024,256]{1,0:T(8,128)(2,1)} collective-permute-done((bf16[1024,256]{1,0:T(8,128)(2,1)}, bf16[1024,256]{1,0:T(8,128)(2,1)}, u32[]{:S(2)}, u32[]{:S(2)}) %collective-permute-start.6) | collective-permute-done | bytes 524320 | tf_op jit(solution)/shard_map/ppermute | solution.py:27
  109.8 2.2 %add_convert_fusion = bf16[1024,256]{1,0:T(8,128)(2,1)} fusion(f32[1024,256]{1,0:T(8,128)S(1)} %get-tuple-element.83, bf16[1024,256]{1,0:T(8,128)(2,1)} %collective-permute-done.7, bf16[1024,256]{1,0:T(8,128)(2,1)} %collective-permute-done.6, bf16[1024,256]{1,0:T(8,128)(2,1)S(1)} %collective-permute-done.5), kind=kLoop, calls=%fused_computation.12 | loop fusion | flops 1835008 | bytes 3145728 | tf_op jit(solution)/shard_map/convert_element_type | solution.py:312
  112.1 7.0 %all-to-all-start.3 = ((bf16[32,32,256]{2,1,0:T(8,128)(2,1)}), bf16[32,32,256]{2,1,0:T(8,128)(2,1)S(1)}, u32[]{:S(2)}, u32[]{:S(2)}) async-start(bf16[32,32,256]{2,1,0:T(8,128)(2,1)} %bitcast.22), calls=%async_computation.3 | async-start | bytes 1048576 | tf_op jit(solution)/shard_map/all_to_all | solution.py:35
  120.3 2.6 %collective-permute-start.11 = (f32[8,128]{1,0:T(8,128)S(1)}, f32[8,128]{1,0:T(8,128)S(1)}, u32[]{:S(2)}, u32[]{:S(2)}) collective-permute-start(f32[8,128]{1,0:T(8,128)S(1)} %add.241), channel_id=1, source_target_pairs={{0,6},{2,0},{4,2},{6,4},{1,7},{3,1},{5,3},{7,5},{8,14},{10,8},{12,... | collective-permute-start | bytes 12296 | tf_op jit(solution)/shard_map/ppermute | solution.py:27
  124.5 3.5 %collective-permute-done.10 = f32[8,128]{1,0:T(8,128)S(1)} collective-permute-done((f32[8,128]{1,0:T(8,128)S(1)}, f32[8,128]{1,0:T(8,128)S(1)}, u32[]{:S(2)}, u32[]{:S(2)}) %collective-permute-start.10) | collective-permute-done | bytes 4128 | tf_op jit(solution)/shard_map/ppermute | solution.py:27
  128.7 7.6 %all-to-all-done.3 = bf16[32,32,256]{2,1,0:T(8,128)(2,1)S(1)} async-done(((bf16[32,32,256]{2,1,0:T(8,128)(2,1)}), bf16[32,32,256]{2,1,0:T(8,128)(2,1)S(1)}, u32[]{:S(2)}, u32[]{:S(2)}) %all-to-all-start.3) | async-done | bytes 524320 | tf_op jit(solution)/shard_map/all_to_all | solution.py:35
  137.1 16.6 %all_to_all.31 = bf16[32,16,256]{2,1,0:T(8,128)(2,1)S(1)} all-to-all(bf16[32,16,256]{2,1,0:T(8,128)(2,1)S(1)} %bitcast.82), channel_id=1, replica_groups=mesh['y'=4,'z'=8,'x'=4,'core'=2] {'y','z'}, dimensions={0} | all-to-all | bytes 524288 | tf_op jit(solution)/shard_map/all_to_all | solution.py:35
  155.2 3.0 %collective-permute-start.13 = (bf16[2,256,256]{2,1,0:T(8,128)(2,1)S(1)}, bf16[2,256,256]{2,1,0:T(8,128)(2,1)S(1)}, u32[]{:S(2)}, u32[]{:S(2)}) collective-permute-start(bf16[2,256,256]{2,1,0:T(8,128)(2,1)S(1)} %copy_bitcast_fusion.1), channel_id=1, source_target_pairs={{0,4},{2,6},{4,0},{6,2},{1,5},{3,7},{5,1},{7,3},{8,12},{10,14},{12... | collective-permute-start | bytes 786440 | tf_op jit(solution)/shard_map/ppermute | solution.py:27
  158.4 2.5 %fusion.29 = f32[2,256,128]{2,1,0:T(8,128)S(1)} fusion(bf16[2,256,2048]{2,1,0:T(8,128)(2,1)} %all-gather.2.cloned.1.call-done, bf16[2,2048,128]{2,1,0:T(8,128)(2,1)S(1)} %copy-done.4), kind=kOutput, calls=%fused_computation.76 | convolution fusion | flops 268435456 | bytes 3407872 | tf_op jit(solution)/shard_map/esd,edf->esf/dot_general | solution.py:324
  161.6 2.5 %collective-permute-done.14 = bf16[2,256,256]{2,1,0:T(8,128)(2,1)S(1)} collective-permute-done((bf16[2,256,256]{2,1,0:T(8,128)(2,1)S(1)}, bf16[2,256,256]{2,1,0:T(8,128)(2,1)S(1)}, u32[]{:S(2)}, u32[]{:S(2)}) %collective-permute-start.14) | collective-permute-done | bytes 262176 | tf_op jit(solution)/shard_map/ppermute | solution.py:27
  164.2 3.4 %collective-permute-done.13 = bf16[2,256,256]{2,1,0:T(8,128)(2,1)S(1)} collective-permute-done((bf16[2,256,256]{2,1,0:T(8,128)(2,1)S(1)}, bf16[2,256,256]{2,1,0:T(8,128)(2,1)S(1)}, u32[]{:S(2)}, u32[]{:S(2)}) %collective-permute-start.13) | collective-permute-done | bytes 262176 | tf_op jit(solution)/shard_map/ppermute | solution.py:27
  168.3 2.1 collective-permute-done.15
  172.4 2.1 collective-permute-done.16
  176.0 2.4 %collective-permute-start.19 = (bf16[2,256,256]{2,1,0:T(8,128)(2,1)S(1)}, bf16[2,256,256]{2,1,0:T(8,128)(2,1)S(1)}, u32[]{:S(2)}, u32[]{:S(2)}) collective-permute-start(bf16[2,256,256]{2,1,0:T(8,128)(2,1)S(1)} %get-tuple-element.112), channel_id=1, source_target_pairs={{0,6},{2,0},{4,2},{6,4},{1,7},{3,1},{5,3},{7,5},{8,14},{10,8},{12,... | collective-permute-start | bytes 786440 | tf_op jit(solution)/shard_map/ppermute | solution.py:27
  178.9 6.2 %collective-permute-done.17 = bf16[2,256,256]{2,1,0:T(8,128)(2,1)S(1)} collective-permute-done((bf16[2,256,256]{2,1,0:T(8,128)(2,1)S(1)}, bf16[2,256,256]{2,1,0:T(8,128)(2,1)S(1)}, u32[]{:S(2)}, u32[]{:S(2)}) %collective-permute-start.17) | collective-permute-done | bytes 262176 | tf_op jit(solution)/shard_map/ppermute | solution.py:27
  185.1 4.6 %collective-permute-done.19 = bf16[2,256,256]{2,1,0:T(8,128)(2,1)S(1)} collective-permute-done((bf16[2,256,256]{2,1,0:T(8,128)(2,1)S(1)}, bf16[2,256,256]{2,1,0:T(8,128)(2,1)S(1)}, u32[]{:S(2)}, u32[]{:S(2)}) %collective-permute-start.19) | collective-permute-done | bytes 262176 | tf_op jit(solution)/shard_map/ppermute | solution.py:27
  190.9 22.9 %all_to_all.32 = f32[32,16,256]{2,1,0:T(8,128)S(1)} all-to-all(f32[32,16,256]{2,1,0:T(8,128)S(1)} %copy_bitcast_fusion), channel_id=1, replica_groups=mesh['y'=4,'z'=8,'x'=4,'core'=2] {'y','z'}, dimensions={0} | all-to-all | bytes 1048576 | tf_op jit(solution)/shard_map/all_to_all | solution.py:355
  (115 shorter events, 30.0 us)
Async XLA Ops:
  7.2 24.9 %copy-start = (bf16[32,2048]{1,0:T(8,128)(2,1)S(1)}, bf16[32,2048]{1,0:T(8,128)(2,1)}, u32[]{:S(2)}) copy-start(bf16[32,2048]{1,0:T(8,128)(2,1)} %param.13) | copy-start | bytes 393220
  9.2 31.6 %all-to-all-start = ((bf16[32,40,256]{2,1,0:T(8,128)(2,1)}), bf16[32,40,256]{2,1,0:T(8,128)(2,1)S(1)}, u32[]{:S(2)}, u32[]{:S(2)}) async-start(bf16[32,40,256]{2,1,0:T(8,128)(2,1)} %get-tuple-element.54), calls=%async_computation | async-start | bytes 1310720 | tf_op jit(solution)/shard_map/all_to_all | solution.py:35
  40.9 21.7 %collective-permute-start.2 = (bf16[1024,256]{1,0:T(8,128)(2,1)S(1)}, bf16[1024,256]{1,0:T(8,128)(2,1)S(1)}, u32[]{:S(2)}, u32[]{:S(2)}) collective-permute-start(bf16[1024,256]{1,0:T(8,128)(2,1)S(1)} %bitcast.76), channel_id=1, source_target_pairs={{0,2},{2,4},{4,6},{6,0},{1,3},{3,5},{5,7},{7,1},{8,10},{10,12},{12... | collective-permute-start | bytes 1572872 | tf_op jit(solution)/shard_map/ppermute | solution.py:27
  42.4 23.3 %collective-permute-start.1 = (bf16[1024,256]{1,0:T(8,128)(2,1)S(1)}, bf16[1024,256]{1,0:T(8,128)(2,1)S(1)}, u32[]{:S(2)}, u32[]{:S(2)}) collective-permute-start(bf16[1024,256]{1,0:T(8,128)(2,1)S(1)} %bitcast.77), channel_id=1, source_target_pairs={{0,4},{2,6},{4,0},{6,2},{1,5},{3,7},{5,1},{7,3},{8,12},{10,14},{12... | collective-permute-start | bytes 1572872 | tf_op jit(solution)/shard_map/ppermute | solution.py:27
  45.2 20.5 %collective-permute-start = (bf16[1024,256]{1,0:T(8,128)(2,1)S(1)}, bf16[1024,256]{1,0:T(8,128)(2,1)S(1)}, u32[]{:S(2)}, u32[]{:S(2)}) collective-permute-start(bf16[1024,256]{1,0:T(8,128)(2,1)S(1)} %bitcast.78), channel_id=1, source_target_pairs={{0,6},{2,0},{4,2},{6,4},{1,7},{3,1},{5,3},{7,5},{8,14},{10,8},{12,... | collective-permute-start | bytes 1572872 | tf_op jit(solution)/shard_map/ppermute | solution.py:27
  66.0 5.2 %collective-permute-start.3 = (bf16[1024,1024]{1,0:T(8,128)(2,1)S(1)}, bf16[1024,1024]{1,0:T(8,128)(2,1)}, u32[]{:S(2)}, u32[]{:S(2)}) collective-permute-start(bf16[1024,1024]{1,0:T(8,128)(2,1)S(1)} %constant_dynamic-update-slice_fusion.near_ref), channel_id=1, source_target_pairs={{0,1},{1,0},{2,3},{3,2},{4,5},{5,4},{6,7},{7,6},{8,9},{9,8},{10,11... | collective-permute-start | bytes 6291464 | tf_op jit(solution)/shard_map/ppermute | solution.py:31
  76.1 4.2 %collective-permute-start.4 = (bf16[1024,1024]{1,0:T(8,128)(2,1)S(1)}, bf16[1024,1024]{1,0:T(8,128)(2,1)S(1)}, u32[]{:S(2)}, u32[]{:S(2)}) collective-permute-start(bf16[1024,1024]{1,0:T(8,128)(2,1)S(1)} %convolution_convert_fusion), channel_id=1, source_target_pairs={{0,1},{1,0},{2,3},{3,2},{4,5},{5,4},{6,7},{7,6},{8,9},{9,8},{10,11... | collective-permute-start | bytes 6291464 | tf_op jit(solution)/shard_map/ppermute | solution.py:31
  82.2 22.7 %collective-permute-start.5 = (bf16[1024,256]{1,0:T(8,128)(2,1)}, bf16[1024,256]{1,0:T(8,128)(2,1)S(1)}, u32[]{:S(2)}, u32[]{:S(2)}) collective-permute-start(bf16[1024,256]{1,0:T(8,128)(2,1)} %get-tuple-element.75), channel_id=1, source_target_pairs={{0,2},{2,4},{4,6},{6,0},{1,3},{3,5},{5,7},{7,1},{8,10},{10,12},{12... | collective-permute-start | bytes 1572872 | tf_op jit(solution)/shard_map/ppermute | solution.py:27
  83.5 26.1 %collective-permute-start.6 = (bf16[1024,256]{1,0:T(8,128)(2,1)}, bf16[1024,256]{1,0:T(8,128)(2,1)}, u32[]{:S(2)}, u32[]{:S(2)}) collective-permute-start(bf16[1024,256]{1,0:T(8,128)(2,1)} %get-tuple-element.76), channel_id=1, source_target_pairs={{0,4},{2,6},{4,0},{6,2},{1,5},{3,7},{5,1},{7,3},{8,12},{10,14},{12... | collective-permute-start | bytes 1572872 | tf_op jit(solution)/shard_map/ppermute | solution.py:27
  86.0 23.8 %collective-permute-start.7 = (bf16[1024,256]{1,0:T(8,128)(2,1)S(1)}, bf16[1024,256]{1,0:T(8,128)(2,1)}, u32[]{:S(2)}, u32[]{:S(2)}) collective-permute-start(bf16[1024,256]{1,0:T(8,128)(2,1)S(1)} %get-tuple-element.77), channel_id=1, source_target_pairs={{0,6},{2,0},{4,2},{6,4},{1,7},{3,1},{5,3},{7,5},{8,14},{10,8},{12,... | collective-permute-start | bytes 1572872 | tf_op jit(solution)/shard_map/ppermute | solution.py:27
  88.2 16.7 %all-to-all-start.2 = ((f32[32,8,128]{2,1,0:T(8,128)}), f32[32,8,128]{2,1,0:T(8,128)S(1)}, u32[]{:S(2)}, u32[]{:S(2)}) async-start(f32[32,8,128]{2,1,0:T(8,128)} %pad.4), calls=%async_computation.2 | async-start | bytes 262144 | tf_op jit(solution)/shard_map/all_to_all | solution.py:35
  95.1 63.3 %all-gather.2.cloned.1.call-start = ((), (), s32[]{:S(2)}) async-start(), calls=%async_computation.6 | async-start | bytes 2359296 | tf_op jit(solution)/shard_map/all_gather | solution.py:309
  109.8 14.6 %copy-start.11 = (f32[32,1]{1,0:T(8,128)S(1)}, f32[32,1]{1,0:T(8,128)}, u32[]{:S(2)}) copy-start(f32[32,1]{1,0:T(8,128)} %get-tuple-element.89) | copy-start | bytes 388
  109.8 26.6 %copy-start.10 = (f32[32,256]{1,0:T(8,128)S(1)}, f32[32,256]{1,0:T(8,128)}, u32[]{:S(2)}) copy-start(f32[32,256]{1,0:T(8,128)} %get-tuple-element.87) | copy-start | bytes 98308
  109.8 26.6 %copy-start.14 = (f32[1,256]{1,0:T(1,128)S(1)}, f32[1,256]{1,0:T(1,128)}, u32[]{:S(2)}) copy-start(f32[1,256]{1,0:T(1,128)} %get-tuple-element.82) | copy-start | bytes 3076
  109.8 26.7 %copy-start.12 = (f32[512,1]{0,1:T(1,128)S(1)}, f32[512,1]{0,1:T(1,128)}, u32[]{:S(2)}) copy-start(f32[512,1]{0,1:T(1,128)} %reshape.201) | copy-start | bytes 6148
  112.1 46.4 %copy-start.4 = (bf16[2,2048,128]{2,1,0:T(8,128)(2,1)S(1)}, bf16[2,2048,128]{2,1,0:T(8,128)(2,1)}, u32[]{:S(2)}) copy-start(bf16[2,2048,128]{2,1,0:T(8,128)(2,1)} %up_ref.1) | copy-start | bytes 3145732
  112.1 24.3 %all-to-all-start.3 = ((bf16[32,32,256]{2,1,0:T(8,128)(2,1)}), bf16[32,32,256]{2,1,0:T(8,128)(2,1)S(1)}, u32[]{:S(2)}, u32[]{:S(2)}) async-start(bf16[32,32,256]{2,1,0:T(8,128)(2,1)} %bitcast.22), calls=%async_computation.3 | async-start | bytes 1048576 | tf_op jit(solution)/shard_map/all_to_all | solution.py:35
  119.0 1.3 collective-permute-start.8
  120.3 4.2 %collective-permute-start.11 = (f32[8,128]{1,0:T(8,128)S(1)}, f32[8,128]{1,0:T(8,128)S(1)}, u32[]{:S(2)}, u32[]{:S(2)}) collective-permute-start(f32[8,128]{1,0:T(8,128)S(1)} %add.241), channel_id=1, source_target_pairs={{0,6},{2,0},{4,2},{6,4},{1,7},{3,1},{5,3},{7,5},{8,14},{10,8},{12,... | collective-permute-start | bytes 12296 | tf_op jit(solution)/shard_map/ppermute | solution.py:27
  122.9 5.1 %collective-permute-start.10 = (f32[8,128]{1,0:T(8,128)S(1)}, f32[8,128]{1,0:T(8,128)S(1)}, u32[]{:S(2)}, u32[]{:S(2)}) collective-permute-start(f32[8,128]{1,0:T(8,128)S(1)} %add.241), channel_id=1, source_target_pairs={{0,4},{2,6},{4,0},{6,2},{1,5},{3,7},{5,1},{7,3},{8,12},{10,14},{12... | collective-permute-start | bytes 12296 | tf_op jit(solution)/shard_map/ppermute | solution.py:27
  123.9 4.8 %collective-permute-start.9 = (f32[8,128]{1,0:T(8,128)S(1)}, f32[8,128]{1,0:T(8,128)S(1)}, u32[]{:S(2)}, u32[]{:S(2)}) collective-permute-start(f32[8,128]{1,0:T(8,128)S(1)} %add.241), channel_id=1, source_target_pairs={{0,2},{2,4},{4,6},{6,0},{1,3},{3,5},{5,7},{7,1},{8,10},{10,12},{12... | collective-permute-start | bytes 12296 | tf_op jit(solution)/shard_map/ppermute | solution.py:27
  136.5 18.7 %copy-start.9 = (f32[32,256]{1,0:T(8,128)}, f32[32,256]{1,0:T(8,128)S(1)}, u32[]{:S(2)}) copy-start(f32[32,256]{1,0:T(8,128)S(1)} %subtract_divide_fusion) | copy-start | bytes 98308
  137.1 23.8 %copy-start.5 = (bf16[2,2048,128]{2,1,0:T(8,128)(2,1)S(1)}, bf16[2,2048,128]{2,1,0:T(8,128)(2,1)}, u32[]{:S(2)}) copy-start(bf16[2,2048,128]{2,1,0:T(8,128)(2,1)} %gate_ref.1) | copy-start | bytes 3145732
  153.7 10.5 %collective-permute-start.14 = (bf16[2,256,256]{2,1,0:T(8,128)(2,1)S(1)}, bf16[2,256,256]{2,1,0:T(8,128)(2,1)S(1)}, u32[]{:S(2)}, u32[]{:S(2)}) collective-permute-start(bf16[2,256,256]{2,1,0:T(8,128)(2,1)S(1)} %copy_bitcast_fusion.1), channel_id=1, source_target_pairs={{0,2},{2,4},{4,6},{6,0},{1,3},{3,5},{5,7},{7,1},{8,10},{10,12},{12... | collective-permute-start | bytes 786440 | tf_op jit(solution)/shard_map/ppermute | solution.py:27
  155.2 12.3 %collective-permute-start.13 = (bf16[2,256,256]{2,1,0:T(8,128)(2,1)S(1)}, bf16[2,256,256]{2,1,0:T(8,128)(2,1)S(1)}, u32[]{:S(2)}, u32[]{:S(2)}) collective-permute-start(bf16[2,256,256]{2,1,0:T(8,128)(2,1)S(1)} %copy_bitcast_fusion.1), channel_id=1, source_target_pairs={{0,4},{2,6},{4,0},{6,2},{1,5},{3,7},{5,1},{7,3},{8,12},{10,14},{12... | collective-permute-start | bytes 786440 | tf_op jit(solution)/shard_map/ppermute | solution.py:27
  158.2 9.3 %collective-permute-start.12 = (bf16[2,256,256]{2,1,0:T(8,128)(2,1)S(1)}, bf16[2,256,256]{2,1,0:T(8,128)(2,1)S(1)}, u32[]{:S(2)}, u32[]{:S(2)}) collective-permute-start(bf16[2,256,256]{2,1,0:T(8,128)(2,1)S(1)} %copy_bitcast_fusion.1), channel_id=1, source_target_pairs={{0,6},{2,0},{4,2},{6,4},{1,7},{3,1},{5,3},{7,5},{8,14},{10,8},{12,... | collective-permute-start | bytes 786440 | tf_op jit(solution)/shard_map/ppermute | solution.py:27
  167.7 2.7 %collective-permute-start.15 = (bf16[2,256,1024]{2,1,0:T(8,128)(2,1)S(1)}, bf16[2,256,1024]{2,1,0:T(8,128)(2,1)S(1)}, u32[]{:S(2)}, u32[]{:S(2)}) collective-permute-start(bf16[2,256,1024]{2,1,0:T(8,128)(2,1)S(1)} %constant_dynamic-update-slice_fusion.4), channel_id=1, source_target_pairs={{0,1},{1,0},{2,3},{3,2},{4,5},{5,4},{6,7},{7,6},{8,9},{9,8},{10,11... | collective-permute-start | bytes 3145736 | tf_op jit(solution)/shard_map/ppermute | solution.py:31
  171.5 3.0 %collective-permute-start.16 = (bf16[2,256,1024]{2,1,0:T(8,128)(2,1)S(1)}, bf16[2,256,1024]{2,1,0:T(8,128)(2,1)S(1)}, u32[]{:S(2)}, u32[]{:S(2)}) collective-permute-start(bf16[2,256,1024]{2,1,0:T(8,128)(2,1)S(1)} %convolution_convert_fusion.1), channel_id=1, source_target_pairs={{0,1},{1,0},{2,3},{3,2},{4,5},{5,4},{6,7},{7,6},{8,9},{9,8},{10,11... | collective-permute-start | bytes 3145736 | tf_op jit(solution)/shard_map/ppermute | solution.py:31
  175.1 10.0 %collective-permute-start.17 = (bf16[2,256,256]{2,1,0:T(8,128)(2,1)S(1)}, bf16[2,256,256]{2,1,0:T(8,128)(2,1)S(1)}, u32[]{:S(2)}, u32[]{:S(2)}) collective-permute-start(bf16[2,256,256]{2,1,0:T(8,128)(2,1)S(1)} %get-tuple-element.111), channel_id=1, source_target_pairs={{0,2},{2,4},{4,6},{6,0},{1,3},{3,5},{5,7},{7,1},{8,10},{10,12},{12... | collective-permute-start | bytes 786440 | tf_op jit(solution)/shard_map/ppermute | solution.py:27
  176.0 13.6 %collective-permute-start.19 = (bf16[2,256,256]{2,1,0:T(8,128)(2,1)S(1)}, bf16[2,256,256]{2,1,0:T(8,128)(2,1)S(1)}, u32[]{:S(2)}, u32[]{:S(2)}) collective-permute-start(bf16[2,256,256]{2,1,0:T(8,128)(2,1)S(1)} %get-tuple-element.112), channel_id=1, source_target_pairs={{0,6},{2,0},{4,2},{6,4},{1,7},{3,1},{5,3},{7,5},{8,14},{10,8},{12,... | collective-permute-start | bytes 786440 | tf_op jit(solution)/shard_map/ppermute | solution.py:27
  178.4 12.4 %collective-permute-start.18 = (bf16[2,256,256]{2,1,0:T(8,128)(2,1)S(1)}, bf16[2,256,256]{2,1,0:T(8,128)(2,1)S(1)}, u32[]{:S(2)}, u32[]{:S(2)}) collective-permute-start(bf16[2,256,256]{2,1,0:T(8,128)(2,1)S(1)} %get-tuple-element.113), channel_id=1, source_target_pairs={{0,4},{2,6},{4,0},{6,2},{1,5},{3,7},{5,1},{7,3},{8,12},{10,14},{12... | collective-permute-start | bytes 786440 | tf_op jit(solution)/shard_map/ppermute | solution.py:27
  (9 other events, 42.0 us)
Sparse Core Ops, SparseCore 0:
  109.9 27.4 all-gather.1

commit v6 on v5

--- a/solution.py
+++ b/solution.py
@@ -36,7 +36,9 @@
 
 
 def in_ring_order(a, move, ring):
-    return [a] + [move(a, ring - k) for k in range(1, ring)]
+    near = sorted(range(1, ring), key=lambda k: min(k, ring - k))
+    moved = {k: move(a, ring - k) for k in near}
+    return [a] + [moved[k] for k in range(1, ring)]
 
 
 def normed_to_spread(
@@ -300,7 +302,7 @@
     far = across_core(far)
     kept, *sent = near_gradient(score_grad, head_near, far)
     kept, sent, score_grad, along = lax.optimization_barrier((kept, sent, score_grad, along))
-    sent = [along_x(a, k + 1) for k, a in enumerate(sent)]
+    sent = [along_x(sent[k - 1], k) for k in (2, 1, 3)]
     along = jnp.pad(along.reshape(n_expert, 1, rows), ((0, 0), (0, 7), (0, 128 - rows)))
     along = jnp.sum(exchanged(along, ("y", "z")), axis=0)
     head_grad = head_gradient(order, normed_near, normed_far, score_grad)

time: 223 us -> 223 us (level)
  transfers between devices with their start and end apart: 24 -> 24, of which waited for: 16 -> 17; matrix products, arithmetic and copies ran while one was open for 8% -> 8% of each run, Pallas kernels for 8% -> 8%
where the time goes in v6:
time: 223 us; the launch traced here: 222 us
  blocking collectives  55.3 us (25%)
  waiting for transfers between devices  55.2 us (25%)
  starting transfers between devices  49.9 us (22%)
  Pallas kernels  20.7 us (9%)
  between operations  14.6 us (7%)
  matrix products  12.6 us (6%)
  other arithmetic  7.63 us (3%)
  local copies, waits for them, and re-layouts  5.78 us (3%)
    all_to_all x2, blocking collectives, exchanged(): return lax.all_to_all(a, axes, 0, 0, tiled=True)  32.4 us
    ppermute x15, waiting for transfers between devices, along_x(): return lax.ppermute(a, 'x', [(p, (p + step) % XN) for p in range(XN)])  29.3 us
    all_to_all x3, starting transfers between devices, exchanged(): return lax.all_to_all(a, axes, 0, 0, tiled=True)  25.2 us
    ppermute x15, starting transfers between devices, along_x(): return lax.ppermute(a, 'x', [(p, (p + step) % XN) for p in range(XN)])  23.6 us
    all_to_all x1, blocking collectives, on_device(): returned = lax.all_to_all(near, ('y', 'z'), 0, 0, tiled=True)  22.9 us
    all_to_all x3, waiting for transfers between devices, exchanged(): return lax.all_to_all(a, axes, 0, 0, tiled=True)  16.7 us
    ppermute x5, waiting for transfers between devices, across_core(): return lax.ppermute(a, 'core', [(p, CN - 1 - p) for p in range(CN)])  9.2 us
    pallas_call x1, Pallas kernels, head_gradient(): pl.pallas_call(body, grid_spec=pltpu.PrefetchScalarGridSpec(num_scalar_pr...  9.05 us
  transfers between devices with their start and end apart: 24, of which 17 were waited for; matrix products, arithmetic and copies ran while one was open for 8% of the time, Pallas kernels for 8%

profile of v6, /device:TPU:32, one launch (start us, length us, event | category | flops | bytes accessed | tf_op | source)
XLA Modules:
  0.0 221.7 jit_solution(10309797127303893376)
XLA Ops:
  7.2 2.0 normed_to_spread.1
  9.2 11.4 %all-to-all-start = ((bf16[32,40,256]{2,1,0:T(8,128)(2,1)}), bf16[32,40,256]{2,1,0:T(8,128)(2,1)S(1)}, u32[]{:S(2)}, u32[]{:S(2)}) async-start(bf16[32,40,256]{2,1,0:T(8,128)(2,1)} %get-tuple-element.54), calls=%async_computation | async-start | bytes 1310720 | tf_op jit(solution)/shard_map/all_to_all | solution.py:35
  24.2 7.8 %turned_weights.1 = (bf16[1024,384]{1,0:T(8,128)(2,1)}, bf16[1024,384]{1,0:T(8,128)(2,1)}, bf16[2,2048,256]{2,1,0:T(8,128)(2,1)}, bf16[2,128,2048]{2,1,0:T(8,128)(2,1)}) custom-call(s32[8]{0:T(128)} %stack.35.order_ref, bf16[2048,384]{1,0:T(8,128)(2,1)} %head_ref.1, bf16[2,2048,128]{2,1,0:T(8,128)(2,1)} %gate_ref.1, bf16[2,2048,128]{2,1,0:T(8,128)(2,1)} %up_ref.1, ...), custom_call_target="tpu_custom_call" | custom-call | bytes 9437184 | tf_op jit(solution)/shard_map/turned_weights/pallas_call | solution.py:111
  32.4 8.4 %all-to-all-done = bf16[32,40,256]{2,1,0:T(8,128)(2,1)S(1)} async-done(((bf16[32,40,256]{2,1,0:T(8,128)(2,1)}), bf16[32,40,256]{2,1,0:T(8,128)(2,1)S(1)}, u32[]{:S(2)}, u32[]{:S(2)}) %all-to-all-start) | async-done | bytes 655392 | tf_op jit(solution)/shard_map/all_to_all | solution.py:35
  40.9 1.6 collective-permute-start.2
  42.4 2.7 %collective-permute-start.1 = (bf16[1024,256]{1,0:T(8,128)(2,1)S(1)}, bf16[1024,256]{1,0:T(8,128)(2,1)S(1)}, u32[]{:S(2)}, u32[]{:S(2)}) collective-permute-start(bf16[1024,256]{1,0:T(8,128)(2,1)S(1)} %bitcast.77), channel_id=1, source_target_pairs={{0,4},{2,6},{4,0},{6,2},{1,5},{3,7},{5,1},{7,3},{8,12},{10,14},{12... | collective-permute-start | bytes 1572872 | tf_op jit(solution)/shard_map/ppermute | solution.py:27
  46.6 16.0 %all_to_all.30 = bf16[32,16,256]{2,1,0:T(8,128)(2,1)S(1)} all-to-all(bf16[32,16,256]{2,1,0:T(8,128)(2,1)S(1)} %bitcast.81), channel_id=1, replica_groups=mesh['y'=4,'z'=8,'x'=4,'core'=2] {'y','z'}, dimensions={0} | all-to-all | bytes 524288 | tf_op jit(solution)/shard_map/all_to_all | solution.py:35
  62.6 3.1 %collective-permute-done.1 = bf16[1024,256]{1,0:T(8,128)(2,1)S(1)} collective-permute-done((bf16[1024,256]{1,0:T(8,128)(2,1)S(1)}, bf16[1024,256]{1,0:T(8,128)(2,1)S(1)}, u32[]{:S(2)}, u32[]{:S(2)}) %collective-permute-start.1) | collective-permute-done | bytes 524320 | tf_op jit(solution)/shard_map/ppermute | solution.py:27
  71.2 2.8 %fusion.27 = f32[1024,384]{1,0:T(8,128)S(1)} fusion(bf16[1024,1024]{1,0:T(8,128)(2,1)} %collective-permute-done.3.far_ref, bf16[1024,384]{1,0:T(8,128)(2,1)S(1)} %copy-done.16), kind=kOutput, calls=%fused_computation.74 | convolution fusion | flops 805306368 | bytes 4456448 | tf_op jit(solution)/shard_map/dot_general | solution.py:17
  76.5 3.8 %collective-permute-done.4.far_ref = bf16[1024,1024]{1,0:T(8,128)(2,1)S(1)} collective-permute-done((bf16[1024,1024]{1,0:T(8,128)(2,1)S(1)}, bf16[1024,1024]{1,0:T(8,128)(2,1)S(1)}, u32[]{:S(2)}, u32[]{:S(2)}) %collective-permute-start.4) | collective-permute-done | bytes 2097184 | tf_op jit(solution)/shard_map/ppermute | solution.py:31
  80.3 1.9 near_gradient.1
  82.2 2.6 %collective-permute-start.5 = (bf16[1024,256]{1,0:T(8,128)(2,1)}, bf16[1024,256]{1,0:T(8,128)(2,1)S(1)}, u32[]{:S(2)}, u32[]{:S(2)}) collective-permute-start(bf16[1024,256]{1,0:T(8,128)(2,1)} %get-tuple-element.75), channel_id=1, source_target_pairs={{0,4},{2,6},{4,0},{6,2},{1,5},{3,7},{5,1},{7,3},{8,12},{10,14},{12... | collective-permute-start | bytes 1572872 | tf_op jit(solution)/shard_map/ppermute | solution.py:27
  85.3 2.8 %collective-permute-start.7 = (bf16[1024,256]{1,0:T(8,128)(2,1)S(1)}, bf16[1024,256]{1,0:T(8,128)(2,1)}, u32[]{:S(2)}, u32[]{:S(2)}) collective-permute-start(bf16[1024,256]{1,0:T(8,128)(2,1)S(1)} %get-tuple-element.77), channel_id=1, source_target_pairs={{0,6},{2,0},{4,2},{6,4},{1,7},{3,1},{5,3},{7,5},{8,14},{10,8},{12,... | collective-permute-start | bytes 1572872 | tf_op jit(solution)/shard_map/ppermute | solution.py:27
  88.9 6.8 %all-to-all-start.2 = ((f32[32,8,128]{2,1,0:T(8,128)}), f32[32,8,128]{2,1,0:T(8,128)S(1)}, u32[]{:S(2)}, u32[]{:S(2)}) async-start(f32[32,8,128]{2,1,0:T(8,128)} %pad.4), calls=%async_computation.2 | async-start | bytes 262144 | tf_op jit(solution)/shard_map/all_to_all | solution.py:35
  96.5 9.0 %head_gradient.1 = f32[2048,384]{1,0:T(8,128)} custom-call(s32[8]{0:T(128)} %stack.35.order_ref, bf16[1024,1024]{1,0:T(8,128)(2,1)} %copy-done.6, bf16[1024,1024]{1,0:T(8,128)(2,1)} %collective-permute-done.3.far_ref, bf16[1024,384]{1,0:T(8,128)(2,1)} %copy-done.1), custom_call_target="tpu_custom_call" | custom-call | flops 1024 | bytes 1024 | tf_op jit(solution)/shard_map/head_gradient/pallas_call | solution.py:159
  105.6 3.8 %collective-permute-done.6 = bf16[1024,256]{1,0:T(8,128)(2,1)} collective-permute-done((bf16[1024,256]{1,0:T(8,128)(2,1)}, bf16[1024,256]{1,0:T(8,128)(2,1)}, u32[]{:S(2)}, u32[]{:S(2)}) %collective-permute-start.6) | collective-permute-done | bytes 524320 | tf_op jit(solution)/shard_map/ppermute | solution.py:27
  109.5 2.2 %add_convert_fusion = bf16[1024,256]{1,0:T(8,128)(2,1)} fusion(f32[1024,256]{1,0:T(8,128)S(1)} %get-tuple-element.83, bf16[1024,256]{1,0:T(8,128)(2,1)} %collective-permute-done.7, bf16[1024,256]{1,0:T(8,128)(2,1)} %collective-permute-done.6, bf16[1024,256]{1,0:T(8,128)(2,1)S(1)} %collective-permute-done.5), kind=kLoop, calls=%fused_computation.12 | loop fusion | flops 1835008 | bytes 3145728 | tf_op jit(solution)/shard_map/convert_element_type | solution.py:314
  111.7 7.0 %all-to-all-start.3 = ((bf16[32,32,256]{2,1,0:T(8,128)(2,1)}), bf16[32,32,256]{2,1,0:T(8,128)(2,1)S(1)}, u32[]{:S(2)}, u32[]{:S(2)}) async-start(bf16[32,32,256]{2,1,0:T(8,128)(2,1)} %bitcast.22), calls=%async_computation.3 | async-start | bytes 1048576 | tf_op jit(solution)/shard_map/all_to_all | solution.py:35
  120.0 2.3 %collective-permute-start.11 = (f32[8,128]{1,0:T(8,128)S(1)}, f32[8,128]{1,0:T(8,128)S(1)}, u32[]{:S(2)}, u32[]{:S(2)}) collective-permute-start(f32[8,128]{1,0:T(8,128)S(1)} %add.241), channel_id=1, source_target_pairs={{0,6},{2,0},{4,2},{6,4},{1,7},{3,1},{5,3},{7,5},{8,14},{10,8},{12,... | collective-permute-start | bytes 12296 | tf_op jit(solution)/shard_map/ppermute | solution.py:27
  123.6 3.8 %collective-permute-done.10 = f32[8,128]{1,0:T(8,128)S(1)} collective-permute-done((f32[8,128]{1,0:T(8,128)S(1)}, f32[8,128]{1,0:T(8,128)S(1)}, u32[]{:S(2)}, u32[]{:S(2)}) %collective-permute-start.10) | collective-permute-done | bytes 4128 | tf_op jit(solution)/shard_map/ppermute | solution.py:27
  128.2 8.3 %all-to-all-done.3 = bf16[32,32,256]{2,1,0:T(8,128)(2,1)S(1)} async-done(((bf16[32,32,256]{2,1,0:T(8,128)(2,1)}), bf16[32,32,256]{2,1,0:T(8,128)(2,1)S(1)}, u32[]{:S(2)}, u32[]{:S(2)}) %all-to-all-start.3) | async-done | bytes 524320 | tf_op jit(solution)/shard_map/all_to_all | solution.py:35
  137.3 16.4 %all_to_all.31 = bf16[32,16,256]{2,1,0:T(8,128)(2,1)S(1)} all-to-all(bf16[32,16,256]{2,1,0:T(8,128)(2,1)S(1)} %bitcast.82), channel_id=1, replica_groups=mesh['y'=4,'z'=8,'x'=4,'core'=2] {'y','z'}, dimensions={0} | all-to-all | bytes 524288 | tf_op jit(solution)/shard_map/all_to_all | solution.py:35
  155.1 2.4 %collective-permute-start.13 = (bf16[2,256,256]{2,1,0:T(8,128)(2,1)S(1)}, bf16[2,256,256]{2,1,0:T(8,128)(2,1)S(1)}, u32[]{:S(2)}, u32[]{:S(2)}) collective-permute-start(bf16[2,256,256]{2,1,0:T(8,128)(2,1)S(1)} %copy_bitcast_fusion.1), channel_id=1, source_target_pairs={{0,4},{2,6},{4,0},{6,2},{1,5},{3,7},{5,1},{7,3},{8,12},{10,14},{12... | collective-permute-start | bytes 786440 | tf_op jit(solution)/shard_map/ppermute | solution.py:27
  158.2 2.5 %fusion.29 = f32[2,256,128]{2,1,0:T(8,128)S(1)} fusion(bf16[2,256,2048]{2,1,0:T(8,128)(2,1)} %all-gather.2.cloned.1.call-done, bf16[2,2048,128]{2,1,0:T(8,128)(2,1)S(1)} %copy-done.4), kind=kOutput, calls=%fused_computation.76 | convolution fusion | flops 268435456 | bytes 3407872 | tf_op jit(solution)/shard_map/esd,edf->esf/dot_general | solution.py:326
  161.4 2.7 %collective-permute-done.14 = bf16[2,256,256]{2,1,0:T(8,128)(2,1)S(1)} collective-permute-done((bf16[2,256,256]{2,1,0:T(8,128)(2,1)S(1)}, bf16[2,256,256]{2,1,0:T(8,128)(2,1)S(1)}, u32[]{:S(2)}, u32[]{:S(2)}) %collective-permute-start.14) | collective-permute-done | bytes 262176 | tf_op jit(solution)/shard_map/ppermute | solution.py:27
  164.1 2.8 %collective-permute-done.13 = bf16[2,256,256]{2,1,0:T(8,128)(2,1)S(1)} collective-permute-done((bf16[2,256,256]{2,1,0:T(8,128)(2,1)S(1)}, bf16[2,256,256]{2,1,0:T(8,128)(2,1)S(1)}, u32[]{:S(2)}, u32[]{:S(2)}) %collective-permute-start.13) | collective-permute-done | bytes 262176 | tf_op jit(solution)/shard_map/ppermute | solution.py:27
  167.7 2.1 collective-permute-done.15
  171.9 2.1 collective-permute-done.16
  175.9 2.0 collective-permute-start.19
  178.7 5.5 %collective-permute-done.17 = bf16[2,256,256]{2,1,0:T(8,128)(2,1)S(1)} collective-permute-done((bf16[2,256,256]{2,1,0:T(8,128)(2,1)S(1)}, bf16[2,256,256]{2,1,0:T(8,128)(2,1)S(1)}, u32[]{:S(2)}, u32[]{:S(2)}) %collective-permute-start.17) | collective-permute-done | bytes 262176 | tf_op jit(solution)/shard_map/ppermute | solution.py:27
  184.2 4.9 %collective-permute-done.19 = bf16[2,256,256]{2,1,0:T(8,128)(2,1)S(1)} collective-permute-done((bf16[2,256,256]{2,1,0:T(8,128)(2,1)S(1)}, bf16[2,256,256]{2,1,0:T(8,128)(2,1)S(1)}, u32[]{:S(2)}, u32[]{:S(2)}) %collective-permute-start.19) | collective-permute-done | bytes 262176 | tf_op jit(solution)/shard_map/ppermute | solution.py:27
  190.8 22.9 %all_to_all.32 = f32[32,16,256]{2,1,0:T(8,128)S(1)} all-to-all(f32[32,16,256]{2,1,0:T(8,128)S(1)} %copy_bitcast_fusion), channel_id=1, replica_groups=mesh['y'=4,'z'=8,'x'=4,'core'=2] {'y','z'}, dimensions={0} | all-to-all | bytes 1048576 | tf_op jit(solution)/shard_map/all_to_all | solution.py:357
  (115 shorter events, 30.5 us)
Async XLA Ops:
  7.2 24.9 %copy-start = (bf16[32,2048]{1,0:T(8,128)(2,1)S(1)}, bf16[32,2048]{1,0:T(8,128)(2,1)}, u32[]{:S(2)}) copy-start(bf16[32,2048]{1,0:T(8,128)(2,1)} %param.13) | copy-start | bytes 393220
  9.2 31.6 %all-to-all-start = ((bf16[32,40,256]{2,1,0:T(8,128)(2,1)}), bf16[32,40,256]{2,1,0:T(8,128)(2,1)S(1)}, u32[]{:S(2)}, u32[]{:S(2)}) async-start(bf16[32,40,256]{2,1,0:T(8,128)(2,1)} %get-tuple-element.54), calls=%async_computation | async-start | bytes 1310720 | tf_op jit(solution)/shard_map/all_to_all | solution.py:35
  40.9 21.7 %collective-permute-start.2 = (bf16[1024,256]{1,0:T(8,128)(2,1)S(1)}, bf16[1024,256]{1,0:T(8,128)(2,1)S(1)}, u32[]{:S(2)}, u32[]{:S(2)}) collective-permute-start(bf16[1024,256]{1,0:T(8,128)(2,1)S(1)} %bitcast.76), channel_id=1, source_target_pairs={{0,2},{2,4},{4,6},{6,0},{1,3},{3,5},{5,7},{7,1},{8,10},{10,12},{12... | collective-permute-start | bytes 1572872 | tf_op jit(solution)/shard_map/ppermute | solution.py:27
  42.4 23.3 %collective-permute-start.1 = (bf16[1024,256]{1,0:T(8,128)(2,1)S(1)}, bf16[1024,256]{1,0:T(8,128)(2,1)S(1)}, u32[]{:S(2)}, u32[]{:S(2)}) collective-permute-start(bf16[1024,256]{1,0:T(8,128)(2,1)S(1)} %bitcast.77), channel_id=1, source_target_pairs={{0,4},{2,6},{4,0},{6,2},{1,5},{3,7},{5,1},{7,3},{8,12},{10,14},{12... | collective-permute-start | bytes 1572872 | tf_op jit(solution)/shard_map/ppermute | solution.py:27
  45.2 20.5 %collective-permute-start = (bf16[1024,256]{1,0:T(8,128)(2,1)S(1)}, bf16[1024,256]{1,0:T(8,128)(2,1)S(1)}, u32[]{:S(2)}, u32[]{:S(2)}) collective-permute-start(bf16[1024,256]{1,0:T(8,128)(2,1)S(1)} %bitcast.78), channel_id=1, source_target_pairs={{0,6},{2,0},{4,2},{6,4},{1,7},{3,1},{5,3},{7,5},{8,14},{10,8},{12,... | collective-permute-start | bytes 1572872 | tf_op jit(solution)/shard_map/ppermute | solution.py:27
  66.0 5.2 %collective-permute-start.3 = (bf16[1024,1024]{1,0:T(8,128)(2,1)S(1)}, bf16[1024,1024]{1,0:T(8,128)(2,1)}, u32[]{:S(2)}, u32[]{:S(2)}) collective-permute-start(bf16[1024,1024]{1,0:T(8,128)(2,1)S(1)} %constant_dynamic-update-slice_fusion.near_ref), channel_id=1, source_target_pairs={{0,1},{1,0},{2,3},{3,2},{4,5},{5,4},{6,7},{7,6},{8,9},{9,8},{10,11... | collective-permute-start | bytes 6291464 | tf_op jit(solution)/shard_map/ppermute | solution.py:31
  76.1 4.2 %collective-permute-start.4 = (bf16[1024,1024]{1,0:T(8,128)(2,1)S(1)}, bf16[1024,1024]{1,0:T(8,128)(2,1)S(1)}, u32[]{:S(2)}, u32[]{:S(2)}) collective-permute-start(bf16[1024,1024]{1,0:T(8,128)(2,1)S(1)} %convolution_convert_fusion), channel_id=1, source_target_pairs={{0,1},{1,0},{2,3},{3,2},{4,5},{5,4},{6,7},{7,6},{8,9},{9,8},{10,11... | collective-permute-start | bytes 6291464 | tf_op jit(solution)/shard_map/ppermute | solution.py:31
  82.2 23.4 %collective-permute-start.5 = (bf16[1024,256]{1,0:T(8,128)(2,1)}, bf16[1024,256]{1,0:T(8,128)(2,1)S(1)}, u32[]{:S(2)}, u32[]{:S(2)}) collective-permute-start(bf16[1024,256]{1,0:T(8,128)(2,1)} %get-tuple-element.75), channel_id=1, source_target_pairs={{0,4},{2,6},{4,0},{6,2},{1,5},{3,7},{5,1},{7,3},{8,12},{10,14},{12... | collective-permute-start | bytes 1572872 | tf_op jit(solution)/shard_map/ppermute | solution.py:27
  84.9 24.6 %collective-permute-start.6 = (bf16[1024,256]{1,0:T(8,128)(2,1)}, bf16[1024,256]{1,0:T(8,128)(2,1)}, u32[]{:S(2)}, u32[]{:S(2)}) collective-permute-start(bf16[1024,256]{1,0:T(8,128)(2,1)} %get-tuple-element.76), channel_id=1, source_target_pairs={{0,2},{2,4},{4,6},{6,0},{1,3},{3,5},{5,7},{7,1},{8,10},{10,12},{12... | collective-permute-start | bytes 1572872 | tf_op jit(solution)/shard_map/ppermute | solution.py:27
  85.3 24.1 %collective-permute-start.7 = (bf16[1024,256]{1,0:T(8,128)(2,1)S(1)}, bf16[1024,256]{1,0:T(8,128)(2,1)}, u32[]{:S(2)}, u32[]{:S(2)}) collective-permute-start(bf16[1024,256]{1,0:T(8,128)(2,1)S(1)} %get-tuple-element.77), channel_id=1, source_target_pairs={{0,6},{2,0},{4,2},{6,4},{1,7},{3,1},{5,3},{7,5},{8,14},{10,8},{12,... | collective-permute-start | bytes 1572872 | tf_op jit(solution)/shard_map/ppermute | solution.py:27
  88.9 16.7 %all-to-all-start.2 = ((f32[32,8,128]{2,1,0:T(8,128)}), f32[32,8,128]{2,1,0:T(8,128)S(1)}, u32[]{:S(2)}, u32[]{:S(2)}) async-start(f32[32,8,128]{2,1,0:T(8,128)} %pad.4), calls=%async_computation.2 | async-start | bytes 262144 | tf_op jit(solution)/shard_map/all_to_all | solution.py:35
  95.7 62.5 %all-gather.2.cloned.1.call-start = ((), (), s32[]{:S(2)}) async-start(), calls=%async_computation.6 | async-start | bytes 2359296 | tf_op jit(solution)/shard_map/all_gather | solution.py:311
  109.4 13.9 %copy-start.11 = (f32[32,1]{1,0:T(8,128)S(1)}, f32[32,1]{1,0:T(8,128)}, u32[]{:S(2)}) copy-start(f32[32,1]{1,0:T(8,128)} %get-tuple-element.89) | copy-start | bytes 388
  109.5 27.2 %copy-start.10 = (f32[32,256]{1,0:T(8,128)S(1)}, f32[32,256]{1,0:T(8,128)}, u32[]{:S(2)}) copy-start(f32[32,256]{1,0:T(8,128)} %get-tuple-element.87) | copy-start | bytes 98308
  109.5 27.2 %copy-start.14 = (f32[1,256]{1,0:T(1,128)S(1)}, f32[1,256]{1,0:T(1,128)}, u32[]{:S(2)}) copy-start(f32[1,256]{1,0:T(1,128)} %get-tuple-element.82) | copy-start | bytes 3076
  109.5 27.3 %copy-start.12 = (f32[512,1]{0,1:T(1,128)S(1)}, f32[512,1]{0,1:T(1,128)}, u32[]{:S(2)}) copy-start(f32[512,1]{0,1:T(1,128)} %reshape.201) | copy-start | bytes 6148
  111.7 46.4 %copy-start.4 = (bf16[2,2048,128]{2,1,0:T(8,128)(2,1)S(1)}, bf16[2,2048,128]{2,1,0:T(8,128)(2,1)}, u32[]{:S(2)}) copy-start(bf16[2,2048,128]{2,1,0:T(8,128)(2,1)} %up_ref.1) | copy-start | bytes 3145732
  111.7 24.8 %all-to-all-start.3 = ((bf16[32,32,256]{2,1,0:T(8,128)(2,1)}), bf16[32,32,256]{2,1,0:T(8,128)(2,1)S(1)}, u32[]{:S(2)}, u32[]{:S(2)}) async-start(bf16[32,32,256]{2,1,0:T(8,128)(2,1)} %bitcast.22), calls=%async_computation.3 | async-start | bytes 1048576 | tf_op jit(solution)/shard_map/all_to_all | solution.py:35
  118.7 1.3 collective-permute-start.8
  120.0 3.6 %collective-permute-start.11 = (f32[8,128]{1,0:T(8,128)S(1)}, f32[8,128]{1,0:T(8,128)S(1)}, u32[]{:S(2)}, u32[]{:S(2)}) collective-permute-start(f32[8,128]{1,0:T(8,128)S(1)} %add.241), channel_id=1, source_target_pairs={{0,6},{2,0},{4,2},{6,4},{1,7},{3,1},{5,3},{7,5},{8,14},{10,8},{12,... | collective-permute-start | bytes 12296 | tf_op jit(solution)/shard_map/ppermute | solution.py:27
  122.3 5.1 %collective-permute-start.10 = (f32[8,128]{1,0:T(8,128)S(1)}, f32[8,128]{1,0:T(8,128)S(1)}, u32[]{:S(2)}, u32[]{:S(2)}) collective-permute-start(f32[8,128]{1,0:T(8,128)S(1)} %add.241), channel_id=1, source_target_pairs={{0,4},{2,6},{4,0},{6,2},{1,5},{3,7},{5,1},{7,3},{8,12},{10,14},{12... | collective-permute-start | bytes 12296 | tf_op jit(solution)/shard_map/ppermute | solution.py:27
  123.4 4.8 %collective-permute-start.9 = (f32[8,128]{1,0:T(8,128)S(1)}, f32[8,128]{1,0:T(8,128)S(1)}, u32[]{:S(2)}, u32[]{:S(2)}) collective-permute-start(f32[8,128]{1,0:T(8,128)S(1)} %add.241), channel_id=1, source_target_pairs={{0,2},{2,4},{4,6},{6,0},{1,3},{3,5},{5,7},{7,1},{8,10},{10,12},{12... | collective-permute-start | bytes 12296 | tf_op jit(solution)/shard_map/ppermute | solution.py:27
  136.7 18.4 %copy-start.9 = (f32[32,256]{1,0:T(8,128)}, f32[32,256]{1,0:T(8,128)S(1)}, u32[]{:S(2)}) copy-start(f32[32,256]{1,0:T(8,128)S(1)} %subtract_divide_fusion) | copy-start | bytes 98308
  137.3 23.3 %copy-start.5 = (bf16[2,2048,128]{2,1,0:T(8,128)(2,1)S(1)}, bf16[2,2048,128]{2,1,0:T(8,128)(2,1)}, u32[]{:S(2)}) copy-start(bf16[2,2048,128]{2,1,0:T(8,128)(2,1)} %gate_ref.1) | copy-start | bytes 3145732
  153.7 10.3 %collective-permute-start.14 = (bf16[2,256,256]{2,1,0:T(8,128)(2,1)S(1)}, bf16[2,256,256]{2,1,0:T(8,128)(2,1)S(1)}, u32[]{:S(2)}, u32[]{:S(2)}) collective-permute-start(bf16[2,256,256]{2,1,0:T(8,128)(2,1)S(1)} %copy_bitcast_fusion.1), channel_id=1, source_target_pairs={{0,2},{2,4},{4,6},{6,0},{1,3},{3,5},{5,7},{7,1},{8,10},{10,12},{12... | collective-permute-start | bytes 786440 | tf_op jit(solution)/shard_map/ppermute | solution.py:27
  155.1 11.7 %collective-permute-start.13 = (bf16[2,256,256]{2,1,0:T(8,128)(2,1)S(1)}, bf16[2,256,256]{2,1,0:T(8,128)(2,1)S(1)}, u32[]{:S(2)}, u32[]{:S(2)}) collective-permute-start(bf16[2,256,256]{2,1,0:T(8,128)(2,1)S(1)} %copy_bitcast_fusion.1), channel_id=1, source_target_pairs={{0,4},{2,6},{4,0},{6,2},{1,5},{3,7},{5,1},{7,3},{8,12},{10,14},{12... | collective-permute-start | bytes 786440 | tf_op jit(solution)/shard_map/ppermute | solution.py:27
  157.6 9.4 %collective-permute-start.12 = (bf16[2,256,256]{2,1,0:T(8,128)(2,1)S(1)}, bf16[2,256,256]{2,1,0:T(8,128)(2,1)S(1)}, u32[]{:S(2)}, u32[]{:S(2)}) collective-permute-start(bf16[2,256,256]{2,1,0:T(8,128)(2,1)S(1)} %copy_bitcast_fusion.1), channel_id=1, source_target_pairs={{0,6},{2,0},{4,2},{6,4},{1,7},{3,1},{5,3},{7,5},{8,14},{10,8},{12,... | collective-permute-start | bytes 786440 | tf_op jit(solution)/shard_map/ppermute | solution.py:27
  167.1 2.7 %collective-permute-start.15 = (bf16[2,256,1024]{2,1,0:T(8,128)(2,1)S(1)}, bf16[2,256,1024]{2,1,0:T(8,128)(2,1)S(1)}, u32[]{:S(2)}, u32[]{:S(2)}) collective-permute-start(bf16[2,256,1024]{2,1,0:T(8,128)(2,1)S(1)} %constant_dynamic-update-slice_fusion.4), channel_id=1, source_target_pairs={{0,1},{1,0},{2,3},{3,2},{4,5},{5,4},{6,7},{7,6},{8,9},{9,8},{10,11... | collective-permute-start | bytes 3145736 | tf_op jit(solution)/shard_map/ppermute | solution.py:31
  171.0 3.0 %collective-permute-start.16 = (bf16[2,256,1024]{2,1,0:T(8,128)(2,1)S(1)}, bf16[2,256,1024]{2,1,0:T(8,128)(2,1)S(1)}, u32[]{:S(2)}, u32[]{:S(2)}) collective-permute-start(bf16[2,256,1024]{2,1,0:T(8,128)(2,1)S(1)} %convolution_convert_fusion.1), channel_id=1, source_target_pairs={{0,1},{1,0},{2,3},{3,2},{4,5},{5,4},{6,7},{7,6},{8,9},{9,8},{10,11... | collective-permute-start | bytes 3145736 | tf_op jit(solution)/shard_map/ppermute | solution.py:31
  174.6 9.6 %collective-permute-start.17 = (bf16[2,256,256]{2,1,0:T(8,128)(2,1)S(1)}, bf16[2,256,256]{2,1,0:T(8,128)(2,1)S(1)}, u32[]{:S(2)}, u32[]{:S(2)}) collective-permute-start(bf16[2,256,256]{2,1,0:T(8,128)(2,1)S(1)} %get-tuple-element.111), channel_id=1, source_target_pairs={{0,2},{2,4},{4,6},{6,0},{1,3},{3,5},{5,7},{7,1},{8,10},{10,12},{12... | collective-permute-start | bytes 786440 | tf_op jit(solution)/shard_map/ppermute | solution.py:27
  175.9 13.2 %collective-permute-start.19 = (bf16[2,256,256]{2,1,0:T(8,128)(2,1)S(1)}, bf16[2,256,256]{2,1,0:T(8,128)(2,1)S(1)}, u32[]{:S(2)}, u32[]{:S(2)}) collective-permute-start(bf16[2,256,256]{2,1,0:T(8,128)(2,1)S(1)} %get-tuple-element.112), channel_id=1, source_target_pairs={{0,6},{2,0},{4,2},{6,4},{1,7},{3,1},{5,3},{7,5},{8,14},{10,8},{12,... | collective-permute-start | bytes 786440 | tf_op jit(solution)/shard_map/ppermute | solution.py:27
  177.9 12.8 %collective-permute-start.18 = (bf16[2,256,256]{2,1,0:T(8,128)(2,1)S(1)}, bf16[2,256,256]{2,1,0:T(8,128)(2,1)S(1)}, u32[]{:S(2)}, u32[]{:S(2)}) collective-permute-start(bf16[2,256,256]{2,1,0:T(8,128)(2,1)S(1)} %get-tuple-element.113), channel_id=1, source_target_pairs={{0,4},{2,6},{4,0},{6,2},{1,5},{3,7},{5,1},{7,3},{8,12},{10,14},{12... | collective-permute-start | bytes 786440 | tf_op jit(solution)/shard_map/ppermute | solution.py:27
  (9 other events, 41.8 us)
Sparse Core Ops, SparseCore 0:
  109.6 27.1 all-gather.1
